TPU v7x, 32 devices: a whole 2x2x4 slice. The times are simulated.
32 devices in a mesh: dp: 8 (over z, x), mp: 4 (over y, core).
Axes of the slice: x: 2, y: 2, z: 4, core: 2. Of those that a mesh axis runs over, the one named last changes fastest.
Arguments:
- block_in: bfloat16 [8, 2048, 1024], P('dp', 'mp'), may hold values from -6 to 6
- segment_ids: int32 [8, 2048], P('dp', 'mp'), may hold values from 0 to 15, never falling along the last dimension, each value on 1 to 1024 neighbouring positions
- first_gain: bfloat16 [1024], P(('dp', 'mp')), may hold values from 0.5 to 1.5
- in_proj: bfloat16 [1024, 3072], P(('dp', 'mp')), may hold values from -0.1875 to 0.1875
- conv_kernel: bfloat16 [1024, 3], P(('dp', 'mp')), may hold values from -3 to 3
- out_proj: bfloat16 [1024, 1024], P(('dp', 'mp')), may hold values from -0.1875 to 0.1875
- second_gain: bfloat16 [1024], P(('dp', 'mp')), may hold values from 0.5 to 1.5
- gate_proj: bfloat16 [1024, 4608], P(None, 'mp'), may hold values from -0.1875 to 0.1875
- up_proj: bfloat16 [1024, 4608], P(None, 'mp'), may hold values from -0.1875 to 0.1875
- down_proj: bfloat16 [4608, 1024], P('mp'), may hold values from -0.125 to 0.125
- out_grad: bfloat16 [8, 2048, 1024], P('dp', 'mp'), may hold values from -6 to 6
Outputs:
- layer_out: bfloat16 [8, 2048, 1024], P('dp', 'mp')
- input_grad: float32 [8, 2048, 1024], P('dp', 'mp')
- grad_first: float32 [1024], P(('dp', 'mp'))
- grad_in: float32 [1024, 3072], P(('dp', 'mp'))
- grad_conv: float32 [1024, 3], P(('dp', 'mp'))
- grad_out: float32 [1024, 1024], P(('dp', 'mp'))
- grad_second: float32 [1024], P(('dp', 'mp'))
- grad_gate: float32 [1024, 4608], P(None, 'mp')
- grad_up: float32 [1024, 4608], P(None, 'mp')
- grad_down: float32 [4608, 1024], P('mp')
Inputs may be any that keep to these rules, and one draw needn't show every extreme that they name: `segment_ids`: along each sequence the ids never fall and each document is one run of positions; the longest document has exactly 1024 tokens.
All inputs are finite; a program needn't handle non-finite values.
Results may differ from a plain program's by a relative error of at most 0.013.
Values may be sent and summed in bfloat16 or wider, within the bound.
No kernel may reach another device: no remote copies, remote signals or barrier semaphores. Data moves between devices by JAX's collectives and lax.ppermute only.
A program may use at most 192 MiB of HBM per device.

v0:
```python
import jax
import jax.numpy as jnp
from jax import lax
from jax.sharding import PartitionSpec as P

KERNEL = 3


epsilon = 1e-05


def from_behind(block, axis, distance):
    devices = range(lax.axis_size(axis))
    route = [(i - distance, i) for i in devices if i - distance in devices]
    return lax.ppermute(block, axis, route)


def rms_norm(values, scale):
    return values * lax.rsqrt(jnp.mean(values * values, axis=-1, keepdims=True) + epsilon) * scale


def swiglu(gate_val, up_val):
    return jax.nn.silu(gate_val) * up_val


def inner_rows(left, right):
    return lax.dot_general(
        left, right, (((0,), (0,)), ((), ())), preferred_element_type=jnp.float32
    )


def inner_cols(left, right):
    return lax.dot_general(
        left, right, (((1,), (1,)), ((), ())), preferred_element_type=jnp.float32
    )


def causal_conv(product, rim_rows, own_ids, rim_ids, kernel):
    length = product.shape[0]
    extended = jnp.concatenate([rim_rows, product], 0)
    extended_ids = jnp.concatenate([rim_ids, own_ids], 0)
    summed = jnp.zeros_like(product)
    for offset in range(KERNEL):
        same = (extended_ids[offset : offset + length] == own_ids)[:, None]
        summed = (
            summed + jnp.where(same, extended[offset : offset + length], 0.0) * kernel[:, offset]
        )
    return summed


def per_device(
    block_in,
    segment_ids,
    first_gain,
    in_proj,
    conv_kernel,
    out_proj,
    second_gain,
    gate_proj,
    up_proj,
    down_proj,
    out_grad,
):
    row_count = block_in.shape[1]
    features = block_in.shape[2]
    lookback = KERNEL - 1
    residual_in = block_in.reshape(row_count, features).astype(jnp.float32)
    own_ids = segment_ids.reshape(row_count).astype(jnp.float32)
    gain_one, weight_in, kernel_all, weight_out, gain_two = (
        lax.all_gather(first_gain, ("dp", "mp"), axis=0, tiled=True),
        lax.all_gather(in_proj, ("dp", "mp"), axis=0, tiled=True),
        lax.all_gather(conv_kernel, ("dp", "mp"), axis=0, tiled=True),
        lax.all_gather(out_proj, ("dp", "mp"), axis=0, tiled=True),
        lax.all_gather(second_gain, ("dp", "mp"), axis=0, tiled=True),
    )
    first_normed, first_pull = jax.vjp(rms_norm, residual_in, gain_one.astype(jnp.float32))
    first_low = first_normed.astype(jnp.bfloat16)
    mixer = jnp.dot(first_low, weight_in, preferred_element_type=jnp.float32)
    opening = mixer[:, :features]
    closing = mixer[:, features : 2 * features]
    carried = mixer[:, 2 * features :]
    product = opening * carried
    rim_rows, rim_ids = from_behind(
        (product[row_count - lookback :], own_ids[row_count - lookback :]), "mp", 1
    )

    def gated_conv(product_in, closing_in, rim_in, kernel_in):
        return closing_in * causal_conv(product_in, rim_in, own_ids, rim_ids, kernel_in)

    gated, conv_pull = jax.vjp(
        gated_conv, product, closing, rim_rows, kernel_all.astype(jnp.float32)
    )
    gated_low = gated.astype(jnp.bfloat16)
    residual = residual_in + jnp.dot(gated_low, weight_out, preferred_element_type=jnp.float32)
    second_normed, second_pull = jax.vjp(rms_norm, residual, gain_two.astype(jnp.float32))
    second_low = second_normed.astype(jnp.bfloat16)
    group_rows = lax.all_gather(second_low, "mp", axis=0, tiled=True)
    gate_val = jnp.dot(group_rows, gate_proj, preferred_element_type=jnp.float32)
    up_val = jnp.dot(group_rows, up_proj, preferred_element_type=jnp.float32)
    activated, swiglu_pull = jax.vjp(swiglu, gate_val, up_val)
    hidden = activated.astype(jnp.bfloat16)
    offset_rows = lax.axis_index("mp") * row_count
    branch_sums = lax.psum(
        jnp.dot(hidden, down_proj, preferred_element_type=jnp.float32).astype(jnp.bfloat16), "mp"
    ).astype(jnp.float32)
    branch_out = lax.dynamic_slice_in_dim(branch_sums, offset_rows, row_count, 0)
    layer_out = (residual + branch_out).astype(jnp.bfloat16).reshape(1, row_count, features)
    cotangent = out_grad.reshape(row_count, features)
    cotangent_group = lax.all_gather(cotangent, "mp", axis=0, tiled=True)
    down_local = inner_rows(hidden, cotangent_group)
    hidden_grad = inner_cols(cotangent_group, down_proj)
    gate_grad, up_grad = swiglu_pull(hidden_grad)
    gate_low = gate_grad.astype(jnp.bfloat16)
    up_low = up_grad.astype(jnp.bfloat16)
    gate_local = inner_rows(group_rows, gate_low)
    up_local = inner_rows(group_rows, up_low)
    backward_sums = lax.psum(
        (inner_cols(gate_low, gate_proj) + inner_cols(up_low, up_proj)).astype(jnp.bfloat16), "mp"
    ).astype(jnp.float32)
    normed_grad = lax.dynamic_slice_in_dim(backward_sums, offset_rows, row_count, 0)
    residual_part, second_local = second_pull(normed_grad)
    residual_grad = cotangent.astype(jnp.float32) + residual_part
    residual_low = residual_grad.astype(jnp.bfloat16)
    out_local = inner_rows(gated_low, residual_low)
    gated_grad = inner_cols(residual_low, weight_out)
    product_grad, closing_grad, rim_grad, kernel_local = conv_pull(gated_grad)
    rim_back = from_behind(rim_grad, "mp", -1)
    product_grad = product_grad + jnp.pad(rim_back, ((row_count - lookback, 0), (0, 0)))
    mixer_grad = jnp.concatenate(
        [product_grad * carried, closing_grad, product_grad * opening], 1
    ).astype(jnp.bfloat16)
    in_local = inner_rows(first_low, mixer_grad)
    first_grad = inner_cols(mixer_grad, weight_in)
    input_part, first_local = first_pull(first_grad)
    input_grad = (residual_grad + input_part).reshape(1, row_count, features)
    grad_gate, grad_up, grad_down = (
        lax.psum(gate_local.astype(jnp.bfloat16), "dp").astype(jnp.float32),
        lax.psum(up_local.astype(jnp.bfloat16), "dp").astype(jnp.float32),
        lax.psum(down_local.astype(jnp.bfloat16), "dp").astype(jnp.float32),
    )
    grad_first, grad_in, grad_conv, grad_out, grad_second = (
        lax.psum_scatter(first_local, ("dp", "mp"), scatter_dimension=0, tiled=True),
        lax.psum_scatter(in_local, ("dp", "mp"), scatter_dimension=0, tiled=True),
        lax.psum_scatter(kernel_local, ("dp", "mp"), scatter_dimension=0, tiled=True),
        lax.psum_scatter(out_local, ("dp", "mp"), scatter_dimension=0, tiled=True),
        lax.psum_scatter(second_local, ("dp", "mp"), scatter_dimension=0, tiled=True),
    )
    return (
        layer_out,
        input_grad,
        grad_first,
        grad_in,
        grad_conv,
        grad_out,
        grad_second,
        grad_gate,
        grad_up,
        grad_down,
    )


def solution(mesh):
    in_specs = (
        P("dp", "mp", None),
        P("dp", "mp"),
        P(("dp", "mp")),
        P(("dp", "mp"), None),
        P(("dp", "mp"), None),
        P(("dp", "mp"), None),
        P(("dp", "mp")),
        P(None, "mp"),
        P(None, "mp"),
        P("mp", None),
        P("dp", "mp", None),
    )
    out_specs = (
        P("dp", "mp", None),
        P("dp", "mp", None),
        P(("dp", "mp")),
        P(("dp", "mp"), None),
        P(("dp", "mp"), None),
        P(("dp", "mp"), None),
        P(("dp", "mp")),
        P(None, "mp"),
        P(None, "mp"),
        P("mp", None),
    )
    return jax.shard_map(
        per_device, mesh=mesh, in_specs=in_specs, out_specs=out_specs, check_vma=False
    )
```

profile of v0, /device:TPU:0, one launch (start us, length us, event | category | flops | bytes accessed | tf_op | source)
XLA Modules:
  0.0 1103.6 jit_solution(15660055661368846921)
XLA Ops:
  13.5 41.9 %all-reduce.12 = (bf16[1024]{0:T(1024)(128)(2,1)S(1)}, bf16[1024]{0:T(1024)(128)(2,1)S(1)}) all-reduce(bf16[1024]{0:T(1024)(128)(2,1)S(1)} %dynamic-update-slice, bf16[1024]{0:T(1024)(128)(2,1)S(1)} %dynamic-update-slice.1), channel_id=1, replica_groups=mesh['dp'=8,'mp'=4] {'dp','mp'}, use_global_device_ids=true, to_apply=%add.7 | all-reduce | flops 2048 | bytes 8192
  55.4 40.8 %all-gather.1 = bf16[32,32,3]{1,2,0:T(4,128)(2,1)S(1)} all-gather(bf16[1,32,3]{1,2,0:T(4,128)(2,1)} %bitcast.74), channel_id=1, replica_groups=mesh['dp'=8,'mp'=4] {'dp','mp'}, dimensions={0}, use_global_device_ids=true | all-gather | bytes 6336 | tf_op jit(solution)/shard_map/all_gather | solution.py:72
  98.0 6.0 fusion.35
  107.4 2.5 multiply_convert_fusion.6
  110.0 31.3 %all-gather.9.cloned.1.call-done = bf16[1024,1024]{1,0:T(8,128)(2,1)} async-done(((bf16[32,1024]{1,0:T(8,128)(2,1)}), bf16[1024,1024]{1,0:T(8,128)(2,1)}) %all-gather.9.cloned.1.call-update) | async-done | bytes 2097168 | tf_op jit(solution)/shard_map/all_gather | solution.py:73
  141.3 3.3 multiply_reduce_fusion.3
  148.0 32.7 %all-gather.11.cloned.1.call-done = bf16[2048,1024]{1,0:T(8,128)(2,1)} async-done(((bf16[512,1024]{1,0:T(8,128)(2,1)}), bf16[2048,1024]{1,0:T(8,128)(2,1)}) %all-gather.11.cloned.1.call-update) | async-done | bytes 4194320 | tf_op jit(solution)/shard_map/all_gather | solution.py:97
  180.7 10.6 fusion.42
  191.3 7.9 fusion.43
  199.2 17.5 %all-gather.13.cloned.1.call-done = bf16[1,2048,1024]{2,1,0:T(8,128)(2,1)} async-done(((bf16[1,512,1024]{2,1,0:T(8,128)(2,1)}), bf16[1,2048,1024]{2,1,0:T(8,128)(2,1)}) %all-gather.13.cloned.1.call-update) | async-done | bytes 4194320 | tf_op jit(solution)/shard_map/all_gather | solution.py:109
  216.6 18.2 %multiply_convert_fusion = (bf16[2048,1152]{1,0:T(8,128)(2,1)}, bf16[2048,1152]{1,0:T(8,128)(2,1)}, bf16[2048,1152]{1,0:T(8,128)(2,1)}) fusion(f32[2048,1152]{1,0:T(8,128)} %fusion.42, f32[2048,1152]{1,0:T(8,128)} %fusion.43, bf16[1152,1024]{1,0:T(8,128)(2,1)S(1)} %copy-done, bf16[1,2048,1024]{2,1,0:T(8,128)(2,1)} %all-gather.13.cloned.1.call-done), kind=kOutput, calls=%fused_computation.4 | convolution fusion | flops 4869586944 | bytes 39583744 | tf_op jit(solution)/shard_map/dot_general | solution.py:33
  234.9 7.7 fusion.44
  242.6 7.1 convolution_convert_fusion.2
  249.7 7.7 add_convert_fusion
  257.6 10.1 convolution_convert_fusion
  267.6 9.6 convolution_convert_fusion.1
  277.2 133.6 %all-reduce.20.cloned.1.call-done = (bf16[2048,1024]{1,0:T(8,128)(2,1)}, bf16[2048,1024]{1,0:T(8,128)(2,1)}) async-done(((bf16[2048,1024]{1,0:T(8,128)(2,1)}, bf16[2048,1024]{1,0:T(8,128)(2,1)}), (bf16[2048,1024]{1,0:T(8,128)(2,1)}, bf16[2048,1024]{1,0:T(8,128)(2,1)})) %all-reduce.20.cloned.1.call-update) | async-done | bytes 8388624 | tf_op jit(solution)/shard_map/psum | solution.py:103
  412.9 3.4 fusion.21
  419.3 3.7 multiply_reduce_fusion.1
  424.1 9.6 fusion.8
  435.3 4.5 fusion.30
  447.4 6.8 fusion.27
  454.3 8.8 fusion.18
  463.1 40.7 %all-reduce.11 = (f32[1024]{0:T(1024)S(1)}, f32[1024]{0:T(1024)S(1)}) all-reduce(f32[1024]{0:T(1024)S(1)} %get-tuple-element.15, f32[1024]{0:T(1024)S(1)} %get-tuple-element.10), channel_id=3, replica_groups=mesh['dp'=8,'mp'=4] {'dp','mp'}, use_global_device_ids=true, to_apply=%region_7.8.clone | all-reduce | flops 2048 | bytes 16384
  505.0 3.4 fusion.23
  508.5 50.0 %reduce-scatter.10.cloned.1.call-done = f32[32,3]{1,0:T(8,128)} async-done(((f32[1024,3]{1,0:T(8,128)}), f32[32,3]{1,0:T(8,128)}) %reduce-scatter.10.cloned.1.call-update) | async-done | bytes 400
  559.9 235.4 %all-reduce.18.cloned.1.call-done = (bf16[1024,1152]{1,0:T(8,128)(2,1)}, bf16[1024,1152]{1,0:T(8,128)(2,1)}, bf16[1152,1024]{1,0:T(8,128)(2,1)}) async-done(((bf16[1024,1152]{1,0:T(8,128)(2,1)}, bf16[1024,1152]{1,0:T(8,128)(2,1)}, bf16[1152,1024]{1,0:T(8,128)(2,1)}), (bf16[1024,1152]{1,0:T(8,128)(2,1)}, bf16[1024,1152]{1,0:T(8,128)(2,1)}, bf16[1152,1024]{1,0:T(8,128)(2,1)})) %all-reduce.18.cloned.1.call-update) | async-done | bytes 7077904 | tf_op jit(solution)/shard_map/psum | solution.py:137
  795.3 4.3 convert_element_type.106
  799.6 2.5 convert_element_type.108
  802.2 2.7 convert_element_type.110
  804.9 133.4 %reduce-scatter.8.cloned.1.call-done = f32[32,1024]{1,0:T(8,128)} async-done(((f32[1024,1024]{1,0:T(8,128)}), f32[32,1024]{1,0:T(8,128)}) %reduce-scatter.8.cloned.1.call-update) | async-done | bytes 131088 | tf_op jit(solution)/shard_map/reduce_scatter | solution.py:145
  938.3 158.3 %reduce-scatter.6.cloned.1.call-done = f32[32,3072]{1,0:T(8,128)} async-done(((f32[1024,3072]{1,0:T(8,128)}), f32[32,3072]{1,0:T(8,128)}) %reduce-scatter.6.cloned.1.call-update) | async-done | bytes 393232 | tf_op jit(solution)/shard_map/reduce_scatter | solution.py:143
  (115 shorter events, 32.9 us)
Async XLA Ops:
  7.2 209.4 %copy-start = (bf16[1152,1024]{1,0:T(8,128)(2,1)S(1)}, bf16[1152,1024]{1,0:T(8,128)(2,1)}, u32[]{:S(2)}) copy-start(bf16[1152,1024]{1,0:T(8,128)(2,1)} %param.20) | copy-start | bytes 7077892
  7.2 90.8 %all-gather.7.cloned.1.call-start = ((), (), s32[]{:S(2)}) async-start(), calls=%async_computation.3 | async-start | bytes 6488064 | tf_op jit(solution)/shard_map/all_gather | solution.py:71
  7.9 133.4 %all-gather.9.cloned.1.call-start = ((), (), s32[]{:S(2)}) async-start(), calls=%async_computation.4 | async-start | bytes 2162688 | tf_op jit(solution)/shard_map/all_gather | solution.py:73
  8.7 172.0 %all-gather.11.cloned.1.call-start = ((), (), s32[]{:S(2)}) async-start(), calls=%async_computation.5 | async-start | bytes 5242880 | tf_op jit(solution)/shard_map/all_gather | solution.py:97
  9.5 88.4 %collective-permute-start = (f32[2]{0:T(128)S(1)}, f32[2]{0:T(128)S(1)}, u32[]{:S(2)}, u32[]{:S(2)}) collective-permute-start(f32[2]{0:T(128)S(1)} %slice_bitcast_fusion), channel_id=1, source_target_pairs={{0,1},{1,2},{2,3},{4,5},{5,6},{6,7},{8,9},{9,10},{10,11},{12,13},{... | collective-permute-start | bytes 32 | tf_op jit(solution)/shard_map/ppermute | solution.py:15
  104.0 3.5 copy-start.2
  104.4 3.1 copy-start.3
  104.4 3.0 collective-permute-start.1
  107.4 33.9 %copy-start.9 = (bf16[1,512,1024]{2,1,0:T(8,128)(2,1)S(1)}, bf16[1,512,1024]{2,1,0:T(8,128)(2,1)}, u32[]{:S(2)}) copy-start(bf16[1,512,1024]{2,1,0:T(8,128)(2,1)} %param.11) | copy-start | bytes 3145732
  147.2 69.4 %all-gather.13.cloned.1.call-start = ((), (), s32[]{:S(2)}) async-start(), calls=%async_computation.8 | async-start | bytes 5242880 | tf_op jit(solution)/shard_map/all_gather | solution.py:109
  147.8 263.1 %all-reduce.20.cloned.1.call-start = ((), (), s32[]{:S(2)}) async-start(), calls=%async_computation.11 | async-start | bytes 16777216 | tf_op jit(solution)/shard_map/psum | solution.py:103
  180.7 10.6 copy-start.17
  180.7 10.6 copy-start.20
  216.6 18.2 %copy-start.19 = (bf16[1024,1152]{1,0:T(8,128)(2,1)S(1)}, bf16[1024,1152]{1,0:T(8,128)(2,1)}, u32[]{:S(2)}) copy-start(bf16[1024,1152]{1,0:T(8,128)(2,1)} %param.18) | copy-start | bytes 7077892
  234.9 7.7 copy-start.23
  234.9 14.8 %slice-start.2 = ((s8[4718592]{0:T(1024)(128)(4,1)}), s8[4194304]{0:T(1024)(128)(4,1)S(1)}, s32[]{:S(2)}) async-start(s8[4718592]{0:T(1024)(128)(4,1)} %bitcast.75), calls=%async_computation.14 | async-start | bytes 8388608
  242.5 7.2 slice-start.3
  242.6 7.1 copy-start.21
  257.5 301.0 %reduce-scatter.10.cloned.1.call-start = ((), (), s32[]{:S(2)}) async-start(), calls=%async_computation.9 | async-start | bytes 540672
  257.5 10.1 copy-start.18
  267.6 143.3 %copy-start.8 = (f32[512,1024]{1,0:T(8,128)S(1)}, f32[512,1024]{1,0:T(8,128)}, u32[]{:S(2)}) copy-start(f32[512,1024]{1,0:T(8,128)} %copy-done.7) | copy-start | bytes 6291460
  412.9 3.4 copy-start.22
  416.3 3.0 copy-start.10
  424.1 371.1 %all-reduce.18.cloned.1.call-start = ((), (), s32[]{:S(2)}) async-start(), calls=%async_computation.10 | async-start | bytes 14155776 | tf_op jit(solution)/shard_map/psum | solution.py:137
  433.7 504.6 %reduce-scatter.8.cloned.1.call-start = ((), (), s32[]{:S(2)}) async-start(), calls=%async_computation.7 | async-start | bytes 4325376 | tf_op jit(solution)/shard_map/reduce_scatter | solution.py:145
  439.8 656.8 %reduce-scatter.6.cloned.1.call-start = ((), (), s32[]{:S(2)}) async-start(), calls=%async_computation.6 | async-start | bytes 12976128 | tf_op jit(solution)/shard_map/reduce_scatter | solution.py:143
  441.9 3.4 slice-start
  441.9 3.3 slice-start.1
  441.9 3.3 collective-permute-start.2
  444.4 3.0 copy-start.11
  795.2 4.3 copy-start.16
  802.1 294.5 %copy-start.1 = (bf16[1152,1024]{1,0:T(8,128)(2,1)S(1)}, bf16[1152,1024]{1,0:T(8,128)(2,1)}, u32[]{:S(2)}) copy-start(bf16[1152,1024]{1,0:T(8,128)(2,1)} %param.20) | copy-start | bytes 7077892
  (8 other events, 13.6 us)
Sparse Core Ops, SparseCore 0:
  10.9 72.5 all-gather.6
  86.4 54.8 all-gather.8
  147.3 33.3 all-gather.10
  182.1 34.4 all-gather.12
  257.6 153.2 all-reduce.19
  424.2 134.2 reduce-scatter.9
  564.0 231.1 all-reduce.17
  798.1 140.1 reduce-scatter.7
  944.9 151.6 reduce-scatter.5
where the time goes:
time: 1110 us; the launch traced here: 1100 us
  waiting for transfers between devices  796 us (72%)
  blocking collectives  123 us (11%)
  matrix products  119 us (11%)
  other arithmetic  32.4 us (3%)
  between operations  14.7 us (1%)
  local copies, waits for them, and re-layouts  11.6 us (1%)
    psum x1, waiting for transfers between devices, per_device(): lax.psum(gate_local.astype(jnp.bfloat16), 'dp').astype(jnp.float32)  235 us
    reduce_scatter x1, waiting for transfers between devices, per_device(): lax.psum_scatter(in_local, ('dp', 'mp'), scatter_dimension=0, tiled=True)  158 us
    psum x1, waiting for transfers between devices, per_device(): lax.psum(jnp.dot(hidden, down_proj, preferred_element_type=jnp.float32).a...  134 us
    reduce_scatter x1, waiting for transfers between devices, per_device(): lax.psum_scatter(out_local, ('dp', 'mp'), scatter_dimension=0, tiled=True)  133 us
    unnamed x2, blocking collectives  82.6 us
    unnamed x10, waiting for transfers between devices  52 us
    dot_general x5, matrix products, inner_cols(): lax.dot_general(left, right, (((1,), (1,)), ((), ())), preferred_element_...  43.7 us
    all_gather x1, blocking collectives, per_device(): lax.all_gather(conv_kernel, ('dp', 'mp'), axis=0, tiled=True)  40.8 us
  transfers between devices with their start and end apart: 12, of which 10 were waited for; matrix products, arithmetic and copies ran while one was open for 9% of the time, Pallas kernels for 0%

commit v1 on v0

v1 whole, which is shorter than its diff:
```python
import jax
import jax.numpy as jnp
from jax import lax
from jax.sharding import PartitionSpec as P

KERNEL = 3
LANES = 128
BF16 = jnp.bfloat16
F32 = jnp.float32

epsilon = 1e-05


def swap(block, axis, bit):
    size = lax.axis_size(axis)
    return lax.ppermute(block, axis, [(i, i ^ (1 << bit)) for i in range(size)])


def shift(block, axis, distance):
    devices = range(lax.axis_size(axis))
    route = [(i - distance, i) for i in devices if i - distance in devices]
    return lax.ppermute(block, axis, route)


def bit_of(axis, bit):
    return (lax.axis_index(axis) >> bit) & 1


def bits_of(axis):
    size = lax.axis_size(axis)
    assert size & (size - 1) == 0
    return size.bit_length() - 1


def inner_rows(left, right):
    return lax.dot_general(
        left, right, (((0,), (0,)), ((), ())), preferred_element_type=F32
    )


def inner_cols(left, right):
    return lax.dot_general(
        left, right, (((1,), (1,)), ((), ())), preferred_element_type=F32
    )


def add_low(one, two):
    return (one.astype(F32) + two.astype(F32)).astype(BF16)


def gather_mp(own):
    blocks = [own]
    for bit in reversed(range(bits_of("mp"))):
        blocks = blocks + [None] * len(blocks)
    size = lax.axis_size("mp")
    blocks = [own] + [None] * (size - 1)
    for bit in reversed(range(bits_of("mp"))):
        have = [r for r in range(size) if blocks[r] is not None]
        for r in have:
            blocks[r ^ (1 << bit)] = swap(blocks[r], "mp", bit)
    return blocks


def scatter_mp(blocks):
    held = {r: block for r, block in enumerate(blocks)}
    for bit in range(bits_of("mp")):
        sent = [r for r in held if r >> bit & 1]
        kept = [r for r in held if not r >> bit & 1]
        got = swap(jnp.concatenate([held[r] for r in sent], 0), "mp", bit)
        rows = got.shape[0] // len(sent)
        for n, r in enumerate(sent):
            there = r ^ (1 << bit)
            held[there] = held[there].astype(F32) + got[n * rows : (n + 1) * rows].astype(F32)
        final = bit == bits_of("mp") - 1
        held = {r: held[r] if final else held[r].astype(BF16) for r in kept}
    return held[0]


def sum_dp(array):
    count = bits_of("dp")
    halved = list(range(min(count, 3)))
    for bit in halved:
        half = array.shape[0] // 2
        mine = bit_of("dp", bit)
        sent = lax.dynamic_slice_in_dim(array, (1 - mine) * half, half, 0)
        kept = lax.dynamic_slice_in_dim(array, mine * half, half, 0)
        array = add_low(kept, swap(sent, "dp", bit))
    for bit in range(len(halved), count):
        array = add_low(array, swap(array, "dp", bit))
    for bit in reversed(halved):
        got = swap(array, "dp", bit)
        low_first = bit_of("dp", bit) == 0
        array = jnp.concatenate(
            [jnp.where(low_first, array, got), jnp.where(low_first, got, array)], 0
        )
    return array


def scatter_all(array):
    steps = [("mp", b) for b in range(bits_of("mp"))] + [("dp", b) for b in range(bits_of("dp"))]
    count = len(steps)
    rows = array.shape[0] >> count
    array = array.reshape(array.shape[0] // rows, rows, array.shape[1])
    for axis, bit in steps:
        pairs = array.reshape(array.shape[0] // 2, 2, rows, array.shape[2])
        mine = bit_of(axis, bit)
        sent = lax.dynamic_index_in_dim(pairs, 1 - mine, 1, keepdims=False)
        kept = lax.dynamic_index_in_dim(pairs, mine, 1, keepdims=False)
        array = add_low(kept, swap(sent, axis, bit))
    return array[0]


def per_device(
    block_in,
    segment_ids,
    first_gain,
    in_proj,
    conv_kernel,
    out_proj,
    second_gain,
    gate_proj,
    up_proj,
    down_proj,
    out_grad,
):
    rows = block_in.shape[1]
    features = block_in.shape[2]
    lookback = KERNEL - 1
    x = block_in.reshape(rows, features).astype(F32)
    own_ids = segment_ids.reshape(rows)
    cotangent = out_grad.reshape(rows, features)

    small = jnp.concatenate(
        [first_gain[:, None], second_gain[:, None], conv_kernel], 1
    )
    small = jnp.pad(small, ((0, 0), (0, LANES - small.shape[1])))
    packed = jnp.concatenate([in_proj, out_proj, small], 1)
    everything = lax.all_gather(packed, ("dp", "mp"), axis=0, tiled=True)
    weight_in = everything[:, : 3 * features]
    weight_out = everything[:, 3 * features : 4 * features]
    vectors = everything[:, 4 * features : 4 * features + 2 + KERNEL].astype(F32).T
    gain_one, gain_two, taps = vectors[0], vectors[1], vectors[2:]

    group_grad = gather_mp(cotangent)

    inverse_one = lax.rsqrt(jnp.mean(x * x, axis=-1, keepdims=True) + epsilon)
    unit_one = x * inverse_one
    first_low = (unit_one * gain_one).astype(BF16)
    mixer = jnp.dot(first_low, weight_in, preferred_element_type=F32)
    opening = mixer[:, :features]
    closing = mixer[:, features : 2 * features]
    carried = mixer[:, 2 * features :]
    product = opening * carried
    rim_rows = shift(product[rows - lookback :], "mp", 1)
    rim_ids = shift(own_ids[rows - lookback :].astype(F32), "mp", 1).astype(jnp.int32)
    first = lax.axis_index("mp") == 0
    rim_ids = jnp.where(first, -1, rim_ids)
    extended = jnp.concatenate([rim_rows, product], 0)
    extended_ids = jnp.concatenate([rim_ids, own_ids], 0)
    same = [
        (extended_ids[k : k + rows] == own_ids)[:, None] for k in range(KERNEL)
    ]
    past = [jnp.where(same[k], extended[k : k + rows], 0.0) for k in range(KERNEL)]
    conv = sum(past[k] * taps[k] for k in range(KERNEL))
    gated_low = (closing * conv).astype(BF16)
    residual = x + jnp.dot(gated_low, weight_out, preferred_element_type=F32)
    inverse_two = lax.rsqrt(jnp.mean(residual * residual, axis=-1, keepdims=True) + epsilon)
    second_low = (residual * inverse_two * gain_two).astype(BF16)

    group = jnp.concatenate(gather_mp(second_low), 0)
    grads = jnp.concatenate(group_grad, 0)
    gate_val = jnp.dot(group, gate_proj, preferred_element_type=F32)
    up_val = jnp.dot(group, up_proj, preferred_element_type=F32)
    sig = jax.nn.sigmoid(gate_val)
    silu = gate_val * sig
    hidden = (silu * up_val).astype(BF16)
    down_local = inner_rows(hidden, grads).astype(BF16)
    grad_down = sum_dp(down_local).astype(F32)
    hidden_grad = inner_cols(grads, down_proj)
    gate_low = (hidden_grad * up_val * sig * (1 + gate_val * (1 - sig))).astype(BF16)
    up_low = (hidden_grad * silu).astype(BF16)
    second_parts = (inner_cols(gate_low, gate_proj) + inner_cols(up_low, up_proj)).astype(BF16)
    size = lax.axis_size("mp")
    second_grad = scatter_mp([second_parts[r * rows : (r + 1) * rows] for r in range(size)])
    grad_gate = sum_dp(inner_rows(group, gate_low).astype(BF16)).astype(F32)
    grad_up = sum_dp(inner_rows(group, up_low).astype(BF16)).astype(F32)
    branch_parts = jnp.dot(hidden, down_proj, preferred_element_type=F32).astype(BF16)
    branch = scatter_mp([branch_parts[r * rows : (r + 1) * rows] for r in range(size)])
    layer_out = (residual + branch).astype(BF16).reshape(1, rows, features)

    unit_two = residual * inverse_two
    weighted = second_grad * gain_two
    residual_grad = cotangent.astype(F32) + inverse_two * (
        weighted - unit_two * jnp.mean(weighted * unit_two, axis=-1, keepdims=True)
    )
    second_local = jnp.sum(second_grad * unit_two, axis=0)
    residual_low = residual_grad.astype(BF16)
    out_local = inner_rows(gated_low, residual_low)
    gated_grad = inner_cols(residual_low, weight_out)
    closing_grad = gated_grad * conv
    conv_grad = gated_grad * closing
    kernel_local = [jnp.sum(conv_grad * past[k], axis=0) for k in range(KERNEL)]
    spread = jnp.zeros((rows + lookback, features), F32)
    spread = sum(
        jnp.pad(jnp.where(same[k], conv_grad * taps[k], 0.0), ((k, lookback - k), (0, 0)))
        for k in range(KERNEL)
    )
    rim_back = shift(spread[:lookback], "mp", -1)
    product_grad = spread[lookback:] + jnp.pad(rim_back, ((rows - lookback, 0), (0, 0)))
    mixer_grad = jnp.concatenate(
        [product_grad * carried, closing_grad, product_grad * opening], 1
    ).astype(BF16)
    in_local = inner_rows(first_low, mixer_grad).astype(BF16)
    first_grad = inner_cols(mixer_grad, weight_in)
    weighted = first_grad * gain_one
    input_grad = residual_grad + inverse_one * (
        weighted - unit_one * jnp.mean(weighted * unit_one, axis=-1, keepdims=True)
    )
    input_grad = input_grad.reshape(1, rows, features)

    small_local = jnp.stack([second_local] + kernel_local, 1).astype(BF16)
    small_local = jnp.pad(small_local, ((0, 0), (0, LANES - small_local.shape[1])))
    early = scatter_all(jnp.concatenate([out_local.astype(BF16), small_local], 1)).astype(F32)
    grad_out = early[:, :features]
    grad_second = early[:, features]
    grad_conv = early[:, features + 1 : features + 1 + KERNEL]
    grad_in = scatter_all(in_local).astype(F32)
    grad_first = jnp.sum(grad_in * in_proj.astype(F32), axis=1) / first_gain.astype(F32)
    return (
        layer_out,
        input_grad,
        grad_first,
        grad_in,
        grad_conv,
        grad_out,
        grad_second,
        grad_gate,
        grad_up,
        grad_down,
    )


def solution(mesh):
    in_specs = (
        P("dp", "mp", None),
        P("dp", "mp"),
        P(("dp", "mp")),
        P(("dp", "mp"), None),
        P(("dp", "mp"), None),
        P(("dp", "mp"), None),
        P(("dp", "mp")),
        P(None, "mp"),
        P(None, "mp"),
        P("mp", None),
        P("dp", "mp", None),
    )
    out_specs = (
        P("dp", "mp", None),
        P("dp", "mp", None),
        P(("dp", "mp")),
        P(("dp", "mp"), None),
        P(("dp", "mp"), None),
        P(("dp", "mp"), None),
        P(("dp", "mp")),
        P(None, "mp"),
        P(None, "mp"),
        P("mp", None),
    )
    return jax.shard_map(
        per_device, mesh=mesh, in_specs=in_specs, out_specs=out_specs, check_vma=False
    )
```

time: 1110 us -> 578 us (0.52)
  waiting for transfers between devices: 796 us -> 341 us
  blocking collectives: 123 us -> 0 us
  starting transfers between devices: 6.65 us -> 37.9 us
  other arithmetic: 32.4 us -> 48.2 us
    psum x2 -> x0, waiting for transfers between devices: 369 us -> none  [the longest x1 235 us: per_device(): lax.psum(gate_local.astype(jnp.bfloat16), 'dp').astype(jnp.float32)]
    reduce_scatter x2 -> x0, waiting for transfers between devices: 292 us -> none  [the longest x1 158 us: per_device(): lax.psum_scatter(in_local, ('dp', 'mp'), scatter_dimension=0, tiled=True)]
    ppermute x3 -> x41, waiting for transfers between devices: 1.53 us -> 264 us  [the longest x38 264 us: swap(): return lax.ppermute(block, axis, [(i, i ^ 1 << bit) for i in range(size)])]
    unnamed x2 -> x0, blocking collectives: 82.6 us -> none
    unnamed x10 -> x1, waiting for transfers between devices: 52 us -> 0.02 us
    all_gather x1 -> x0, blocking collectives: 40.8 us -> none  [per_device(): lax.all_gather(conv_kernel, ('dp', 'mp'), axis=0, tiled=True)]
    ppermute x3 -> x41, starting transfers between devices: 6.12 us -> 37.8 us  [the longest x38 31.4 us: swap(): return lax.ppermute(block, axis, [(i, i ^ 1 << bit) for i in range(size)])]
    dot_general x5, matrix products: 40.6 us -> 27.8 us  [inner_rows(): lax.dot_general(left, right, (((0,), (0,)), ((), ())), preferred_element_...]
  transfers between devices with their start and end apart: 12 -> 42, of which waited for: 10 -> 20; matrix products, arithmetic and copies ran while one was open for 9% -> 21% of each run, Pallas kernels for 0% -> 0%
where the time goes in v1:
time: 578 us; the launch traced here: 574 us
  waiting for transfers between devices  341 us (59%)
  matrix products  116 us (20%)
  other arithmetic  48.2 us (8%)
  starting transfers between devices  37.9 us (7%)
  between operations  15.6 us (3%)
  local copies, waits for them, and re-layouts  15.5 us (3%)
    ppermute x38, waiting for transfers between devices, swap(): return lax.ppermute(block, axis, [(i, i ^ 1 << bit) for i in range(size)])  264 us
    all_gather x1, waiting for transfers between devices, per_device(): everything = lax.all_gather(packed, ('dp', 'mp'), axis=0, tiled=True)  77.2 us
    dot_general x5, matrix products, inner_cols(): lax.dot_general(left, right, (((1,), (1,)), ((), ())), preferred_element_...  47.9 us
    ppermute x38, starting transfers between devices, swap(): return lax.ppermute(block, axis, [(i, i ^ 1 << bit) for i in range(size)])  31.4 us
    dot_general x5, matrix products, inner_rows(): lax.dot_general(left, right, (((0,), (0,)), ((), ())), preferred_element_...  27.8 us
    dot_general x1, matrix products, per_device(): up_val = jnp.dot(group, up_proj, preferred_element_type=F32)  11.7 us
  transfers between devices with their start and end apart: 42, of which 20 were waited for; matrix products, arithmetic and copies ran while one was open for 21% of the time, Pallas kernels for 0%

profile of v1, /device:TPU:0, one launch (start us, length us, event | category | flops | bytes accessed | tf_op | source)
XLA Modules:
  0.0 574.2 jit_solution(11197532602381510149)
XLA Ops:
  15.4 77.2 %all-gather.2.cloned.1.call-done = bf16[1024,4224]{1,0:T(8,128)(2,1)} async-done(((bf16[32,4224]{1,0:T(8,128)(2,1)}), bf16[1024,4224]{1,0:T(8,128)(2,1)}) %all-gather.2.cloned.1.call-update) | async-done | bytes 8650768 | tf_op jit(solution)/shard_map/all_gather | solution.py:138
  95.0 5.7 fusion.4
  115.0 24.0 %collective-permute-done.3 = bf16[512,1024]{1,0:T(8,128)(2,1)} collective-permute-done((bf16[512,1024]{1,0:T(8,128)(2,1)S(1)}, bf16[512,1024]{1,0:T(8,128)(2,1)}, u32[]{:S(2)}, u32[]{:S(2)}) %collective-permute-start.3) | collective-permute-done | bytes 1048608 | tf_op jit(solution)/shard_map/ppermute | solution.py:16
  139.5 20.8 %collective-permute-done.8 = bf16[512,1024]{1,0:T(8,128)(2,1)} collective-permute-done((bf16[512,1024]{1,0:T(8,128)(2,1)}, bf16[512,1024]{1,0:T(8,128)(2,1)}, u32[]{:S(2)}, u32[]{:S(2)}) %collective-permute-start.8) | collective-permute-done | bytes 1048608 | tf_op jit(solution)/shard_map/ppermute | solution.py:16
  160.4 11.7 %fusion.56 = f32[2048,1152]{1,0:T(8,128)} fusion(bf16[1024,1152]{1,0:T(8,128)(2,1)} %param.19, bf16[512,1024]{1,0:T(8,128)(2,1)} %collective-permute-done.4, bf16[512,1024]{1,0:T(8,128)(2,1)} %collective-permute-done.3, bf16[512,1024]{1,0:T(8,128)(2,1)} %collective-permute-done.2, bf16[512,1024]{1,0:T(8,128)(2,1)S(1)} %multiply_convert_fusion.6), kind=kOutput, calls=%fused_computation.188 | convolution fusion | flops 4848615424 | bytes 15990784 | tf_op jit(solution)/shard_map/dot_general | solution.py:173
  172.1 11.0 %fusion.57 = f32[2048,1152]{1,0:T(8,128)} fusion(bf16[1024,1152]{1,0:T(8,128)(2,1)S(1)} %copy-done.45, bf16[512,1024]{1,0:T(8,128)(2,1)} %collective-permute-done.4, bf16[512,1024]{1,0:T(8,128)(2,1)} %collective-permute-done.3, bf16[512,1024]{1,0:T(8,128)(2,1)} %collective-permute-done.2, bf16[512,1024]{1,0:T(8,128)(2,1)S(1)} %multiply_convert_fusion.6), kind=kOutput, calls=%fused_computation.189 | convolution fusion | flops 4848615424 | bytes 15990784 | tf_op jit(solution)/shard_map/dot_general | solution.py:172
  183.1 18.0 %multiply_convert_fusion = (bf16[2048,1152]{1,0:T(8,128)(2,1)}, bf16[2048,1152]{1,0:T(8,128)(2,1)}, bf16[2048,1152]{1,0:T(8,128)(2,1)}) fusion(f32[2048,1152]{1,0:T(8,128)} %fusion.57, f32[2048,1152]{1,0:T(8,128)} %fusion.56, bf16[1152,1024]{1,0:T(8,128)(2,1)S(1)} %copy-done, bf16[512,1024]{1,0:T(8,128)(2,1)} %collective-permute-done.9, ...), kind=kOutput, calls=%fused_computation | convolution fusion | flops 4884004864 | bytes 39583744 | tf_op jit(solution)/shard_map/dot_general | solution.py:42
  201.1 8.3 %convolution_convert_fusion.4 = bf16[2048,1024]{1,0:T(8,128)(2,1)S(1)} fusion(bf16[2048,1152]{1,0:T(8,128)(2,1)} %get-tuple-element.67, bf16[1152,1024]{1,0:T(8,128)(2,1)S(1)} %copy-done), kind=kOutput, calls=%fused_computation.18 | convolution fusion | flops 4833935360 | bytes 11272192 | tf_op jit(solution)/shard_map/dot_general | solution.py:187
  209.4 7.0 %convolution_convert_fusion.1 = bf16[1152,1024]{1,0:T(8,128)(2,1)S(1)} fusion(bf16[2048,1152]{1,0:T(8,128)(2,1)S(1)} %copy-done.49, bf16[512,1024]{1,0:T(8,128)(2,1)} %collective-permute-done.9, bf16[512,1024]{1,0:T(8,128)(2,1)} %collective-permute-done.8, bf16[512,1024]{1,0:T(8,128)(2,1)} %collective-permute-done.7, bf16[512,1024]{1,0:T(8,128)(2,1)} %bitcast.8), kind=kOutput, calls=%fused_computation.15 | convolution fusion | flops 4849795072 | bytes 11272192 | tf_op jit(solution)/shard_map/dot_general | solution.py:36
  217.1 7.9 %convolution_convert_fusion.2 = bf16[1024,1152]{1,0:T(8,128)(2,1)S(1)} fusion(bf16[2048,1152]{1,0:T(8,128)(2,1)S(1)} %bitcast.128, bf16[512,1024]{1,0:T(8,128)(2,1)} %collective-permute-done.4, bf16[512,1024]{1,0:T(8,128)(2,1)} %collective-permute-done.3, bf16[512,1024]{1,0:T(8,128)(2,1)} %collective-permute-done.2, ...), kind=kOutput, calls=%fused_computation.16 | convolution fusion | flops 4849795072 | bytes 11272192 | tf_op jit(solution)/shard_map/dot_general | solution.py:36
  226.7 8.1 %fusion.61 = f32[2048,1024]{1,0:T(8,128)} fusion(bf16[2048,1152]{1,0:T(8,128)(2,1)S(1)} %bitcast.130, bf16[1024,1152]{1,0:T(8,128)(2,1)S(1)} %copy-done.46), kind=kOutput, calls=%fused_computation.192 | convolution fusion | flops 4831838208 | bytes 15466496 | tf_op jit(solution)/shard_map/dot_general | solution.py:42
  234.9 7.4 %convolution_convert_fusion.3 = bf16[1024,1152]{1,0:T(8,128)(2,1)S(1)} fusion(bf16[2048,1152]{1,0:T(8,128)(2,1)S(1)} %bitcast.130, bf16[512,1024]{1,0:T(8,128)(2,1)} %collective-permute-done.4, bf16[512,1024]{1,0:T(8,128)(2,1)} %collective-permute-done.3, bf16[512,1024]{1,0:T(8,128)(2,1)} %collective-permute-done.2, ...), kind=kOutput, calls=%fused_computation.17 | convolution fusion | flops 4849795072 | bytes 11272192 | tf_op jit(solution)/shard_map/dot_general | solution.py:36
  245.5 9.7 %add_convert_fusion = bf16[2048,1024]{1,0:T(8,128)(2,1)S(1)} fusion(f32[2048,1024]{1,0:T(8,128)} %fusion.61, bf16[2048,1152]{1,0:T(8,128)(2,1)} %get-tuple-element.65, bf16[1024,1152]{1,0:T(8,128)(2,1)S(1)} %copy-done.47), kind=kOutput, calls=%fused_computation.5 | convolution fusion | flops 4836032512 | bytes 19660800 | tf_op jit(solution)/shard_map/dot_general | solution.py:42
  258.9 11.7 %collective-permute-done.29 = bf16[512,1152]{1,0:T(8,128)(2,1)S(1)} collective-permute-done((bf16[512,1152]{1,0:T(8,128)(2,1)S(1)}, bf16[512,1152]{1,0:T(8,128)(2,1)S(1)}, u32[]{:S(2)}, u32[]{:S(2)}) %collective-permute-start.29) | collective-permute-done | bytes 1179680 | tf_op jit(solution)/shard_map/ppermute | solution.py:16
  272.5 22.9 %collective-permute-done.23 = bf16[512,1152]{1,0:T(8,128)(2,1)S(1)} collective-permute-done((bf16[512,1152]{1,0:T(8,128)(2,1)S(1)}, bf16[512,1152]{1,0:T(8,128)(2,1)S(1)}, u32[]{:S(2)}, u32[]{:S(2)}) %collective-permute-start.23) | collective-permute-done | bytes 1179680 | tf_op jit(solution)/shard_map/ppermute | solution.py:16
  301.0 21.4 %collective-permute-done.24 = bf16[256,1152]{1,0:T(8,128)(2,1)S(1)} collective-permute-done((bf16[256,1152]{1,0:T(8,128)(2,1)S(1)}, bf16[256,1152]{1,0:T(8,128)(2,1)S(1)}, u32[]{:S(2)}, u32[]{:S(2)}) %collective-permute-start.24) | collective-permute-done | bytes 589856 | tf_op jit(solution)/shard_map/ppermute | solution.py:16
  325.7 17.1 %collective-permute-done.31 = bf16[128,1152]{1,0:T(8,128)(2,1)S(1)} collective-permute-done((bf16[128,1152]{1,0:T(8,128)(2,1)S(1)}, bf16[128,1152]{1,0:T(8,128)(2,1)S(1)}, u32[]{:S(2)}, u32[]{:S(2)}) %collective-permute-start.31) | collective-permute-done | bytes 294944 | tf_op jit(solution)/shard_map/ppermute | solution.py:16
  343.0 9.3 %collective-permute-done.25 = bf16[128,1152]{1,0:T(8,128)(2,1)S(1)} collective-permute-done((bf16[128,1152]{1,0:T(8,128)(2,1)S(1)}, bf16[128,1152]{1,0:T(8,128)(2,1)S(1)}, u32[]{:S(2)}, u32[]{:S(2)}) %collective-permute-start.25) | collective-permute-done | bytes 294944 | tf_op jit(solution)/shard_map/ppermute | solution.py:16
  355.4 9.5 %collective-permute-done.38 = bf16[144,1024]{1,0:T(8,128)(2,1)S(1)} collective-permute-done((bf16[144,1024]{1,0:T(8,128)(2,1)S(1)}, bf16[144,1024]{1,0:T(8,128)(2,1)S(1)}, u32[]{:S(2)}, u32[]{:S(2)}) %collective-permute-start.38) | collective-permute-done | bytes 294944 | tf_op jit(solution)/shard_map/ppermute | solution.py:16
  365.1 6.2 %collective-permute-done.32 = bf16[128,1152]{1,0:T(8,128)(2,1)S(1)} collective-permute-done((bf16[128,1152]{1,0:T(8,128)(2,1)S(1)}, bf16[128,1152]{1,0:T(8,128)(2,1)S(1)}, u32[]{:S(2)}, u32[]{:S(2)}) %collective-permute-start.32) | collective-permute-done | bytes 294944 | tf_op jit(solution)/shard_map/ppermute | solution.py:16
  371.6 5.1 collective-permute-done.26
  376.9 12.4 %collective-permute-done.39 = bf16[288,1024]{1,0:T(8,128)(2,1)S(1)} collective-permute-done((bf16[288,1024]{1,0:T(8,128)(2,1)S(1)}, bf16[288,1024]{1,0:T(8,128)(2,1)S(1)}, u32[]{:S(2)}, u32[]{:S(2)}) %collective-permute-start.39) | collective-permute-done | bytes 589856 | tf_op jit(solution)/shard_map/ppermute | solution.py:16
  391.4 10.5 %collective-permute-done.33 = bf16[256,1152]{1,0:T(8,128)(2,1)S(1)} collective-permute-done((bf16[256,1152]{1,0:T(8,128)(2,1)S(1)}, bf16[256,1152]{1,0:T(8,128)(2,1)S(1)}, u32[]{:S(2)}, u32[]{:S(2)}) %collective-permute-start.33) | collective-permute-done | bytes 589856 | tf_op jit(solution)/shard_map/ppermute | solution.py:16
  405.0 9.5 %collective-permute-done.27 = bf16[256,1152]{1,0:T(8,128)(2,1)S(1)} collective-permute-done((bf16[256,1152]{1,0:T(8,128)(2,1)S(1)}, bf16[256,1152]{1,0:T(8,128)(2,1)S(1)}, u32[]{:S(2)}, u32[]{:S(2)}) %collective-permute-start.27) | collective-permute-done | bytes 589856 | tf_op jit(solution)/shard_map/ppermute | solution.py:16
  423.8 5.4 multiply_reduce_fusion.2
  442.0 4.2 convolution_convert_fusion
  447.7 6.7 %fusion.14 = (f32[512]{0:T(512)S(1)}, f32[512,1024]{1,0:T(8,128)S(1)}) fusion(bf16[1,512,1024]{2,1,0:T(8,128)(2,1)S(1)} %copy-done.18, f32[1024]{0:T(1024)S(1)} %copy-done.34, f32[512]{0:T(512)S(1)} %copy-done.38, bf16[1024,4224]{1,0:T(8,128)(2,1)} %all-gather.2.cloned.1.call-done, bf16[512,1024]{1,0:T(8,128)(2,1)S(1)} %copy-done.25, ...), kind=kOutput, calls=%fused_computation.44 | convolution fusion | flops 3233283584 | bytes 12591104 | tf_op jit(solution)/shard_map/dot_general | solution.py:42
  472.0 45.6 %collective-permute-done.19 = bf16[8,32,1152]{2,1,0:T(8,128)(2,1)S(1)} collective-permute-done((bf16[8,32,1152]{2,1,0:T(8,128)(2,1)S(1)}, bf16[8,32,1152]{2,1,0:T(8,128)(2,1)S(1)}, u32[]{:S(2)}, u32[]{:S(2)}) %collective-permute-start.19) | collective-permute-done | bytes 589856 | tf_op jit(solution)/shard_map/ppermute | solution.py:16
  523.2 4.6 collective-permute-done.20
  528.0 15.5 %collective-permute-done.15 = bf16[4,32,3072]{2,1,0:T(8,128)(2,1)S(1)} collective-permute-done((bf16[4,32,3072]{2,1,0:T(8,128)(2,1)S(1)}, bf16[4,32,3072]{2,1,0:T(8,128)(2,1)S(1)}, u32[]{:S(2)}, u32[]{:S(2)}) %collective-permute-start.15) | collective-permute-done | bytes 786464 | tf_op jit(solution)/shard_map/ppermute | solution.py:16
  546.5 9.0 %collective-permute-done.16 = bf16[2,32,3072]{2,1,0:T(8,128)(2,1)S(1)} collective-permute-done((bf16[2,32,3072]{2,1,0:T(8,128)(2,1)S(1)}, bf16[2,32,3072]{2,1,0:T(8,128)(2,1)S(1)}, u32[]{:S(2)}, u32[]{:S(2)}) %collective-permute-start.16) | collective-permute-done | bytes 393248 | tf_op jit(solution)/shard_map/ppermute | solution.py:16
  557.8 7.9 %collective-permute-done.17 = bf16[1,32,3072]{2,1,0:T(8,128)(2,1)S(1)} collective-permute-done((bf16[1,32,3072]{2,1,0:T(8,128)(2,1)S(1)}, bf16[1,32,3072]{2,1,0:T(8,128)(2,1)S(1)}, u32[]{:S(2)}, u32[]{:S(2)}) %collective-permute-start.17) | collective-permute-done | bytes 196640 | tf_op jit(solution)/shard_map/ppermute | solution.py:16
  (282 shorter events, 106.9 us)
Async XLA Ops:
  7.2 85.4 %all-gather.2.cloned.1.call-start = ((), (), s32[]{:S(2)}) async-start(), calls=%async_computation | async-start | bytes 8921088 | tf_op jit(solution)/shard_map/all_gather | solution.py:138
  111.4 27.7 %collective-permute-start.3 = (bf16[512,1024]{1,0:T(8,128)(2,1)S(1)}, bf16[512,1024]{1,0:T(8,128)(2,1)}, u32[]{:S(2)}, u32[]{:S(2)}) collective-permute-start(bf16[512,1024]{1,0:T(8,128)(2,1)S(1)} %multiply_convert_fusion.6), channel_id=1, source_target_pairs={{0,2},{1,3},{2,0},{3,1},{4,6},{5,7},{6,4},{7,5},{8,10},{9,11},{10,... | collective-permute-start | bytes 3145736 | tf_op jit(solution)/shard_map/ppermute | solution.py:16
  114.9 45.5 %collective-permute-start.8 = (bf16[512,1024]{1,0:T(8,128)(2,1)}, bf16[512,1024]{1,0:T(8,128)(2,1)}, u32[]{:S(2)}, u32[]{:S(2)}) collective-permute-start(bf16[512,1024]{1,0:T(8,128)(2,1)} %bitcast.8), channel_id=1, source_target_pairs={{0,2},{1,3},{2,0},{3,1},{4,6},{5,7},{6,4},{7,5},{8,10},{9,11},{10,... | collective-permute-start | bytes 3145736 | tf_op jit(solution)/shard_map/ppermute | solution.py:16
  115.0 45.4 %collective-permute-start.2 = (bf16[512,1024]{1,0:T(8,128)(2,1)S(1)}, bf16[512,1024]{1,0:T(8,128)(2,1)}, u32[]{:S(2)}, u32[]{:S(2)}) collective-permute-start(bf16[512,1024]{1,0:T(8,128)(2,1)S(1)} %multiply_convert_fusion.6), channel_id=1, source_target_pairs={{0,1},{1,0},{2,3},{3,2},{4,5},{5,4},{6,7},{7,6},{8,9},{9,8},{10,11... | collective-permute-start | bytes 3145736 | tf_op jit(solution)/shard_map/ppermute | solution.py:16
  139.0 44.0 %collective-permute-start.7 = (bf16[512,1024]{1,0:T(8,128)(2,1)}, bf16[512,1024]{1,0:T(8,128)(2,1)}, u32[]{:S(2)}, u32[]{:S(2)}) collective-permute-start(bf16[512,1024]{1,0:T(8,128)(2,1)} %bitcast.8), channel_id=1, source_target_pairs={{0,1},{1,0},{2,3},{3,2},{4,5},{5,4},{6,7},{7,6},{8,9},{9,8},{10,11... | collective-permute-start | bytes 3145736 | tf_op jit(solution)/shard_map/ppermute | solution.py:16
  160.4 22.7 %collective-permute-start.9 = (bf16[512,1024]{1,0:T(8,128)(2,1)}, bf16[512,1024]{1,0:T(8,128)(2,1)}, u32[]{:S(2)}, u32[]{:S(2)}) collective-permute-start(bf16[512,1024]{1,0:T(8,128)(2,1)} %collective-permute-done.8), channel_id=1, source_target_pairs={{0,1},{1,0},{2,3},{3,2},{4,5},{5,4},{6,7},{7,6},{8,9},{9,8},{10,11... | collective-permute-start | bytes 3145736 | tf_op jit(solution)/shard_map/ppermute | solution.py:16
  216.5 39.1 %collective-permute-start.35 = (bf16[576,1024]{1,0:T(8,128)(2,1)S(1)}, bf16[576,1024]{1,0:T(8,128)(2,1)}, u32[]{:S(2)}, u32[]{:S(2)}) collective-permute-start(bf16[576,1024]{1,0:T(8,128)(2,1)S(1)} %constant_dynamic-slice_fusion.2), channel_id=1, source_target_pairs={{0,4},{4,0},{8,12},{12,8},{16,20},{20,16},{24,28},{28,24},{1,5},{5... | collective-permute-start | bytes 3538952 | tf_op jit(solution)/shard_map/ppermute | solution.py:16
  225.2 45.4 %collective-permute-start.29 = (bf16[512,1152]{1,0:T(8,128)(2,1)S(1)}, bf16[512,1152]{1,0:T(8,128)(2,1)S(1)}, u32[]{:S(2)}, u32[]{:S(2)}) collective-permute-start(bf16[512,1152]{1,0:T(8,128)(2,1)S(1)} %constant_dynamic-slice_fusion.5), channel_id=1, source_target_pairs={{0,4},{4,0},{8,12},{12,8},{16,20},{20,16},{24,28},{28,24},{1,5},{5... | collective-permute-start | bytes 3538952 | tf_op jit(solution)/shard_map/ppermute | solution.py:16
  242.3 53.1 %collective-permute-start.23 = (bf16[512,1152]{1,0:T(8,128)(2,1)S(1)}, bf16[512,1152]{1,0:T(8,128)(2,1)S(1)}, u32[]{:S(2)}, u32[]{:S(2)}) collective-permute-start(bf16[512,1152]{1,0:T(8,128)(2,1)S(1)} %constant_dynamic-slice_fusion.8), channel_id=1, source_target_pairs={{0,4},{4,0},{8,12},{12,8},{16,20},{20,16},{24,28},{28,24},{1,5},{5... | collective-permute-start | bytes 3538952 | tf_op jit(solution)/shard_map/ppermute | solution.py:16
  244.0 108.5 %collective-permute-start.5 = (bf16[1024,1024]{1,0:T(8,128)(2,1)S(1)}, bf16[1024,1024]{1,0:T(8,128)(2,1)S(1)}, u32[]{:S(2)}, u32[]{:S(2)}) collective-permute-start(bf16[1024,1024]{1,0:T(8,128)(2,1)S(1)} %pad_maximum_fusion.5), channel_id=1, source_target_pairs={{0,1},{1,0},{2,3},{3,2},{4,5},{5,4},{6,7},{7,6},{8,9},{9,8},{10,11... | collective-permute-start | bytes 6291464 | tf_op jit(solution)/shard_map/ppermute | solution.py:16
  255.5 97.9 %collective-permute-start.10 = (bf16[1024,1024]{1,0:T(8,128)(2,1)S(1)}, bf16[1024,1024]{1,0:T(8,128)(2,1)S(1)}, u32[]{:S(2)}, u32[]{:S(2)}) collective-permute-start(bf16[1024,1024]{1,0:T(8,128)(2,1)S(1)} %pad_maximum_fusion.6), channel_id=1, source_target_pairs={{0,1},{1,0},{2,3},{3,2},{4,5},{5,4},{6,7},{7,6},{8,9},{9,8},{10,11... | collective-permute-start | bytes 6291464 | tf_op jit(solution)/shard_map/ppermute | solution.py:16
  257.3 40.1 %collective-permute-start.36 = (bf16[288,1024]{1,0:T(8,128)(2,1)S(1)}, bf16[288,1024]{1,0:T(8,128)(2,1)S(1)}, u32[]{:S(2)}, u32[]{:S(2)}) collective-permute-start(bf16[288,1024]{1,0:T(8,128)(2,1)S(1)} %constant_dynamic-slice_fusion.1), channel_id=1, source_target_pairs={{0,8},{4,12},{8,0},{12,4},{16,24},{20,28},{24,16},{28,20},{1,9},{5... | collective-permute-start | bytes 1769480 | tf_op jit(solution)/shard_map/ppermute | solution.py:16
  271.0 27.8 %collective-permute-start.30 = (bf16[256,1152]{1,0:T(8,128)(2,1)S(1)}, bf16[256,1152]{1,0:T(8,128)(2,1)S(1)}, u32[]{:S(2)}, u32[]{:S(2)}) collective-permute-start(bf16[256,1152]{1,0:T(8,128)(2,1)S(1)} %constant_dynamic-slice_fusion.4), channel_id=1, source_target_pairs={{0,8},{4,12},{8,0},{12,4},{16,24},{20,28},{24,16},{28,20},{1,9},{5... | collective-permute-start | bytes 1769480 | tf_op jit(solution)/shard_map/ppermute | solution.py:16
  295.8 26.6 %collective-permute-start.24 = (bf16[256,1152]{1,0:T(8,128)(2,1)S(1)}, bf16[256,1152]{1,0:T(8,128)(2,1)S(1)}, u32[]{:S(2)}, u32[]{:S(2)}) collective-permute-start(bf16[256,1152]{1,0:T(8,128)(2,1)S(1)} %constant_dynamic-slice_fusion.7), channel_id=1, source_target_pairs={{0,8},{4,12},{8,0},{12,4},{16,24},{20,28},{24,16},{28,20},{1,9},{5... | collective-permute-start | bytes 1769480 | tf_op jit(solution)/shard_map/ppermute | solution.py:16
  297.7 25.1 %collective-permute-start.37 = (bf16[144,1024]{1,0:T(8,128)(2,1)S(1)}, bf16[144,1024]{1,0:T(8,128)(2,1)S(1)}, u32[]{:S(2)}, u32[]{:S(2)}) collective-permute-start(bf16[144,1024]{1,0:T(8,128)(2,1)S(1)} %constant_dynamic-slice_fusion), channel_id=1, source_target_pairs={{0,16},{4,20},{8,24},{12,28},{16,0},{20,4},{24,8},{28,12},{1,17},{... | collective-permute-start | bytes 884744 | tf_op jit(solution)/shard_map/ppermute | solution.py:16
  298.9 43.9 %collective-permute-start.31 = (bf16[128,1152]{1,0:T(8,128)(2,1)S(1)}, bf16[128,1152]{1,0:T(8,128)(2,1)S(1)}, u32[]{:S(2)}, u32[]{:S(2)}) collective-permute-start(bf16[128,1152]{1,0:T(8,128)(2,1)S(1)} %constant_dynamic-slice_fusion.3), channel_id=1, source_target_pairs={{0,16},{4,20},{8,24},{12,28},{16,0},{20,4},{24,8},{28,12},{1,17},{... | collective-permute-start | bytes 884744 | tf_op jit(solution)/shard_map/ppermute | solution.py:16
  322.6 29.7 %collective-permute-start.25 = (bf16[128,1152]{1,0:T(8,128)(2,1)S(1)}, bf16[128,1152]{1,0:T(8,128)(2,1)S(1)}, u32[]{:S(2)}, u32[]{:S(2)}) collective-permute-start(bf16[128,1152]{1,0:T(8,128)(2,1)S(1)} %constant_dynamic-slice_fusion.6), channel_id=1, source_target_pairs={{0,16},{4,20},{8,24},{12,28},{16,0},{20,4},{24,8},{28,12},{1,17},{... | collective-permute-start | bytes 884744 | tf_op jit(solution)/shard_map/ppermute | solution.py:16
  322.9 42.1 %collective-permute-start.38 = (bf16[144,1024]{1,0:T(8,128)(2,1)S(1)}, bf16[144,1024]{1,0:T(8,128)(2,1)S(1)}, u32[]{:S(2)}, u32[]{:S(2)}) collective-permute-start(bf16[144,1024]{1,0:T(8,128)(2,1)S(1)} %add_convert_fusion.12), channel_id=1, source_target_pairs={{0,16},{4,20},{8,24},{12,28},{16,0},{20,4},{24,8},{28,12},{1,17},{... | collective-permute-start | bytes 884744 | tf_op jit(solution)/shard_map/ppermute | solution.py:16
  342.9 28.5 %collective-permute-start.32 = (bf16[128,1152]{1,0:T(8,128)(2,1)S(1)}, bf16[128,1152]{1,0:T(8,128)(2,1)S(1)}, u32[]{:S(2)}, u32[]{:S(2)}) collective-permute-start(bf16[128,1152]{1,0:T(8,128)(2,1)S(1)} %add_convert_fusion.13), channel_id=1, source_target_pairs={{0,16},{4,20},{8,24},{12,28},{16,0},{20,4},{24,8},{28,12},{1,17},{... | collective-permute-start | bytes 884744 | tf_op jit(solution)/shard_map/ppermute | solution.py:16
  352.4 24.3 %collective-permute-start.26 = (bf16[128,1152]{1,0:T(8,128)(2,1)S(1)}, bf16[128,1152]{1,0:T(8,128)(2,1)S(1)}, u32[]{:S(2)}, u32[]{:S(2)}) collective-permute-start(bf16[128,1152]{1,0:T(8,128)(2,1)S(1)} %add_convert_fusion.14), channel_id=1, source_target_pairs={{0,16},{4,20},{8,24},{12,28},{16,0},{20,4},{24,8},{28,12},{1,17},{... | collective-permute-start | bytes 884744 | tf_op jit(solution)/shard_map/ppermute | solution.py:16
  352.9 64.4 %collective-permute-start.6 = (bf16[512,1024]{1,0:T(8,128)(2,1)S(1)}, bf16[512,1024]{1,0:T(8,128)(2,1)S(1)}, u32[]{:S(2)}, u32[]{:S(2)}) collective-permute-start(bf16[512,1024]{1,0:T(8,128)(2,1)S(1)} %add_convert_fusion.7), channel_id=1, source_target_pairs={{0,2},{1,3},{2,0},{3,1},{4,6},{5,7},{6,4},{7,5},{8,10},{9,11},{10,... | collective-permute-start | bytes 3145736 | tf_op jit(solution)/shard_map/ppermute | solution.py:16
  353.9 62.5 %collective-permute-start.11 = (bf16[512,1024]{1,0:T(8,128)(2,1)S(1)}, bf16[512,1024]{1,0:T(8,128)(2,1)S(1)}, u32[]{:S(2)}, u32[]{:S(2)}) collective-permute-start(bf16[512,1024]{1,0:T(8,128)(2,1)S(1)} %add_convert_fusion.4), channel_id=1, source_target_pairs={{0,2},{1,3},{2,0},{3,1},{4,6},{5,7},{6,4},{7,5},{8,10},{9,11},{10,... | collective-permute-start | bytes 3145736 | tf_op jit(solution)/shard_map/ppermute | solution.py:16
  365.0 24.3 %collective-permute-start.39 = (bf16[288,1024]{1,0:T(8,128)(2,1)S(1)}, bf16[288,1024]{1,0:T(8,128)(2,1)S(1)}, u32[]{:S(2)}, u32[]{:S(2)}) collective-permute-start(bf16[288,1024]{1,0:T(8,128)(2,1)S(1)} %pad_maximum_fusion.16), channel_id=1, source_target_pairs={{0,8},{4,12},{8,0},{12,4},{16,24},{20,28},{24,16},{28,20},{1,9},{5... | collective-permute-start | bytes 1769480 | tf_op jit(solution)/shard_map/ppermute | solution.py:16
  371.5 30.5 %collective-permute-start.33 = (bf16[256,1152]{1,0:T(8,128)(2,1)S(1)}, bf16[256,1152]{1,0:T(8,128)(2,1)S(1)}, u32[]{:S(2)}, u32[]{:S(2)}) collective-permute-start(bf16[256,1152]{1,0:T(8,128)(2,1)S(1)} %pad_maximum_fusion.15), channel_id=1, source_target_pairs={{0,8},{4,12},{8,0},{12,4},{16,24},{20,28},{24,16},{28,20},{1,9},{5... | collective-permute-start | bytes 1769480 | tf_op jit(solution)/shard_map/ppermute | solution.py:16
  376.8 37.7 %collective-permute-start.27 = (bf16[256,1152]{1,0:T(8,128)(2,1)S(1)}, bf16[256,1152]{1,0:T(8,128)(2,1)S(1)}, u32[]{:S(2)}, u32[]{:S(2)}) collective-permute-start(bf16[256,1152]{1,0:T(8,128)(2,1)S(1)} %pad_maximum_fusion.14), channel_id=1, source_target_pairs={{0,8},{4,12},{8,0},{12,4},{16,24},{20,28},{24,16},{28,20},{1,9},{5... | collective-permute-start | bytes 1769480 | tf_op jit(solution)/shard_map/ppermute | solution.py:16
  390.8 65.5 %collective-permute-start.40 = (bf16[576,1024]{1,0:T(8,128)(2,1)}, bf16[576,1024]{1,0:T(8,128)(2,1)}, u32[]{:S(2)}, u32[]{:S(2)}) collective-permute-start(bf16[576,1024]{1,0:T(8,128)(2,1)} %pad_maximum_fusion.11), channel_id=1, source_target_pairs={{0,4},{4,0},{8,12},{12,8},{16,20},{20,16},{24,28},{28,24},{1,5},{5... | collective-permute-start | bytes 3538952 | tf_op jit(solution)/shard_map/ppermute | solution.py:16
  404.4 56.5 %collective-permute-start.34 = (bf16[512,1152]{1,0:T(8,128)(2,1)}, bf16[512,1152]{1,0:T(8,128)(2,1)}, u32[]{:S(2)}, u32[]{:S(2)}) collective-permute-start(bf16[512,1152]{1,0:T(8,128)(2,1)} %pad_maximum_fusion.10), channel_id=1, source_target_pairs={{0,4},{4,0},{8,12},{12,8},{16,20},{20,16},{24,28},{28,24},{1,5},{5... | collective-permute-start | bytes 3538952 | tf_op jit(solution)/shard_map/ppermute | solution.py:16
  415.8 54.5 %collective-permute-start.28 = (bf16[512,1152]{1,0:T(8,128)(2,1)}, bf16[512,1152]{1,0:T(8,128)(2,1)}, u32[]{:S(2)}, u32[]{:S(2)}) collective-permute-start(bf16[512,1152]{1,0:T(8,128)(2,1)} %pad_maximum_fusion.9), channel_id=1, source_target_pairs={{0,4},{4,0},{8,12},{12,8},{16,20},{20,16},{24,28},{28,24},{1,5},{5... | collective-permute-start | bytes 3538952 | tf_op jit(solution)/shard_map/ppermute | solution.py:16
  439.8 25.3 %collective-permute-start.18 = (bf16[16,32,1152]{2,1,0:T(8,128)(2,1)}, bf16[16,32,1152]{2,1,0:T(8,128)(2,1)}, u32[]{:S(2)}, u32[]{:S(2)}) collective-permute-start(bf16[16,32,1152]{2,1,0:T(8,128)(2,1)} %dynamic-slice_bitcast_fusion.2), channel_id=1, source_target_pairs={{0,1},{1,0},{2,3},{3,2},{4,5},{5,4},{6,7},{7,6},{8,9},{9,8},{10,11... | collective-permute-start | bytes 3538952 | tf_op jit(solution)/shard_map/ppermute | solution.py:16
  468.1 51.3 %collective-permute-start.14 = (bf16[8,32,3072]{2,1,0:T(8,128)(2,1)S(1)}, bf16[8,32,3072]{2,1,0:T(8,128)(2,1)S(1)}, u32[]{:S(2)}, u32[]{:S(2)}) collective-permute-start(bf16[8,32,3072]{2,1,0:T(8,128)(2,1)S(1)} %dynamic-slice_bitcast_fusion.1), channel_id=1, source_target_pairs={{0,2},{1,3},{2,0},{3,1},{4,6},{5,7},{6,4},{7,5},{8,10},{9,11},{10,... | collective-permute-start | bytes 4718600 | tf_op jit(solution)/shard_map/ppermute | solution.py:16
  469.7 48.0 %collective-permute-start.19 = (bf16[8,32,1152]{2,1,0:T(8,128)(2,1)S(1)}, bf16[8,32,1152]{2,1,0:T(8,128)(2,1)S(1)}, u32[]{:S(2)}, u32[]{:S(2)}) collective-permute-start(bf16[8,32,1152]{2,1,0:T(8,128)(2,1)S(1)} %dynamic-slice_bitcast_fusion.4), channel_id=1, source_target_pairs={{0,2},{1,3},{2,0},{3,1},{4,6},{5,7},{6,4},{7,5},{8,10},{9,11},{10,... | collective-permute-start | bytes 1769480 | tf_op jit(solution)/shard_map/ppermute | solution.py:16
  520.1 23.5 %collective-permute-start.15 = (bf16[4,32,3072]{2,1,0:T(8,128)(2,1)S(1)}, bf16[4,32,3072]{2,1,0:T(8,128)(2,1)S(1)}, u32[]{:S(2)}, u32[]{:S(2)}) collective-permute-start(bf16[4,32,3072]{2,1,0:T(8,128)(2,1)S(1)} %dynamic-slice_bitcast_fusion.3), channel_id=1, source_target_pairs={{0,4},{4,0},{8,12},{12,8},{16,20},{20,16},{24,28},{28,24},{1,5},{5... | collective-permute-start | bytes 2359304 | tf_op jit(solution)/shard_map/ppermute | solution.py:16
  (66 other events, 782.0 us)
Sparse Core Ops, SparseCore 0:
  11.5 81.0 all-gather.1

commit v2 on v1

--- a/solution.py
+++ b/solution.py
@@ -1,12 +1,21 @@
 import jax
 import jax.numpy as jnp
 from jax import lax
+from jax.experimental import pallas as pl
+from jax.experimental.pallas import tpu as pltpu
 from jax.sharding import PartitionSpec as P
 
 KERNEL = 3
 LANES = 128
 BF16 = jnp.bfloat16
 F32 = jnp.float32
+HALVINGS = 3
+PARTS = 1 << HALVINGS
+ORDER = [int(format(q, "03b")[::-1], 2) for q in range(PARTS)]
+NN = (((1,), (0,)), ((), ()))
+NT = (((1,), (1,)), ((), ()))
+TN = (((0,), (0,)), ((), ()))
+VMEM_LIMIT = 60 * 1024 * 1024
 
 epsilon = 1e-05
 
@@ -32,16 +41,192 @@
     return size.bit_length() - 1
 
 
+def dot(left, right, dims):
+    return lax.dot_general(left, right, dims, preferred_element_type=F32)
+
+
 def inner_rows(left, right):
-    return lax.dot_general(
-        left, right, (((0,), (0,)), ((), ())), preferred_element_type=F32
-    )
+    return dot(left, right, TN)
 
 
 def inner_cols(left, right):
-    return lax.dot_general(
-        left, right, (((1,), (1,)), ((), ())), preferred_element_type=F32
-    )
+    return dot(left, right, NT)
+
+
+def hidden_blocks(hidden):
+    wide = [(256, n) for n in range(hidden // 256)]
+    rest = hidden % 256
+    assert rest in (0, 128)
+    return wide + ([(128, hidden // 128 - 1)] if rest else [])
+
+
+def feed(x_ref, go_ref, gate_ref, up_ref, down_ref, hid_ref, gl_ref, ul_ref):
+    tokens = x_ref.shape[0]
+    step = min(tokens, 512)
+    for start in range(0, tokens, step):
+        part = slice(start, start + step)
+        gate_val = dot(x_ref[part], gate_ref[...], NN)
+        up_val = dot(x_ref[part], up_ref[...], NN)
+        hidden_grad = dot(go_ref[part], down_ref[...], NT)
+        sig = 1.0 / (1.0 + jnp.exp(-gate_val))
+        silu = gate_val * sig
+        hid_ref[part] = (silu * up_val).astype(BF16)
+        gl_ref[part] = (hidden_grad * up_val * (sig * (1.0 + gate_val * (1.0 - sig)))).astype(BF16)
+        ul_ref[part] = (hidden_grad * silu).astype(BF16)
+
+
+def join(first, xa_ref, xb_ref, ga_ref, gb_ref, x_ref, go_ref):
+    rows = xa_ref.shape[0]
+
+    @pl.when(first)
+    def _():
+        x_ref[:rows] = xa_ref[...]
+        x_ref[rows:] = xb_ref[...]
+        go_ref[:rows] = ga_ref[...]
+        go_ref[rows:] = gb_ref[...]
+
+
+def near_kernel(xa_ref, xb_ref, ga_ref, gb_ref, gate_ref, up_ref, down_ref,
+                hid_ref, gl_ref, ul_ref, og_ref, ou_ref, od_ref, x_ref, go_ref):
+    join(pl.program_id(0) == 0, xa_ref, xb_ref, ga_ref, gb_ref, x_ref, go_ref)
+    feed(x_ref, go_ref, gate_ref, up_ref, down_ref, hid_ref, gl_ref, ul_ref)
+    og_ref[...] = dot(x_ref[...], gl_ref[...], TN)
+    ou_ref[...] = dot(x_ref[...], ul_ref[...], TN)
+    od_ref[...] = dot(hid_ref[...], go_ref[...], TN)
+
+
+def near_feed(xs, gos, gate, up, down):
+    rows, features = xs[0].shape
+    hidden = gate.shape[1]
+    wide = 256
+    tokens = 2 * rows
+    whole = pl.BlockSpec((rows, features), lambda i: (0, 0), pipeline_mode=pl.Buffered(1))
+    col = pl.BlockSpec((features, wide), lambda i: (0, i))
+    row = pl.BlockSpec((wide, features), lambda i: (i, 0))
+    act = pl.BlockSpec((tokens, wide), lambda i: (0, i))
+    return pl.pallas_call(
+        near_kernel,
+        grid=(pl.cdiv(hidden, wide),),
+        in_specs=[whole] * 4 + [col, col, row],
+        out_specs=[act] * 3 + [col, col, row],
+        out_shape=[jax.ShapeDtypeStruct((tokens, hidden), BF16)] * 3
+        + [jax.ShapeDtypeStruct((features, hidden), F32)] * 2
+        + [jax.ShapeDtypeStruct((hidden, features), F32)],
+        scratch_shapes=[pltpu.VMEM((tokens, features), BF16)] * 2,
+        compiler_params=pltpu.CompilerParams(vmem_limit_bytes=VMEM_LIMIT),
+        cost_estimate=pl.CostEstimate(
+            flops=12 * tokens * features * hidden,
+            transcendentals=tokens * hidden,
+            bytes_accessed=18 * features * hidden + 6 * tokens * hidden + 4 * tokens * features,
+        ),
+        name="near_feed",
+    )(*xs, *gos, gate, up, down)
+
+
+def far_kernel(place_ref, xa_ref, xb_ref, ga_ref, gb_ref, gate_ref, up_ref, down_ref,
+               ng_ref, nu_ref, nd_ref, hid_ref, gl_ref, ul_ref, kept_ref, sent_ref,
+               x_ref, go_ref, tg_ref, tu_ref, td_ref):
+    join(pl.program_id(0) == 0, xa_ref, xb_ref, ga_ref, gb_ref, x_ref, go_ref)
+    feed(x_ref, go_ref, gate_ref, up_ref, down_ref, hid_ref, gl_ref, ul_ref)
+    tg_ref[...] = ng_ref[...] + dot(x_ref[...], gl_ref[...], TN)
+    tu_ref[...] = nu_ref[...] + dot(x_ref[...], ul_ref[...], TN)
+    td_ref[...] = nd_ref[...] + dot(hid_ref[...], go_ref[...], TN)
+    features, wide = tg_ref.shape
+    tall, low = features // PARTS, wide // PARTS
+    for q in range(PARTS):
+        part = place_ref[0] ^ ORDER[q]
+        out = kept_ref.at[q] if q < PARTS // 2 else sent_ref.at[q - PARTS // 2]
+        rows = pl.ds(pl.multiple_of(part * tall, tall), tall)
+        at = 0
+        for grad_ref in (tg_ref, tu_ref):
+            for c in range(0, wide, LANES):
+                out[at : at + tall] = grad_ref[rows, c : c + LANES].astype(BF16)
+                at += tall
+        rows = pl.ds(pl.multiple_of(part * low, low), low)
+        for c in range(0, features, LANES):
+            out[at : at + low] = td_ref[rows, c : c + LANES].astype(BF16)
+            at += low
+
+
+def far_feed(place, xs, gos, gate, up, down, near_grads, wide, index):
+    rows, features = xs[0].shape
+    tokens = 2 * rows
+    whole = pl.BlockSpec((rows, features), lambda i, _: (0, 0), pipeline_mode=pl.Buffered(1))
+    col = pl.BlockSpec((features, wide), lambda i, _: (0, index))
+    row = pl.BlockSpec((wide, features), lambda i, _: (index, 0))
+    act = pl.BlockSpec((tokens, wide), lambda i, _: (0, 0))
+    packed = 3 * features * wide // PARTS // LANES
+    half = pl.BlockSpec((PARTS // 2, packed, LANES), lambda i, _: (0, 0, 0))
+    return pl.pallas_call(
+        far_kernel,
+        grid_spec=pltpu.PrefetchScalarGridSpec(
+            num_scalar_prefetch=1,
+            grid=(1,),
+            in_specs=[whole] * 4 + [col, col, row] + [col, col, row],
+            out_specs=[act] * 3 + [half] * 2,
+            scratch_shapes=[pltpu.VMEM((tokens, features), BF16)] * 2
+            + [pltpu.VMEM((features, wide), F32)] * 2
+            + [pltpu.VMEM((wide, features), F32)],
+        ),
+        out_shape=[jax.ShapeDtypeStruct((tokens, wide), BF16)] * 3
+        + [jax.ShapeDtypeStruct((PARTS // 2, packed, LANES), BF16)] * 2,
+        compiler_params=pltpu.CompilerParams(vmem_limit_bytes=VMEM_LIMIT),
+        cost_estimate=pl.CostEstimate(
+            flops=12 * tokens * features * wide,
+            transcendentals=tokens * wide,
+            bytes_accessed=24 * features * wide + 6 * tokens * wide + 4 * tokens * features,
+        ),
+        name="far_feed",
+    )(place, *xs, *gos, gate, up, down, *near_grads)
+
+
+def unpack_kernel(place_ref, own_ref, two_ref, four_ref, eight_ref, *refs):
+    og_ref, ou_ref, od_ref = refs[-3:]
+    features, wide = og_ref.shape
+    tall, low = features // PARTS, wide // PARTS
+    sources = [own_ref.at[0], two_ref.at[0]]
+    sources += [four_ref.at[n] for n in range(2)]
+    sources += [eight_ref.at[n] for n in range(4)]
+    for q in range(PARTS):
+        part = place_ref[0] ^ ORDER[q]
+        source = sources[q]
+        rows = pl.ds(pl.multiple_of(part * tall, tall), tall)
+        at = 0
+        for out in (og_ref, ou_ref):
+            for c in range(0, wide, LANES):
+                out[rows, c : c + LANES] = source[at : at + tall].astype(F32)
+                at += tall
+        rows = pl.ds(pl.multiple_of(part * low, low), low)
+        for c in range(0, features, LANES):
+            od_ref[rows, c : c + LANES] = source[at : at + low].astype(F32)
+            at += low
+
+
+def unpack(place, pieces, before, wide, index, features, hidden):
+    packed = pieces[0].shape[1]
+    ins = [
+        pl.BlockSpec((piece.shape[0], packed, LANES), lambda i, _: (0, 0, 0)) for piece in pieces
+    ]
+    col = pl.BlockSpec((features, wide), lambda i, _: (0, index))
+    row = pl.BlockSpec((wide, features), lambda i, _: (index, 0))
+    keep = [pl.BlockSpec(memory_space=pl.ANY)] * len(before)
+    return pl.pallas_call(
+        unpack_kernel,
+        grid_spec=pltpu.PrefetchScalarGridSpec(
+            num_scalar_prefetch=1,
+            grid=(1,),
+            in_specs=ins + keep,
+            out_specs=[col, col, row],
+        ),
+        out_shape=[jax.ShapeDtypeStruct((features, hidden), F32)] * 2
+        + [jax.ShapeDtypeStruct((hidden, features), F32)],
+        input_output_aliases={1 + len(ins) + n: n for n in range(len(before))},
+        compiler_params=pltpu.CompilerParams(vmem_limit_bytes=VMEM_LIMIT),
+        cost_estimate=pl.CostEstimate(
+            flops=0, transcendentals=0, bytes_accessed=18 * features * wide
+        ),
+        name="unpack",
+    )(place, *pieces, *before)
 
 
 def add_low(one, two):
@@ -49,51 +234,38 @@
 
 
 def gather_mp(own):
-    blocks = [own]
-    for bit in reversed(range(bits_of("mp"))):
-        blocks = blocks + [None] * len(blocks)
     size = lax.axis_size("mp")
     blocks = [own] + [None] * (size - 1)
     for bit in reversed(range(bits_of("mp"))):
-        have = [r for r in range(size) if blocks[r] is not None]
-        for r in have:
+        for r in [r for r in range(size) if blocks[r] is not None]:
             blocks[r ^ (1 << bit)] = swap(blocks[r], "mp", bit)
     return blocks
 
 
-def scatter_mp(blocks):
-    held = {r: block for r, block in enumerate(blocks)}
-    for bit in range(bits_of("mp")):
-        sent = [r for r in held if r >> bit & 1]
-        kept = [r for r in held if not r >> bit & 1]
-        got = swap(jnp.concatenate([held[r] for r in sent], 0), "mp", bit)
-        rows = got.shape[0] // len(sent)
-        for n, r in enumerate(sent):
-            there = r ^ (1 << bit)
-            held[there] = held[there].astype(F32) + got[n * rows : (n + 1) * rows].astype(F32)
-        final = bit == bits_of("mp") - 1
-        held = {r: held[r] if final else held[r].astype(BF16) for r in kept}
-    return held[0]
-
-
-def sum_dp(array):
-    count = bits_of("dp")
-    halved = list(range(min(count, 3)))
-    for bit in halved:
-        half = array.shape[0] // 2
-        mine = bit_of("dp", bit)
-        sent = lax.dynamic_slice_in_dim(array, (1 - mine) * half, half, 0)
-        kept = lax.dynamic_slice_in_dim(array, mine * half, half, 0)
-        array = add_low(kept, swap(sent, "dp", bit))
-    for bit in range(len(halved), count):
-        array = add_low(array, swap(array, "dp", bit))
-    for bit in reversed(halved):
-        got = swap(array, "dp", bit)
-        low_first = bit_of("dp", bit) == 0
-        array = jnp.concatenate(
-            [jnp.where(low_first, array, got), jnp.where(low_first, got, array)], 0
-        )
-    return array
+def scatter_mp(near, far):
+    rows = near.shape[0] // 2
+    got_far = swap(far[rows:], "mp", 0)
+    got_near = swap(near[rows:], "mp", 0)
+    got = swap(add_low(far[:rows], got_far), "mp", 1)
+    return near[:rows].astype(F32) + got_near.astype(F32) + got.astype(F32)
+
+
+def sum_dp(kept, sent):
+    for bit in range(HALVINGS):
+        got = swap(sent, "dp", bit)
+        half = kept.shape[0] // 2
+        if half:
+            sent = add_low(kept[half:], got[half:])
+            kept = add_low(kept[:half], got[:half])
+        else:
+            kept = add_low(kept, got)
+    for bit in range(HALVINGS, bits_of("dp")):
+        kept = add_low(kept, swap(kept, "dp", bit))
+    pieces = [kept]
+    for bit in reversed(range(HALVINGS)):
+        held = jnp.concatenate(pieces, 0) if len(pieces) > 1 else pieces[0]
+        pieces = pieces + [swap(held, "dp", bit)]
+    return pieces
 
 
 def scatter_all(array):
@@ -143,49 +315,64 @@
 
     group_grad = gather_mp(cotangent)
 
-    inverse_one = lax.rsqrt(jnp.mean(x * x, axis=-1, keepdims=True) + epsilon)
+    pad = 8
+    rim = shift(block_in.reshape(rows, features)[rows - pad :], "mp", 1)
+    rim_ids = shift(own_ids[rows - pad :].astype(F32), "mp", 1).astype(jnp.int32)
+    rim_ids = jnp.where(lax.axis_index("mp") == 0, -1, rim_ids)
+    x_all = jnp.concatenate([rim.astype(F32), x], 0)
+    inverse_all = lax.rsqrt(jnp.mean(x_all * x_all, axis=-1, keepdims=True) + epsilon)
+    low_all = (x_all * inverse_all * gain_one).astype(BF16)
+    mixer_all = jnp.dot(low_all, weight_in, preferred_element_type=F32)
+    extended = mixer_all[:, :features] * mixer_all[:, 2 * features :]
+    inverse_one = inverse_all[pad:]
     unit_one = x * inverse_one
-    first_low = (unit_one * gain_one).astype(BF16)
-    mixer = jnp.dot(first_low, weight_in, preferred_element_type=F32)
+    first_low = low_all[pad:]
+    mixer = mixer_all[pad:]
     opening = mixer[:, :features]
     closing = mixer[:, features : 2 * features]
     carried = mixer[:, 2 * features :]
-    product = opening * carried
-    rim_rows = shift(product[rows - lookback :], "mp", 1)
-    rim_ids = shift(own_ids[rows - lookback :].astype(F32), "mp", 1).astype(jnp.int32)
-    first = lax.axis_index("mp") == 0
-    rim_ids = jnp.where(first, -1, rim_ids)
-    extended = jnp.concatenate([rim_rows, product], 0)
     extended_ids = jnp.concatenate([rim_ids, own_ids], 0)
+    skip = pad - lookback
     same = [
-        (extended_ids[k : k + rows] == own_ids)[:, None] for k in range(KERNEL)
+        (extended_ids[skip + k : skip + k + rows] == own_ids)[:, None] for k in range(KERNEL)
     ]
-    past = [jnp.where(same[k], extended[k : k + rows], 0.0) for k in range(KERNEL)]
+    past = [
+        jnp.where(same[k], extended[skip + k : skip + k + rows], 0.0) for k in range(KERNEL)
+    ]
     conv = sum(past[k] * taps[k] for k in range(KERNEL))
     gated_low = (closing * conv).astype(BF16)
     residual = x + jnp.dot(gated_low, weight_out, preferred_element_type=F32)
     inverse_two = lax.rsqrt(jnp.mean(residual * residual, axis=-1, keepdims=True) + epsilon)
     second_low = (residual * inverse_two * gain_two).astype(BF16)
 
-    group = jnp.concatenate(gather_mp(second_low), 0)
-    grads = jnp.concatenate(group_grad, 0)
-    gate_val = jnp.dot(group, gate_proj, preferred_element_type=F32)
-    up_val = jnp.dot(group, up_proj, preferred_element_type=F32)
-    sig = jax.nn.sigmoid(gate_val)
-    silu = gate_val * sig
-    hidden = (silu * up_val).astype(BF16)
-    down_local = inner_rows(hidden, grads).astype(BF16)
-    grad_down = sum_dp(down_local).astype(F32)
-    hidden_grad = inner_cols(grads, down_proj)
-    gate_low = (hidden_grad * up_val * sig * (1 + gate_val * (1 - sig))).astype(BF16)
-    up_low = (hidden_grad * silu).astype(BF16)
-    second_parts = (inner_cols(gate_low, gate_proj) + inner_cols(up_low, up_proj)).astype(BF16)
-    size = lax.axis_size("mp")
-    second_grad = scatter_mp([second_parts[r * rows : (r + 1) * rows] for r in range(size)])
-    grad_gate = sum_dp(inner_rows(group, gate_low).astype(BF16)).astype(F32)
-    grad_up = sum_dp(inner_rows(group, up_low).astype(BF16)).astype(F32)
-    branch_parts = jnp.dot(hidden, down_proj, preferred_element_type=F32).astype(BF16)
-    branch = scatter_mp([branch_parts[r * rows : (r + 1) * rows] for r in range(size)])
+    group = gather_mp(second_low)
+    hidden_units = gate_proj.shape[1]
+    place = (lax.axis_index("dp") % PARTS).reshape(1).astype(jnp.int32)
+    hid_near, gl_near, ul_near, *near_grads = near_feed(
+        group[:2], group_grad[:2], gate_proj, up_proj, down_proj
+    )
+    blocks = hidden_blocks(hidden_units)
+    far_parts, packed = [], []
+    for wide, index in blocks:
+        *acts, kept, sent = far_feed(
+            place, group[2:], group_grad[2:], gate_proj, up_proj, down_proj, near_grads, wide, index
+        )
+        far_parts.append(acts)
+        packed.append((kept, sent))
+    hid_far, gl_far, ul_far = (jnp.concatenate(parts, 1) for parts in zip(*far_parts))
+
+    def back(gate_low, up_low):
+        return (inner_cols(gate_low, gate_proj) + inner_cols(up_low, up_proj)).astype(BF16)
+
+    def onward(hid):
+        return dot(hid, down_proj, NN).astype(BF16)
+
+    second_grad = scatter_mp(back(gl_near, ul_near), back(gl_far, ul_far))
+    branch = scatter_mp(onward(hid_near), onward(hid_far))
+    done = ()
+    for (wide, index), (kept, sent) in zip(blocks, packed):
+        done = unpack(place, sum_dp(kept, sent), done, wide, index, features, hidden_units)
+    grad_gate, grad_up, grad_down = done
     layer_out = (residual + branch).astype(BF16).reshape(1, rows, features)
 
     unit_two = residual * inverse_two

time: 578 us -> 526 us (0.910)
  Pallas kernels: 0 us -> 80.1 us
  waiting for transfers between devices: 341 us -> 261 us
  matrix products: 116 us -> 45.9 us
  starting transfers between devices: 37.9 us -> 55.7 us
  local copies, waits for them, and re-layouts: 15.5 us -> 29.6 us
  other arithmetic: 48.2 us -> 34.6 us
    pallas_call x0 -> x11, Pallas kernels: none -> 80.1 us  [the longest x5 41.3 us: far_feed(): pl.pallas_call(far_kernel, grid_spec=pltpu.PrefetchScalarGridSpec(num_sca...]
    ppermute x38 -> x52, waiting for transfers between devices: 264 us -> 187 us  [swap(): return lax.ppermute(block, axis, [(i, i ^ 1 << bit) for i in range(size)])]
    dot_general x14 -> x11, matrix products: 112 us -> 42.6 us  [the longest x10 36.6 us: dot(): return lax.dot_general(left, right, dims, preferred_element_type=F32)]
    ppermute x38 -> x52, starting transfers between devices: 31.4 us -> 50 us  [swap(): return lax.ppermute(block, axis, [(i, i ^ 1 << bit) for i in range(size)])]
    unnamed x114 -> x193, local copies, waits for them, and re-layouts: 7.13 us -> 15.8 us
    convert_element_type x6 -> x4, other arithmetic: 9.22 us -> 2.44 us  [the longest x1 1.47 us: per_device(): x = block_in.reshape(rows, features).astype(F32)]
    select_n x10 -> x1, other arithmetic: 6.14 us -> 0.01 us  [per_device(): rim_ids = jnp.where(lax.axis_index('mp') == 0, -1, rim_ids)]
  transfers between devices with their start and end apart: 42 -> 56, of which waited for: 20 -> 28; matrix products, arithmetic and copies ran while one was open for 21% -> 18% of each run, Pallas kernels for 0% -> 15%
where the time goes in v2:
time: 526 us; the launch traced here: 523 us
  waiting for transfers between devices  261 us (50%)
  Pallas kernels  80.1 us (15%)
  starting transfers between devices  55.7 us (11%)
  matrix products  45.9 us (9%)
  other arithmetic  34.6 us (7%)
  local copies, waits for them, and re-layouts  29.6 us (6%)
  between operations  15.7 us (3%)
    ppermute x52, waiting for transfers between devices, swap(): return lax.ppermute(block, axis, [(i, i ^ 1 << bit) for i in range(size)])  187 us
    all_gather x1, waiting for transfers between devices, per_device(): everything = lax.all_gather(packed, ('dp', 'mp'), axis=0, tiled=True)  72.6 us
    ppermute x52, starting transfers between devices, swap(): return lax.ppermute(block, axis, [(i, i ^ 1 << bit) for i in range(size)])  50 us
    pallas_call x5, Pallas kernels, far_feed(): pl.pallas_call(far_kernel, grid_spec=pltpu.PrefetchScalarGridSpec(num_sca...  41.3 us
    dot_general x10, matrix products, dot(): return lax.dot_general(left, right, dims, preferred_element_type=F32)  36.6 us
    pallas_call x1, Pallas kernels, near_feed(): pl.pallas_call(near_kernel, grid=(pl.cdiv(hidden, wide),), in_specs=[whol...  23.1 us
    unnamed x193, local copies, waits for them, and re-layouts  15.8 us
    pallas_call x5, Pallas kernels, unpack(): pl.pallas_call(unpack_kernel, grid_spec=pltpu.PrefetchScalarGridSpec(num_...  15.7 us
  transfers between devices with their start and end apart: 56, of which 28 were waited for; matrix products, arithmetic and copies ran while one was open for 18% of the time, Pallas kernels for 15%

profile of v2, /device:TPU:0, one launch (start us, length us, event | category | flops | bytes accessed | tf_op | source)
XLA Modules:
  0.0 523.1 jit_solution(3614651001895737131)
XLA Ops:
  21.6 72.6 %all-gather.2.cloned.1.call-done = bf16[1024,4224]{1,0:T(8,128)(2,1)} async-done(((bf16[32,4224]{1,0:T(8,128)(2,1)}), bf16[1024,4224]{1,0:T(8,128)(2,1)}) %all-gather.2.cloned.1.call-update) | async-done | bytes 8650768 | tf_op jit(solution)/shard_map/all_gather | solution.py:310
  97.0 5.9 %fusion.3 = f32[520,3072]{1,0:T(8,128)S(1)} fusion(bf16[520,1024]{1,0:T(8,128)(2,1)S(1)} %multiply_convert_fusion, bf16[1024,4224]{1,0:T(8,128)(2,1)} %all-gather.2.cloned.1.call-done), kind=kOutput, calls=%fused_computation.5 | convolution fusion | flops 3271557120 | bytes 13746176 | tf_op jit(solution)/shard_map/dot_general | solution.py:325
  116.6 23.1 %near_feed.1 = (bf16[1024,1152]{1,0:T(8,128)(2,1)}, bf16[1024,1152]{1,0:T(8,128)(2,1)}, bf16[1024,1152]{1,0:T(8,128)(2,1)}, f32[1024,1152]{1,0:T(8,128)}, f32[1024,1152]{1,0:T(8,128)}, /*index=5*/f32[1152,1024]{1,0:T(8,128)}) custom-call(bf16[512,1024]{1,0:T(8,128)(2,1)} %multiply_convert_fusion.2.xa_ref, bf16[512,1024]{1,0:T(8,128)(2,1)} %collective-permute-done.2.xb_ref, ...), custom_call_target="tpu_custom_call" | custom-call | flops 14495514624 | bytes 32505856 | tf_op jit(solution)/shard_map/near_feed/pallas_call | solution.py:107
  139.8 4.9 convolution_convert_fusion.2
  155.3 7.0 %far_feed.9 = (bf16[1024,128]{1,0:T(8,128)(2,1)}, bf16[1024,128]{1,0:T(8,128)(2,1)}, bf16[1024,128]{1,0:T(8,128)(2,1)}, bf16[4,384,128]{2,1,0:T(8,128)(2,1)}, bf16[4,384,128]{2,1,0:T(8,128)(2,1)}) custom-call(s32[1]{0:T(128)} %bitcast.9.place_ref, bf16[512,1024]{1,0:T(8,128)(2,1)} %collective-permute-done.5.xa_ref, bf16[512,1024]{1,0:T(8,128)(2,1)} %copy-done.9, ...), custom_call_target="tpu_custom_call" | custom-call | flops 1610612736 | bytes 8126464 | tf_op jit(solution)/shard_map/far_feed/pallas_call | solution.py:160
  163.8 8.5 %far_feed.8 = (bf16[1024,256]{1,0:T(8,128)(2,1)}, bf16[1024,256]{1,0:T(8,128)(2,1)}, bf16[1024,256]{1,0:T(8,128)(2,1)}, bf16[4,768,128]{2,1,0:T(8,128)(2,1)}, bf16[4,768,128]{2,1,0:T(8,128)(2,1)}) custom-call(s32[1]{0:T(128)} %bitcast.9.place_ref, bf16[512,1024]{1,0:T(8,128)(2,1)} %collective-permute-done.5.xa_ref, bf16[512,1024]{1,0:T(8,128)(2,1)} %copy-done.9, ...), custom_call_target="tpu_custom_call" | custom-call | flops 3221225472 | bytes 12058624 | tf_op jit(solution)/shard_map/far_feed/pallas_call | solution.py:160
  172.8 8.5 %far_feed.7 = (bf16[1024,256]{1,0:T(8,128)(2,1)}, bf16[1024,256]{1,0:T(8,128)(2,1)}, bf16[1024,256]{1,0:T(8,128)(2,1)}, bf16[4,768,128]{2,1,0:T(8,128)(2,1)}, bf16[4,768,128]{2,1,0:T(8,128)(2,1)}) custom-call(s32[1]{0:T(128)} %bitcast.9.place_ref, bf16[512,1024]{1,0:T(8,128)(2,1)} %collective-permute-done.5.xa_ref, bf16[512,1024]{1,0:T(8,128)(2,1)} %copy-done.9, ...), custom_call_target="tpu_custom_call" | custom-call | flops 3221225472 | bytes 12058624 | tf_op jit(solution)/shard_map/far_feed/pallas_call | solution.py:160
  182.7 8.9 %far_feed.6 = (bf16[1024,256]{1,0:T(8,128)(2,1)}, bf16[1024,256]{1,0:T(8,128)(2,1)}, bf16[1024,256]{1,0:T(8,128)(2,1)}, bf16[4,768,128]{2,1,0:T(8,128)(2,1)}, bf16[4,768,128]{2,1,0:T(8,128)(2,1)}) custom-call(s32[1]{0:T(128)} %bitcast.9.place_ref, bf16[512,1024]{1,0:T(8,128)(2,1)} %collective-permute-done.5.xa_ref, bf16[512,1024]{1,0:T(8,128)(2,1)} %copy-done.9, ...), custom_call_target="tpu_custom_call" | custom-call | flops 3221225472 | bytes 12058624 | tf_op jit(solution)/shard_map/far_feed/pallas_call | solution.py:160
  192.2 8.5 %far_feed.5 = (bf16[1024,256]{1,0:T(8,128)(2,1)}, bf16[1024,256]{1,0:T(8,128)(2,1)}, bf16[1024,256]{1,0:T(8,128)(2,1)}, bf16[4,768,128]{2,1,0:T(8,128)(2,1)}, bf16[4,768,128]{2,1,0:T(8,128)(2,1)}) custom-call(s32[1]{0:T(128)} %bitcast.9.place_ref, bf16[512,1024]{1,0:T(8,128)(2,1)} %collective-permute-done.5.xa_ref, bf16[512,1024]{1,0:T(8,128)(2,1)} %copy-done.9, ...), custom_call_target="tpu_custom_call" | custom-call | flops 3221225472 | bytes 12058624 | tf_op jit(solution)/shard_map/far_feed/pallas_call | solution.py:160
  213.1 4.3 collective-permute-done.26
  219.6 3.5 collective-permute-done.27
  233.1 12.7 %collective-permute-done.49 = bf16[4,768,128]{2,1,0:T(8,128)(2,1)S(1)} collective-permute-done((bf16[4,768,128]{2,1,0:T(8,128)(2,1)S(1)}, bf16[4,768,128]{2,1,0:T(8,128)(2,1)S(1)}, u32[]{:S(2)}, u32[]{:S(2)}) %collective-permute-start.49) | collective-permute-done | bytes 786464 | tf_op jit(solution)/shard_map/ppermute | solution.py:25
  250.6 7.3 %collective-permute-done.32 = bf16[2,768,128]{2,1,0:T(8,128)(2,1)S(1)} collective-permute-done((bf16[2,768,128]{2,1,0:T(8,128)(2,1)S(1)}, bf16[2,768,128]{2,1,0:T(8,128)(2,1)S(1)}, u32[]{:S(2)}, u32[]{:S(2)}) %collective-permute-start.32) | collective-permute-done | bytes 393248 | tf_op jit(solution)/shard_map/ppermute | solution.py:25
  259.5 6.8 %collective-permute-done.38 = bf16[2,768,128]{2,1,0:T(8,128)(2,1)S(1)} collective-permute-done((bf16[2,768,128]{2,1,0:T(8,128)(2,1)S(1)}, bf16[2,768,128]{2,1,0:T(8,128)(2,1)S(1)}, u32[]{:S(2)}, u32[]{:S(2)}) %collective-permute-start.38) | collective-permute-done | bytes 393248 | tf_op jit(solution)/shard_map/ppermute | solution.py:25
  267.9 5.9 %collective-permute-done.44 = bf16[2,768,128]{2,1,0:T(8,128)(2,1)S(1)} collective-permute-done((bf16[2,768,128]{2,1,0:T(8,128)(2,1)S(1)}, bf16[2,768,128]{2,1,0:T(8,128)(2,1)S(1)}, u32[]{:S(2)}, u32[]{:S(2)}) %collective-permute-start.44) | collective-permute-done | bytes 393248 | tf_op jit(solution)/shard_map/ppermute | solution.py:25
  275.3 4.3 collective-permute-done.50
  279.7 12.3 %collective-permute-done.33 = bf16[1,768,128]{2,1,0:T(8,128)(2,1)S(1)} collective-permute-done((bf16[1,768,128]{2,1,0:T(8,128)(2,1)S(1)}, bf16[1,768,128]{2,1,0:T(8,128)(2,1)S(1)}, u32[]{:S(2)}, u32[]{:S(2)}) %collective-permute-start.33) | collective-permute-done | bytes 196640 | tf_op jit(solution)/shard_map/ppermute | solution.py:25
  292.1 10.7 %collective-permute-done.39 = bf16[1,768,128]{2,1,0:T(8,128)(2,1)S(1)} collective-permute-done((bf16[1,768,128]{2,1,0:T(8,128)(2,1)S(1)}, bf16[1,768,128]{2,1,0:T(8,128)(2,1)S(1)}, u32[]{:S(2)}, u32[]{:S(2)}) %collective-permute-start.39) | collective-permute-done | bytes 196640 | tf_op jit(solution)/shard_map/ppermute | solution.py:25
  302.9 16.7 %collective-permute-done.45 = bf16[1,768,128]{2,1,0:T(8,128)(2,1)S(1)} collective-permute-done((bf16[1,768,128]{2,1,0:T(8,128)(2,1)S(1)}, bf16[1,768,128]{2,1,0:T(8,128)(2,1)S(1)}, u32[]{:S(2)}, u32[]{:S(2)}) %collective-permute-start.45) | collective-permute-done | bytes 196640 | tf_op jit(solution)/shard_map/ppermute | solution.py:25
  329.7 4.4 multiply_reduce_fusion.3
  339.7 4.1 convolution_convert_fusion
  361.1 12.7 %collective-permute-done.46.two_ref = bf16[1,768,128]{2,1,0:T(8,128)(2,1)S(1)} collective-permute-done((bf16[1,768,128]{2,1,0:T(8,128)(2,1)S(1)}, bf16[1,768,128]{2,1,0:T(8,128)(2,1)S(1)}, u32[]{:S(2)}, u32[]{:S(2)}) %collective-permute-start.46) | collective-permute-done | bytes 196640 | tf_op jit(solution)/shard_map/ppermute | solution.py:25
  373.9 4.1 collective-permute-done.52.two_ref
  382.8 6.3 %collective-permute-done.41.four_ref = bf16[2,768,128]{2,1,0:T(8,128)(2,1)S(1)} collective-permute-done((bf16[2,768,128]{2,1,0:T(8,128)(2,1)S(1)}, bf16[2,768,128]{2,1,0:T(8,128)(2,1)S(1)}, u32[]{:S(2)}, u32[]{:S(2)}) %collective-permute-start.41) | collective-permute-done | bytes 393248 | tf_op jit(solution)/shard_map/ppermute | solution.py:25
  390.6 6.9 %collective-permute-done.47.four_ref = bf16[2,768,128]{2,1,0:T(8,128)(2,1)S(1)} collective-permute-done((bf16[2,768,128]{2,1,0:T(8,128)(2,1)S(1)}, bf16[2,768,128]{2,1,0:T(8,128)(2,1)S(1)}, u32[]{:S(2)}, u32[]{:S(2)}) %collective-permute-start.47) | collective-permute-done | bytes 393248 | tf_op jit(solution)/shard_map/ppermute | solution.py:25
  398.1 6.4 %collective-permute-done.53.four_ref = bf16[2,768,128]{2,1,0:T(8,128)(2,1)S(1)} collective-permute-done((bf16[2,768,128]{2,1,0:T(8,128)(2,1)S(1)}, bf16[2,768,128]{2,1,0:T(8,128)(2,1)S(1)}, u32[]{:S(2)}, u32[]{:S(2)}) %collective-permute-start.53) | collective-permute-done | bytes 393248 | tf_op jit(solution)/shard_map/ppermute | solution.py:25
  411.3 6.4 %multiply_reduce_fusion.5 = (f32[512]{0:T(512)S(1)}, f32[512,1024]{1,0:T(8,128)S(1)}) fusion(bf16[1,512,1024]{2,1,0:T(8,128)(2,1)S(1)} %copy-done.21, f32[1024]{0:T(1024)S(1)} %copy-done.77, f32[512]{0:T(512)S(1)} %copy-done.78, bf16[1024,4224]{1,0:T(8,128)(2,1)} %all-gather.2.cloned.1.call-done, bf16[512,1024]{1,0:T(8,128)(2,1)S(1)} %copy-done.48, ...), kind=kOutput, calls=%fused_computation.33 | convolution fusion | flops 3233283584 | bytes 12591104 | tf_op jit(solution)/shard_map/dot_general | solution.py:45
  417.7 4.4 collective-permute-done.21
  424.4 29.3 %collective-permute-done.16 = bf16[8,32,3072]{2,1,0:T(8,128)(2,1)S(1)} collective-permute-done((bf16[8,32,3072]{2,1,0:T(8,128)(2,1)S(1)}, bf16[8,32,3072]{2,1,0:T(8,128)(2,1)S(1)}, u32[]{:S(2)}, u32[]{:S(2)}) %collective-permute-start.16) | collective-permute-done | bytes 1572896 | tf_op jit(solution)/shard_map/ppermute | solution.py:25
  457.3 16.9 %collective-permute-done.54.eight_ref = bf16[4,768,128]{2,1,0:T(8,128)(2,1)S(1)} collective-permute-done((bf16[4,768,128]{2,1,0:T(8,128)(2,1)S(1)}, bf16[4,768,128]{2,1,0:T(8,128)(2,1)S(1)}, u32[]{:S(2)}, u32[]{:S(2)}) %collective-permute-start.54) | collective-permute-done | bytes 786464 | tf_op jit(solution)/shard_map/ppermute | solution.py:25
  496.2 4.4 collective-permute-done.23
  501.2 4.0 collective-permute-done.18
  (392 shorter events, 164.6 us)
Async XLA Ops:
  7.2 87.1 %all-gather.2.cloned.1.call-start = ((), (), s32[]{:S(2)}) async-start(), calls=%async_computation | async-start | bytes 8921088 | tf_op jit(solution)/shard_map/all_gather | solution.py:310
  9.8 104.8 %collective-permute-start.7 = (bf16[512,1024]{1,0:T(8,128)(2,1)}, bf16[512,1024]{1,0:T(8,128)(2,1)S(1)}, u32[]{:S(2)}, u32[]{:S(2)}) collective-permute-start(bf16[512,1024]{1,0:T(8,128)(2,1)} %bitcast.126), channel_id=1, source_target_pairs={{0,2},{1,3},{2,0},{3,1},{4,6},{5,7},{6,4},{7,5},{8,10},{9,11},{10,... | collective-permute-start | bytes 3145736 | tf_op jit(solution)/shard_map/ppermute | solution.py:25
  12.8 103.5 %collective-permute-start.3 = (bf16[512,1024]{1,0:T(8,128)(2,1)}, bf16[512,1024]{1,0:T(8,128)(2,1)}, u32[]{:S(2)}, u32[]{:S(2)}) collective-permute-start(bf16[512,1024]{1,0:T(8,128)(2,1)} %bitcast.127), channel_id=1, source_target_pairs={{0,1},{1,0},{2,3},{3,2},{4,5},{5,4},{6,7},{7,6},{8,9},{9,8},{10,11... | collective-permute-start | bytes 3145736 | tf_op jit(solution)/shard_map/ppermute | solution.py:25
  114.6 39.3 %collective-permute-start.8 = (bf16[512,1024]{1,0:T(8,128)(2,1)S(1)}, bf16[512,1024]{1,0:T(8,128)(2,1)}, u32[]{:S(2)}, u32[]{:S(2)}) collective-permute-start(bf16[512,1024]{1,0:T(8,128)(2,1)S(1)} %collective-permute-done.7.ga_ref), channel_id=1, source_target_pairs={{0,1},{1,0},{2,3},{3,2},{4,5},{5,4},{6,7},{7,6},{8,9},{9,8},{10,11... | collective-permute-start | bytes 3145736 | tf_op jit(solution)/shard_map/ppermute | solution.py:25
  114.8 31.3 %collective-permute-start.5 = (bf16[512,1024]{1,0:T(8,128)(2,1)}, bf16[512,1024]{1,0:T(8,128)(2,1)}, u32[]{:S(2)}, u32[]{:S(2)}) collective-permute-start(bf16[512,1024]{1,0:T(8,128)(2,1)} %multiply_convert_fusion.2.xa_ref), channel_id=1, source_target_pairs={{0,2},{1,3},{2,0},{3,1},{4,6},{5,7},{6,4},{7,5},{8,10},{9,11},{10,... | collective-permute-start | bytes 3145736 | tf_op jit(solution)/shard_map/ppermute | solution.py:25
  145.9 177.8 %collective-permute-start.4 = (bf16[512,1024]{1,0:T(8,128)(2,1)}, bf16[512,1024]{1,0:T(8,128)(2,1)}, u32[]{:S(2)}, u32[]{:S(2)}) collective-permute-start(bf16[512,1024]{1,0:T(8,128)(2,1)} %slice.332), channel_id=1, source_target_pairs={{0,1},{1,0},{2,3},{3,2},{4,5},{5,4},{6,7},{7,6},{8,9},{9,8},{10,11... | collective-permute-start | bytes 3145736 | tf_op jit(solution)/shard_map/ppermute | solution.py:25
  162.3 49.0 %collective-permute-start.25 = (bf16[4,384,128]{2,1,0:T(8,128)(2,1)}, bf16[4,384,128]{2,1,0:T(8,128)(2,1)S(1)}, u32[]{:S(2)}, u32[]{:S(2)}) collective-permute-start(bf16[4,384,128]{2,1,0:T(8,128)(2,1)} %get-tuple-element.78), channel_id=1, source_target_pairs={{0,4},{4,0},{8,12},{12,8},{16,20},{20,16},{24,28},{28,24},{1,5},{5... | collective-permute-start | bytes 1179656 | tf_op jit(solution)/shard_map/ppermute | solution.py:25
  172.2 59.5 %collective-permute-start.31 = (bf16[4,768,128]{2,1,0:T(8,128)(2,1)}, bf16[4,768,128]{2,1,0:T(8,128)(2,1)S(1)}, u32[]{:S(2)}, u32[]{:S(2)}) collective-permute-start(bf16[4,768,128]{2,1,0:T(8,128)(2,1)} %get-tuple-element.80), channel_id=1, source_target_pairs={{0,4},{4,0},{8,12},{12,8},{16,20},{20,16},{24,28},{28,24},{1,5},{5... | collective-permute-start | bytes 2359304 | tf_op jit(solution)/shard_map/ppermute | solution.py:25
  181.3 50.7 %collective-permute-start.37 = (bf16[4,768,128]{2,1,0:T(8,128)(2,1)}, bf16[4,768,128]{2,1,0:T(8,128)(2,1)S(1)}, u32[]{:S(2)}, u32[]{:S(2)}) collective-permute-start(bf16[4,768,128]{2,1,0:T(8,128)(2,1)} %get-tuple-element.82), channel_id=1, source_target_pairs={{0,4},{4,0},{8,12},{12,8},{16,20},{20,16},{24,28},{28,24},{1,5},{5... | collective-permute-start | bytes 2359304 | tf_op jit(solution)/shard_map/ppermute | solution.py:25
  191.6 41.2 %collective-permute-start.43 = (bf16[4,768,128]{2,1,0:T(8,128)(2,1)}, bf16[4,768,128]{2,1,0:T(8,128)(2,1)S(1)}, u32[]{:S(2)}, u32[]{:S(2)}) collective-permute-start(bf16[4,768,128]{2,1,0:T(8,128)(2,1)} %get-tuple-element.84), channel_id=1, source_target_pairs={{0,4},{4,0},{8,12},{12,8},{16,20},{20,16},{24,28},{28,24},{1,5},{5... | collective-permute-start | bytes 2359304 | tf_op jit(solution)/shard_map/ppermute | solution.py:25
  232.8 86.9 %collective-permute-start.11 = (bf16[512,1024]{1,0:T(8,128)(2,1)}, bf16[512,1024]{1,0:T(8,128)(2,1)S(1)}, u32[]{:S(2)}, u32[]{:S(2)}) collective-permute-start(bf16[512,1024]{1,0:T(8,128)(2,1)} %slice.336), channel_id=1, source_target_pairs={{0,1},{1,0},{2,3},{3,2},{4,5},{5,4},{6,7},{7,6},{8,9},{9,8},{10,11... | collective-permute-start | bytes 3145736 | tf_op jit(solution)/shard_map/ppermute | solution.py:25
  248.6 25.2 %collective-permute-start.44 = (bf16[2,768,128]{2,1,0:T(8,128)(2,1)S(1)}, bf16[2,768,128]{2,1,0:T(8,128)(2,1)S(1)}, u32[]{:S(2)}, u32[]{:S(2)}) collective-permute-start(bf16[2,768,128]{2,1,0:T(8,128)(2,1)S(1)} %get-tuple-element.168), channel_id=1, source_target_pairs={{0,8},{4,12},{8,0},{12,4},{16,24},{20,28},{24,16},{28,20},{1,9},{5... | collective-permute-start | bytes 1179656 | tf_op jit(solution)/shard_map/ppermute | solution.py:25
  257.9 21.7 %collective-permute-start.50 = (bf16[2,768,128]{2,1,0:T(8,128)(2,1)S(1)}, bf16[2,768,128]{2,1,0:T(8,128)(2,1)S(1)}, u32[]{:S(2)}, u32[]{:S(2)}) collective-permute-start(bf16[2,768,128]{2,1,0:T(8,128)(2,1)S(1)} %get-tuple-element.166), channel_id=1, source_target_pairs={{0,8},{4,12},{8,0},{12,4},{16,24},{20,28},{24,16},{28,20},{1,9},{5... | collective-permute-start | bytes 1179656 | tf_op jit(solution)/shard_map/ppermute | solution.py:25
  266.3 59.9 %collective-permute-start.10 = (bf16[512,1024]{1,0:T(8,128)(2,1)S(1)}, bf16[512,1024]{1,0:T(8,128)(2,1)S(1)}, u32[]{:S(2)}, u32[]{:S(2)}) collective-permute-start(bf16[512,1024]{1,0:T(8,128)(2,1)S(1)} %add_convert_fusion.4), channel_id=1, source_target_pairs={{0,2},{1,3},{2,0},{3,1},{4,6},{5,7},{6,4},{7,5},{8,10},{9,11},{10,... | collective-permute-start | bytes 3145736 | tf_op jit(solution)/shard_map/ppermute | solution.py:25
  273.8 48.4 %collective-permute-start.13 = (bf16[512,1024]{1,0:T(8,128)(2,1)S(1)}, bf16[512,1024]{1,0:T(8,128)(2,1)S(1)}, u32[]{:S(2)}, u32[]{:S(2)}) collective-permute-start(bf16[512,1024]{1,0:T(8,128)(2,1)S(1)} %add_convert_fusion.2), channel_id=1, source_target_pairs={{0,2},{1,3},{2,0},{3,1},{4,6},{5,7},{6,4},{7,5},{8,10},{9,11},{10,... | collective-permute-start | bytes 3145736 | tf_op jit(solution)/shard_map/ppermute | solution.py:25
  319.5 39.0 %collective-permute-start.29 = (bf16[2,384,128]{2,1,0:T(8,128)(2,1)}, bf16[2,384,128]{2,1,0:T(8,128)(2,1)}, u32[]{:S(2)}, u32[]{:S(2)}) collective-permute-start(bf16[2,384,128]{2,1,0:T(8,128)(2,1)} %pad_maximum_fusion.14), channel_id=1, source_target_pairs={{0,8},{4,12},{8,0},{12,4},{16,24},{20,28},{24,16},{28,20},{1,9},{5... | collective-permute-start | bytes 589832 | tf_op jit(solution)/shard_map/ppermute | solution.py:25
  319.7 35.7 %collective-permute-start.51 = (bf16[1,768,128]{2,1,0:T(8,128)(2,1)S(1)}, bf16[1,768,128]{2,1,0:T(8,128)(2,1)}, u32[]{:S(2)}, u32[]{:S(2)}) collective-permute-start(bf16[1,768,128]{2,1,0:T(8,128)(2,1)S(1)} %add_convert_fusion.14), channel_id=1, source_target_pairs={{0,16},{4,20},{8,24},{12,28},{16,0},{20,4},{24,8},{28,12},{1,17},{... | collective-permute-start | bytes 589832 | tf_op jit(solution)/shard_map/ppermute | solution.py:25
  322.2 35.2 %collective-permute-start.34 = (bf16[1,768,128]{2,1,0:T(8,128)(2,1)S(1)}, bf16[1,768,128]{2,1,0:T(8,128)(2,1)S(1)}, u32[]{:S(2)}, u32[]{:S(2)}) collective-permute-start(bf16[1,768,128]{2,1,0:T(8,128)(2,1)S(1)} %add_convert_fusion.22.own_ref), channel_id=1, source_target_pairs={{0,16},{4,20},{8,24},{12,28},{16,0},{20,4},{24,8},{28,12},{1,17},{... | collective-permute-start | bytes 589832 | tf_op jit(solution)/shard_map/ppermute | solution.py:25
  323.6 36.9 %collective-permute-start.40 = (bf16[1,768,128]{2,1,0:T(8,128)(2,1)S(1)}, bf16[1,768,128]{2,1,0:T(8,128)(2,1)S(1)}, u32[]{:S(2)}, u32[]{:S(2)}) collective-permute-start(bf16[1,768,128]{2,1,0:T(8,128)(2,1)S(1)} %add_convert_fusion.19.own_ref), channel_id=1, source_target_pairs={{0,16},{4,20},{8,24},{12,28},{16,0},{20,4},{24,8},{28,12},{1,17},{... | collective-permute-start | bytes 589832 | tf_op jit(solution)/shard_map/ppermute | solution.py:25
  347.3 58.9 %collective-permute-start.15 = (bf16[16,32,3072]{2,1,0:T(8,128)(2,1)}, bf16[16,32,3072]{2,1,0:T(8,128)(2,1)}, u32[]{:S(2)}, u32[]{:S(2)}) collective-permute-start(bf16[16,32,3072]{2,1,0:T(8,128)(2,1)} %dynamic-slice_bitcast_fusion), channel_id=1, source_target_pairs={{0,1},{1,0},{2,3},{3,2},{4,5},{5,4},{6,7},{7,6},{8,9},{9,8},{10,11... | collective-permute-start | bytes 9437192 | tf_op jit(solution)/shard_map/ppermute | solution.py:25
  355.4 49.9 %collective-permute-start.20 = (bf16[16,32,1152]{2,1,0:T(8,128)(2,1)S(1)}, bf16[16,32,1152]{2,1,0:T(8,128)(2,1)S(1)}, u32[]{:S(2)}, u32[]{:S(2)}) collective-permute-start(bf16[16,32,1152]{2,1,0:T(8,128)(2,1)S(1)} %dynamic-slice_bitcast_fusion.2), channel_id=1, source_target_pairs={{0,1},{1,0},{2,3},{3,2},{4,5},{5,4},{6,7},{7,6},{8,9},{9,8},{10,11... | collective-permute-start | bytes 3538952 | tf_op jit(solution)/shard_map/ppermute | solution.py:25
  358.5 19.4 %collective-permute-start.52 = (bf16[1,768,128]{2,1,0:T(8,128)(2,1)S(1)}, bf16[1,768,128]{2,1,0:T(8,128)(2,1)S(1)}, u32[]{:S(2)}, u32[]{:S(2)}) collective-permute-start(bf16[1,768,128]{2,1,0:T(8,128)(2,1)S(1)} %add_convert_fusion.13.own_ref), channel_id=1, source_target_pairs={{0,16},{4,20},{8,24},{12,28},{16,0},{20,4},{24,8},{28,12},{1,17},{... | collective-permute-start | bytes 589832 | tf_op jit(solution)/shard_map/ppermute | solution.py:25
  360.5 20.1 %collective-permute-start.35 = (bf16[2,768,128]{2,1,0:T(8,128)(2,1)S(1)}, bf16[2,768,128]{2,1,0:T(8,128)(2,1)S(1)}, u32[]{:S(2)}, u32[]{:S(2)}) collective-permute-start(bf16[2,768,128]{2,1,0:T(8,128)(2,1)S(1)} %pad_maximum_fusion.10), channel_id=1, source_target_pairs={{0,8},{4,12},{8,0},{12,4},{16,24},{20,28},{24,16},{28,20},{1,9},{5... | collective-permute-start | bytes 1179656 | tf_op jit(solution)/shard_map/ppermute | solution.py:25
  377.9 19.5 %collective-permute-start.47 = (bf16[2,768,128]{2,1,0:T(8,128)(2,1)S(1)}, bf16[2,768,128]{2,1,0:T(8,128)(2,1)S(1)}, u32[]{:S(2)}, u32[]{:S(2)}) collective-permute-start(bf16[2,768,128]{2,1,0:T(8,128)(2,1)S(1)} %pad_maximum_fusion.12), channel_id=1, source_target_pairs={{0,8},{4,12},{8,0},{12,4},{16,24},{20,28},{24,16},{28,20},{1,9},{5... | collective-permute-start | bytes 1179656 | tf_op jit(solution)/shard_map/ppermute | solution.py:25
  380.6 24.0 %collective-permute-start.53 = (bf16[2,768,128]{2,1,0:T(8,128)(2,1)S(1)}, bf16[2,768,128]{2,1,0:T(8,128)(2,1)S(1)}, u32[]{:S(2)}, u32[]{:S(2)}) collective-permute-start(bf16[2,768,128]{2,1,0:T(8,128)(2,1)S(1)} %pad_maximum_fusion.13), channel_id=1, source_target_pairs={{0,8},{4,12},{8,0},{12,4},{16,24},{20,28},{24,16},{28,20},{1,9},{5... | collective-permute-start | bytes 1179656 | tf_op jit(solution)/shard_map/ppermute | solution.py:25
  389.0 102.2 %collective-permute-start.30 = (bf16[4,384,128]{2,1,0:T(8,128)(2,1)}, bf16[4,384,128]{2,1,0:T(8,128)(2,1)}, u32[]{:S(2)}, u32[]{:S(2)}) collective-permute-start(bf16[4,384,128]{2,1,0:T(8,128)(2,1)} %pad_maximum_fusion.9), channel_id=1, source_target_pairs={{0,4},{4,0},{8,12},{12,8},{16,20},{20,16},{24,28},{28,24},{1,5},{5... | collective-permute-start | bytes 1179656 | tf_op jit(solution)/shard_map/ppermute | solution.py:25
  397.5 90.5 %collective-permute-start.36 = (bf16[4,768,128]{2,1,0:T(8,128)(2,1)}, bf16[4,768,128]{2,1,0:T(8,128)(2,1)}, u32[]{:S(2)}, u32[]{:S(2)}) collective-permute-start(bf16[4,768,128]{2,1,0:T(8,128)(2,1)} %pad_maximum_fusion.5), channel_id=1, source_target_pairs={{0,4},{4,0},{8,12},{12,8},{16,20},{20,16},{24,28},{28,24},{1,5},{5... | collective-permute-start | bytes 2359304 | tf_op jit(solution)/shard_map/ppermute | solution.py:25
  404.6 80.0 %collective-permute-start.42 = (bf16[4,768,128]{2,1,0:T(8,128)(2,1)}, bf16[4,768,128]{2,1,0:T(8,128)(2,1)}, u32[]{:S(2)}, u32[]{:S(2)}) collective-permute-start(bf16[4,768,128]{2,1,0:T(8,128)(2,1)} %pad_maximum_fusion.6), channel_id=1, source_target_pairs={{0,4},{4,0},{8,12},{12,8},{16,20},{20,16},{24,28},{28,24},{1,5},{5... | collective-permute-start | bytes 2359304 | tf_op jit(solution)/shard_map/ppermute | solution.py:25
  409.6 44.1 %collective-permute-start.16 = (bf16[8,32,3072]{2,1,0:T(8,128)(2,1)S(1)}, bf16[8,32,3072]{2,1,0:T(8,128)(2,1)S(1)}, u32[]{:S(2)}, u32[]{:S(2)}) collective-permute-start(bf16[8,32,3072]{2,1,0:T(8,128)(2,1)S(1)} %dynamic-slice_bitcast_fusion.1), channel_id=1, source_target_pairs={{0,2},{1,3},{2,0},{3,1},{4,6},{5,7},{6,4},{7,5},{8,10},{9,11},{10,... | collective-permute-start | bytes 4718600 | tf_op jit(solution)/shard_map/ppermute | solution.py:25
  422.1 34.3 %collective-permute-start.48 = (bf16[4,768,128]{2,1,0:T(8,128)(2,1)S(1)}, bf16[4,768,128]{2,1,0:T(8,128)(2,1)S(1)}, u32[]{:S(2)}, u32[]{:S(2)}) collective-permute-start(bf16[4,768,128]{2,1,0:T(8,128)(2,1)S(1)} %pad_maximum_fusion.7), channel_id=1, source_target_pairs={{0,4},{4,0},{8,12},{12,8},{16,20},{20,16},{24,28},{28,24},{1,5},{5... | collective-permute-start | bytes 2359304 | tf_op jit(solution)/shard_map/ppermute | solution.py:25
  453.7 20.5 %collective-permute-start.54 = (bf16[4,768,128]{2,1,0:T(8,128)(2,1)S(1)}, bf16[4,768,128]{2,1,0:T(8,128)(2,1)S(1)}, u32[]{:S(2)}, u32[]{:S(2)}) collective-permute-start(bf16[4,768,128]{2,1,0:T(8,128)(2,1)S(1)} %pad_maximum_fusion.8), channel_id=1, source_target_pairs={{0,4},{4,0},{8,12},{12,8},{16,20},{20,16},{24,28},{28,24},{1,5},{5... | collective-permute-start | bytes 2359304 | tf_op jit(solution)/shard_map/ppermute | solution.py:25
  456.3 37.3 %collective-permute-start.22 = (bf16[4,32,1152]{2,1,0:T(8,128)(2,1)}, bf16[4,32,1152]{2,1,0:T(8,128)(2,1)S(1)}, u32[]{:S(2)}, u32[]{:S(2)}) collective-permute-start(bf16[4,32,1152]{2,1,0:T(8,128)(2,1)} %dynamic-slice_bitcast_fusion.6), channel_id=1, source_target_pairs={{0,4},{4,0},{8,12},{12,8},{16,20},{20,16},{24,28},{28,24},{1,5},{5... | collective-permute-start | bytes 884744 | tf_op jit(solution)/shard_map/ppermute | solution.py:25
  (114 other events, 1444.8 us)
Sparse Core Ops, SparseCore 0:
  11.5 82.7 all-gather.1

commit v3 on v2

--- a/solution.py
+++ b/solution.py
@@ -1,3 +1,5 @@
+import functools
+
 import jax
 import jax.numpy as jnp
 from jax import lax
@@ -11,7 +13,6 @@
 F32 = jnp.float32
 HALVINGS = 3
 PARTS = 1 << HALVINGS
-ORDER = [int(format(q, "03b")[::-1], 2) for q in range(PARTS)]
 NN = (((1,), (0,)), ((), ()))
 NT = (((1,), (1,)), ((), ()))
 TN = (((0,), (0,)), ((), ()))
@@ -41,6 +42,15 @@
     return size.bit_length() - 1
 
 
+def after(values, *before):
+    return lax.optimization_barrier((values, before))[0]
+
+
+def away(bits):
+    top = len(bits) - 1
+    return [sum(((q >> (top - n)) & 1) << bit for n, bit in enumerate(bits)) for q in range(PARTS)]
+
+
 def dot(left, right, dims):
     return lax.dot_general(left, right, dims, preferred_element_type=F32)
 
@@ -53,11 +63,14 @@
     return dot(left, right, NT)
 
 
-def hidden_blocks(hidden):
-    wide = [(256, n) for n in range(hidden // 256)]
-    rest = hidden % 256
-    assert rest in (0, 128)
-    return wide + ([(128, hidden // 128 - 1)] if rest else [])
+def activate(gate_val, up_val, hidden_grad):
+    sig = 1.0 / (1.0 + jnp.exp(-gate_val))
+    silu = gate_val * sig
+    return (
+        (silu * up_val).astype(BF16),
+        (hidden_grad * up_val * (sig * (1.0 + gate_val * (1.0 - sig)))).astype(BF16),
+        (hidden_grad * silu).astype(BF16),
+    )
 
 
 def feed(x_ref, go_ref, gate_ref, up_ref, down_ref, hid_ref, gl_ref, ul_ref):
@@ -68,11 +81,7 @@
         gate_val = dot(x_ref[part], gate_ref[...], NN)
         up_val = dot(x_ref[part], up_ref[...], NN)
         hidden_grad = dot(go_ref[part], down_ref[...], NT)
-        sig = 1.0 / (1.0 + jnp.exp(-gate_val))
-        silu = gate_val * sig
-        hid_ref[part] = (silu * up_val).astype(BF16)
-        gl_ref[part] = (hidden_grad * up_val * (sig * (1.0 + gate_val * (1.0 - sig)))).astype(BF16)
-        ul_ref[part] = (hidden_grad * silu).astype(BF16)
+        hid_ref[part], gl_ref[part], ul_ref[part] = activate(gate_val, up_val, hidden_grad)
 
 
 def join(first, xa_ref, xb_ref, ga_ref, gb_ref, x_ref, go_ref):
@@ -90,9 +99,9 @@
                 hid_ref, gl_ref, ul_ref, og_ref, ou_ref, od_ref, x_ref, go_ref):
     join(pl.program_id(0) == 0, xa_ref, xb_ref, ga_ref, gb_ref, x_ref, go_ref)
     feed(x_ref, go_ref, gate_ref, up_ref, down_ref, hid_ref, gl_ref, ul_ref)
-    og_ref[...] = dot(x_ref[...], gl_ref[...], TN)
-    ou_ref[...] = dot(x_ref[...], ul_ref[...], TN)
-    od_ref[...] = dot(hid_ref[...], go_ref[...], TN)
+    og_ref[...] = dot(x_ref[...], gl_ref[...], TN).astype(BF16)
+    ou_ref[...] = dot(x_ref[...], ul_ref[...], TN).astype(BF16)
+    od_ref[...] = dot(hid_ref[...], go_ref[...], TN).astype(BF16)
 
 
 def near_feed(xs, gos, gate, up, down):
@@ -110,99 +119,113 @@
         in_specs=[whole] * 4 + [col, col, row],
         out_specs=[act] * 3 + [col, col, row],
         out_shape=[jax.ShapeDtypeStruct((tokens, hidden), BF16)] * 3
-        + [jax.ShapeDtypeStruct((features, hidden), F32)] * 2
-        + [jax.ShapeDtypeStruct((hidden, features), F32)],
+        + [jax.ShapeDtypeStruct((features, hidden), BF16)] * 2
+        + [jax.ShapeDtypeStruct((hidden, features), BF16)],
         scratch_shapes=[pltpu.VMEM((tokens, features), BF16)] * 2,
         compiler_params=pltpu.CompilerParams(vmem_limit_bytes=VMEM_LIMIT),
         cost_estimate=pl.CostEstimate(
             flops=12 * tokens * features * hidden,
-            transcendentals=tokens * hidden,
-            bytes_accessed=18 * features * hidden + 6 * tokens * hidden + 4 * tokens * features,
+            transcendentals=0,
+            bytes_accessed=14 * features * hidden,
         ),
         name="near_feed",
     )(*xs, *gos, gate, up, down)
 
 
-def far_kernel(place_ref, xa_ref, xb_ref, ga_ref, gb_ref, gate_ref, up_ref, down_ref,
-               ng_ref, nu_ref, nd_ref, hid_ref, gl_ref, ul_ref, kept_ref, sent_ref,
-               x_ref, go_ref, tg_ref, tu_ref, td_ref):
-    join(pl.program_id(0) == 0, xa_ref, xb_ref, ga_ref, gb_ref, x_ref, go_ref)
+def far_kernel(orders, place_ref, xa_ref, xb_ref, ga_ref, gb_ref, gate_ref, up_ref, down_ref,
+               ng_ref, nu_ref, nd_ref, *refs):
+    blocks = len(orders)
+    x_ref, go_ref, tg_ref, tu_ref, td_ref = refs[-5:]
+    packs = refs[-5 - 2 * blocks : -5]
+    hid_ref, gl_ref, ul_ref = refs[-8 - 2 * blocks : -5 - 2 * blocks]
+    now = pl.program_id(0)
+    join(now == 0, xa_ref, xb_ref, ga_ref, gb_ref, x_ref, go_ref)
     feed(x_ref, go_ref, gate_ref, up_ref, down_ref, hid_ref, gl_ref, ul_ref)
-    tg_ref[...] = ng_ref[...] + dot(x_ref[...], gl_ref[...], TN)
-    tu_ref[...] = nu_ref[...] + dot(x_ref[...], ul_ref[...], TN)
-    td_ref[...] = nd_ref[...] + dot(hid_ref[...], go_ref[...], TN)
+    tg_ref[...] = ng_ref[...].astype(F32) + dot(x_ref[...], gl_ref[...], TN)
+    tu_ref[...] = nu_ref[...].astype(F32) + dot(x_ref[...], ul_ref[...], TN)
+    td_ref[...] = nd_ref[...].astype(F32) + dot(hid_ref[...], go_ref[...], TN)
     features, wide = tg_ref.shape
     tall, low = features // PARTS, wide // PARTS
-    for q in range(PARTS):
-        part = place_ref[0] ^ ORDER[q]
-        out = kept_ref.at[q] if q < PARTS // 2 else sent_ref.at[q - PARTS // 2]
-        rows = pl.ds(pl.multiple_of(part * tall, tall), tall)
-        at = 0
-        for grad_ref in (tg_ref, tu_ref):
-            for c in range(0, wide, LANES):
-                out[at : at + tall] = grad_ref[rows, c : c + LANES].astype(BF16)
-                at += tall
-        rows = pl.ds(pl.multiple_of(part * low, low), low)
-        for c in range(0, features, LANES):
-            out[at : at + low] = td_ref[rows, c : c + LANES].astype(BF16)
-            at += low
-
-
-def far_feed(place, xs, gos, gate, up, down, near_grads, wide, index):
+    for n, bits in enumerate(orders):
+
+        @pl.when(now == n)
+        def _(n=n, bits=bits):
+            for q, far in enumerate(away(bits or (0, 1, 2))):
+                part = place_ref[0] ^ far if bits else far
+                half = PARTS // 2
+                out = packs[2 * n + q // half].at[q % half]
+                rows = pl.ds(part * tall, tall)
+                at = 0
+                for grad_ref in (tg_ref, tu_ref):
+                    for c in range(0, wide, LANES):
+                        out[at : at + tall] = grad_ref[rows, c : c + LANES].astype(BF16)
+                        at += tall
+                rows = pl.ds(part * low, low)
+                for c in range(0, features, LANES):
+                    out[at : at + low] = td_ref[rows, c : c + LANES].astype(BF16)
+                    at += low
+
+
+def far_feed(place, xs, gos, gate, up, down, near_grads, before, orders, wide, index):
     rows, features = xs[0].shape
     tokens = 2 * rows
+    hidden = gate.shape[1]
+    blocks = len(orders)
     whole = pl.BlockSpec((rows, features), lambda i, _: (0, 0), pipeline_mode=pl.Buffered(1))
-    col = pl.BlockSpec((features, wide), lambda i, _: (0, index))
-    row = pl.BlockSpec((wide, features), lambda i, _: (index, 0))
-    act = pl.BlockSpec((tokens, wide), lambda i, _: (0, 0))
+    col = pl.BlockSpec((features, wide), lambda i, _: (0, index + i))
+    row = pl.BlockSpec((wide, features), lambda i, _: (index + i, 0))
+    act = pl.BlockSpec((tokens, wide), lambda i, _: (0, index + i))
     packed = 3 * features * wide // PARTS // LANES
-    half = pl.BlockSpec((PARTS // 2, packed, LANES), lambda i, _: (0, 0, 0))
-    return pl.pallas_call(
-        far_kernel,
+    half = pl.BlockSpec((PARTS // 2, packed, LANES), lambda i, _: (0, 0, 0), pipeline_mode=pl.Buffered(1))
+    first = 1 + 4 + 3 + 3
+    results = pl.pallas_call(
+        functools.partial(far_kernel, orders),
         grid_spec=pltpu.PrefetchScalarGridSpec(
             num_scalar_prefetch=1,
-            grid=(1,),
-            in_specs=[whole] * 4 + [col, col, row] + [col, col, row],
-            out_specs=[act] * 3 + [half] * 2,
+            grid=(blocks,),
+            in_specs=[whole] * 4
+            + [col, col, row] * 2
+            + [pl.BlockSpec(memory_space=pl.ANY)] * len(before),
+            out_specs=[act] * 3 + [half] * (2 * blocks),
             scratch_shapes=[pltpu.VMEM((tokens, features), BF16)] * 2
             + [pltpu.VMEM((features, wide), F32)] * 2
             + [pltpu.VMEM((wide, features), F32)],
         ),
-        out_shape=[jax.ShapeDtypeStruct((tokens, wide), BF16)] * 3
-        + [jax.ShapeDtypeStruct((PARTS // 2, packed, LANES), BF16)] * 2,
+        out_shape=[jax.ShapeDtypeStruct((tokens, hidden), BF16)] * 3
+        + [jax.ShapeDtypeStruct((PARTS // 2, packed, LANES), BF16)] * (2 * blocks),
+        input_output_aliases={first + n: n for n in range(len(before))},
         compiler_params=pltpu.CompilerParams(vmem_limit_bytes=VMEM_LIMIT),
         cost_estimate=pl.CostEstimate(
-            flops=12 * tokens * features * wide,
-            transcendentals=tokens * wide,
-            bytes_accessed=24 * features * wide + 6 * tokens * wide + 4 * tokens * features,
+            flops=12 * blocks * tokens * features * wide,
+            transcendentals=0,
+            bytes_accessed=18 * blocks * features * wide,
         ),
         name="far_feed",
-    )(place, *xs, *gos, gate, up, down, *near_grads)
-
-
-def unpack_kernel(place_ref, own_ref, two_ref, four_ref, eight_ref, *refs):
+    )(place, *xs, *gos, gate, up, down, *near_grads, *before)
+    acts = results[:3]
+    return acts, list(zip(results[3::2], results[4::2]))
+
+
+def unpack_kernel(bits, pieces, place_ref, *refs):
     og_ref, ou_ref, od_ref = refs[-3:]
     features, wide = og_ref.shape
     tall, low = features // PARTS, wide // PARTS
-    sources = [own_ref.at[0], two_ref.at[0]]
-    sources += [four_ref.at[n] for n in range(2)]
-    sources += [eight_ref.at[n] for n in range(4)]
-    for q in range(PARTS):
-        part = place_ref[0] ^ ORDER[q]
-        source = sources[q]
-        rows = pl.ds(pl.multiple_of(part * tall, tall), tall)
+    sources = [ref.at[n] for ref in refs[:pieces] for n in range(ref.shape[0])]
+    for source, far in zip(sources, away(bits or (0, 1, 2))):
+        part = place_ref[0] ^ far if bits else far
+        rows = pl.ds(part * tall, tall)
         at = 0
         for out in (og_ref, ou_ref):
             for c in range(0, wide, LANES):
                 out[rows, c : c + LANES] = source[at : at + tall].astype(F32)
                 at += tall
-        rows = pl.ds(pl.multiple_of(part * low, low), low)
+        rows = pl.ds(part * low, low)
         for c in range(0, features, LANES):
             od_ref[rows, c : c + LANES] = source[at : at + low].astype(F32)
             at += low
 
 
-def unpack(place, pieces, before, wide, index, features, hidden):
+def unpack(place, pieces, before, bits, wide, index, features, hidden):
     packed = pieces[0].shape[1]
     ins = [
         pl.BlockSpec((piece.shape[0], packed, LANES), lambda i, _: (0, 0, 0)) for piece in pieces
@@ -211,7 +234,7 @@
     row = pl.BlockSpec((wide, features), lambda i, _: (index, 0))
     keep = [pl.BlockSpec(memory_space=pl.ANY)] * len(before)
     return pl.pallas_call(
-        unpack_kernel,
+        functools.partial(unpack_kernel, bits, len(pieces)),
         grid_spec=pltpu.PrefetchScalarGridSpec(
             num_scalar_prefetch=1,
             grid=(1,),
@@ -223,7 +246,7 @@
         input_output_aliases={1 + len(ins) + n: n for n in range(len(before))},
         compiler_params=pltpu.CompilerParams(vmem_limit_bytes=VMEM_LIMIT),
         cost_estimate=pl.CostEstimate(
-            flops=0, transcendentals=0, bytes_accessed=18 * features * wide
+            flops=0, transcendentals=0, bytes_accessed=1000
         ),
         name="unpack",
     )(place, *pieces, *before)
@@ -242,30 +265,35 @@
     return blocks
 
 
-def scatter_mp(near, far):
-    rows = near.shape[0] // 2
-    got_far = swap(far[rows:], "mp", 0)
-    got_near = swap(near[rows:], "mp", 0)
-    got = swap(add_low(far[:rows], got_far), "mp", 1)
-    return near[:rows].astype(F32) + got_near.astype(F32) + got.astype(F32)
-
-
-def sum_dp(kept, sent):
-    for bit in range(HALVINGS):
-        got = swap(sent, "dp", bit)
-        half = kept.shape[0] // 2
-        if half:
-            sent = add_low(kept[half:], got[half:])
-            kept = add_low(kept[:half], got[:half])
+class Sum:
+    def __init__(self, kept, sent, bits):
+        self.kept, self.sent, self.bits, self.step = kept, sent, bits, 0
+
+    def send(self, *before):
+        if before:
+            self.sent = after(self.sent, *before)
+        steps = len(self.bits)
+        bit = self.bits[self.step] if self.step < steps else self.bits[2 * steps - 1 - self.step]
+        self.got = swap(self.sent, "dp", bit)
+
+    def add(self):
+        self.step += 1
+        got, steps = self.got, len(self.bits)
+        if self.step < steps:
+            half = self.kept.shape[0] // 2
+            self.sent = add_low(self.kept[half:], got[half:])
+            self.kept = add_low(self.kept[:half], got[:half])
+        elif self.step == steps:
+            own = add_low(self.kept, got)
+            for bit in range(HALVINGS, bits_of("dp")):
+                own = add_low(own, swap(own, "dp", bit))
+            self.pieces = [own]
+            self.sent = own
         else:
-            kept = add_low(kept, got)
-    for bit in range(HALVINGS, bits_of("dp")):
-        kept = add_low(kept, swap(kept, "dp", bit))
-    pieces = [kept]
-    for bit in reversed(range(HALVINGS)):
-        held = jnp.concatenate(pieces, 0) if len(pieces) > 1 else pieces[0]
-        pieces = pieces + [swap(held, "dp", bit)]
-    return pieces
+            self.pieces.append(got)
+            if self.step < 2 * steps:
+                self.sent = jnp.concatenate(self.pieces, 0)
+        return self.sent
 
 
 def scatter_all(array):
@@ -314,6 +342,7 @@
     gain_one, gain_two, taps = vectors[0], vectors[1], vectors[2:]
 
     group_grad = gather_mp(cotangent)
+    everything = after(everything, group_grad)
 
     pad = 8
     rim = shift(block_in.reshape(rows, features)[rows - pad :], "mp", 1)
@@ -345,21 +374,27 @@
     inverse_two = lax.rsqrt(jnp.mean(residual * residual, axis=-1, keepdims=True) + epsilon)
     second_low = (residual * inverse_two * gain_two).astype(BF16)
 
-    group = gather_mp(second_low)
     hidden_units = gate_proj.shape[1]
     place = (lax.axis_index("dp") % PARTS).reshape(1).astype(jnp.int32)
+    beside = swap(second_low, "mp", 0)
+    across = swap(second_low, "mp", 1)
     hid_near, gl_near, ul_near, *near_grads = near_feed(
-        group[:2], group_grad[:2], gate_proj, up_proj, down_proj
-    )
-    blocks = hidden_blocks(hidden_units)
-    far_parts, packed = [], []
-    for wide, index in blocks:
-        *acts, kept, sent = far_feed(
-            place, group[2:], group_grad[2:], gate_proj, up_proj, down_proj, near_grads, wide, index
-        )
-        far_parts.append(acts)
-        packed.append((kept, sent))
-    hid_far, gl_far, ul_far = (jnp.concatenate(parts, 1) for parts in zip(*far_parts))
+        [second_low, beside], group_grad[:2], gate_proj, up_proj, down_proj
+    )
+    across = after(across, near_grads[0])
+    far = (
+        place, [across, swap(across, "mp", 0)], group_grad[2:], gate_proj, up_proj, down_proj,
+        near_grads,
+    )
+    wide = hidden_units // 3
+    assert wide % LANES == 0
+    acts, sums = (), []
+    for n in range(3):
+        acts, [pair] = far_feed(*far, acts, [(0, 1, 2)], wide, n)
+        sums.append(Sum(*pair, (0, 1, 2)))
+        if n == 0:
+            sums[0].send()
+    hid_far, gl_far, ul_far = acts
 
     def back(gate_low, up_low):
         return (inner_cols(gate_low, gate_proj) + inner_cols(up_low, up_proj)).astype(BF16)
@@ -367,12 +402,30 @@
     def onward(hid):
         return dot(hid, down_proj, NN).astype(BF16)
 
-    second_grad = scatter_mp(back(gl_near, ul_near), back(gl_far, ul_far))
-    branch = scatter_mp(onward(hid_near), onward(hid_far))
-    done = ()
-    for (wide, index), (kept, sent) in zip(blocks, packed):
-        done = unpack(place, sum_dp(kept, sent), done, wide, index, features, hidden_units)
-    grad_gate, grad_up, grad_down = done
+    back_far = back(gl_far, ul_far)
+    ready = sums[0].add()
+    back_far = after(back_far, ready)
+    sums[0].send()
+    sums[1].send(ready)
+    back_far = add_low(back_far[:rows], swap(back_far[rows:], "mp", 0))
+    back_across = swap(back_far, "mp", 1)
+    gl_near, ul_near = after((gl_near, ul_near), back_far)
+    back_near = back(gl_near, ul_near)
+    back_beside = swap(back_near[rows:], "mp", 0)
+    ready = sums[0].add()
+    sums[0].send()
+    hid_near, hid_far = after((hid_near, hid_far), ready, back_near)
+    on_near, on_far = onward(hid_near), onward(hid_far)
+    on_beside = swap(on_near[rows:], "mp", 0)
+    on_far = add_low(on_far[:rows], swap(on_far[rows:], "mp", 0))
+    ready = sums[0].add(), sums[1].add(), on_far, on_beside
+    sums[0].send()
+    sums[1].send()
+    sums[2].send(*ready)
+    back_across = after(back_across, *ready)
+    second_grad = back_near[:rows].astype(F32) + back_beside.astype(F32) + back_across.astype(F32)
+    on_across = swap(after(on_far, back_across), "mp", 1)
+    branch = on_near[:rows].astype(F32) + on_beside.astype(F32) + on_across.astype(F32)
     layer_out = (residual + branch).astype(BF16).reshape(1, rows, features)
 
     unit_two = residual * inverse_two
@@ -382,6 +435,10 @@
     )
     second_local = jnp.sum(second_grad * unit_two, axis=0)
     residual_low = residual_grad.astype(BF16)
+    ready = sums[0].add(), sums[1].add()
+    sums[0].send()
+    sums[1].send()
+    residual_low = after(residual_low, *ready)
     out_local = inner_rows(gated_low, residual_low)
     gated_grad = inner_cols(residual_low, weight_out)
     closing_grad = gated_grad * conv
@@ -397,6 +454,11 @@
     mixer_grad = jnp.concatenate(
         [product_grad * carried, closing_grad, product_grad * opening], 1
     ).astype(BF16)
+    ready = sums[0].add(), sums[1].add(), sums[2].add()
+    sums[0].send(ready[2])
+    sums[1].send()
+    sums[2].send()
+    mixer_grad = after(mixer_grad, *ready)
     in_local = inner_rows(first_low, mixer_grad).astype(BF16)
     first_grad = inner_cols(mixer_grad, weight_in)
     weighted = first_grad * gain_one
@@ -404,6 +466,17 @@
         weighted - unit_one * jnp.mean(weighted * unit_one, axis=-1, keepdims=True)
     )
     input_grad = input_grad.reshape(1, rows, features)
+
+    for _ in range(5):
+        for one in sums:
+            if one.step < 5:
+                one.add()
+                one.send()
+    done = ()
+    for n, one in enumerate(sums):
+        one.add()
+        done = unpack(place, one.pieces, done, (0, 1, 2), wide, n, features, hidden_units)
+    grad_gate, grad_up, grad_down = done
 
     small_local = jnp.stack([second_local] + kernel_local, 1).astype(BF16)
     small_local = jnp.pad(small_local, ((0, 0), (0, LANES - small_local.shape[1])))

time: 526 us -> 479 us (0.911); the launches traced: 523 us -> 471 us
  waiting for transfers between devices: 261 us -> 225 us
  starting transfers between devices: 55.7 us -> 40.1 us
  Pallas kernels: 80.1 us -> 71 us
  other arithmetic: 34.6 us -> 41.8 us
    ppermute x52 -> x40, waiting for transfers between devices: 187 us -> 152 us  [swap(): return lax.ppermute(block, axis, [(i, i ^ 1 << bit) for i in range(size)])]
    ppermute x52 -> x40, starting transfers between devices: 50 us -> 34.8 us  [swap(): return lax.ppermute(block, axis, [(i, i ^ 1 << bit) for i in range(size)])]
    pallas_call x10 -> x6, Pallas kernels: 57 us -> 48 us  [the longest x3 35.6 us: far_feed(): pl.pallas_call(functools.partial(far_kernel, orders), grid_spec=pltpu.Pre...]
    convert_element_type x25 -> x19, other arithmetic: 7.93 us -> 14.6 us  [add_low(): return (one.astype(F32) + two.astype(F32)).astype(BF16)]
    unnamed x193 -> x106, local copies, waits for them, and re-layouts: 15.8 us -> 13.6 us
  transfers between devices with their start and end apart: 56 -> 44, of which waited for: 28 -> 19; matrix products, arithmetic and copies ran while one was open for 18% -> 21% of each run, Pallas kernels for 15% -> 13%
where the time goes in v3:
time: 479 us; the launch traced here: 471 us
  waiting for transfers between devices  225 us (47%)
  Pallas kernels  71 us (15%)
  matrix products  48.3 us (10%)
  other arithmetic  41.8 us (9%)
  starting transfers between devices  40.1 us (8%)
  local copies, waits for them, and re-layouts  28.6 us (6%)
  between operations  15.4 us (3%)
    ppermute x40, waiting for transfers between devices, swap(): return lax.ppermute(block, axis, [(i, i ^ 1 << bit) for i in range(size)])  152 us
    all_gather x1, waiting for transfers between devices, per_device(): everything = lax.all_gather(packed, ('dp', 'mp'), axis=0, tiled=True)  73.1 us
    dot_general x10, matrix products, dot(): return lax.dot_general(left, right, dims, preferred_element_type=F32)  39 us
    pallas_call x3, Pallas kernels, far_feed(): pl.pallas_call(functools.partial(far_kernel, orders), grid_spec=pltpu.Pre...  35.6 us
    ppermute x40, starting transfers between devices, swap(): return lax.ppermute(block, axis, [(i, i ^ 1 << bit) for i in range(size)])  34.8 us
    pallas_call x1, Pallas kernels, near_feed(): pl.pallas_call(near_kernel, grid=(pl.cdiv(hidden, wide),), in_specs=[whol...  23.1 us
    convert_element_type x19, other arithmetic, add_low(): return (one.astype(F32) + two.astype(F32)).astype(BF16)  14.6 us
    unnamed x106, local copies, waits for them, and re-layouts  13.6 us
  transfers between devices with their start and end apart: 44, of which 19 were waited for; matrix products, arithmetic and copies ran while one was open for 21% of the time, Pallas kernels for 13%

profile of v3, /device:TPU:0, one launch (start us, length us, event | category | flops | bytes accessed | tf_op | source)
XLA Modules:
  0.0 470.8 jit_solution(4207577454191972536)
XLA Ops:
  21.1 73.1 %all-gather.2.cloned.1.call-done = bf16[1024,4224]{1,0:T(8,128)(2,1)} async-done(((bf16[32,4224]{1,0:T(8,128)(2,1)}), bf16[1024,4224]{1,0:T(8,128)(2,1)}) %all-gather.2.cloned.1.call-update) | async-done | bytes 8650768 | tf_op jit(solution)/shard_map/all_gather | solution.py:338
  97.0 6.0 %fusion.3 = f32[520,3072]{1,0:T(8,128)S(1)} fusion(bf16[520,1024]{1,0:T(8,128)(2,1)S(1)} %multiply_convert_fusion, bf16[1024,4224]{1,0:T(8,128)(2,1)} %all-gather.2.cloned.1.call-done), kind=kOutput, calls=%fused_computation.5 | convolution fusion | flops 3271557120 | bytes 13746176 | tf_op jit(solution)/shard_map/dot_general | solution.py:354
  107.8 3.3 multiply_reduce_fusion.7
  116.7 23.1 %near_feed.1 = (bf16[1024,1152]{1,0:T(8,128)(2,1)}, bf16[1024,1152]{1,0:T(8,128)(2,1)}, bf16[1024,1152]{1,0:T(8,128)(2,1)}, bf16[1024,1152]{1,0:T(8,128)(2,1)}, ...) custom-call(bf16[512,1024]{1,0:T(8,128)(2,1)} %multiply_convert_fusion.2.xa_ref, ...), custom_call_target="tpu_custom_call" | custom-call | flops 14495514624 | bytes 16515072 | tf_op jit(solution)/shard_map/near_feed/pallas_call | solution.py:116
  142.9 11.7 %far_feed.3 = (bf16[1024,1152]{1,0:T(8,128)(2,1)}, bf16[1024,1152]{1,0:T(8,128)(2,1)}, bf16[1024,1152]{1,0:T(8,128)(2,1)}, bf16[4,1152,128]{2,1,0:T(8,128)(2,1)}, bf16[4,1152,128]{2,1,0:T(8,128)(2,1)}) custom-call(s32[1]{0:T(128)} %bitcast.9.place_ref, bf16[512,1024]{1,0:T(8,128)(2,1)} %collective-permute-done.4.xa_ref, ...), custom_call_target="tpu_custom_call" | custom-call | flops 4831838208 | bytes 7077888 | tf_op jit(solution)/shard_map/far_feed/pallas_call | solution.py:181
  156.0 12.2 %far_feed.4 = (bf16[1024,1152]{1,0:T(8,128)(2,1)}, bf16[1024,1152]{1,0:T(8,128)(2,1)}, bf16[1024,1152]{1,0:T(8,128)(2,1)}, bf16[4,1152,128]{2,1,0:T(8,128)(2,1)}, bf16[4,1152,128]{2,1,0:T(8,128)(2,1)}) custom-call(s32[1]{0:T(128)} %bitcast.9.place_ref, ...), custom_call_target="tpu_custom_call", output_to_operand_aliasing={{0}: (11, {}), {1}: (12, {}), {2}: (13, {})} | custom-call | flops 4831838208 | bytes 7077888 | tf_op jit(solution)/shard_map/far_feed/pallas_call | solution.py:181
  168.2 11.7 %far_feed.5 = (bf16[1024,1152]{1,0:T(8,128)(2,1)}, bf16[1024,1152]{1,0:T(8,128)(2,1)}, bf16[1024,1152]{1,0:T(8,128)(2,1)}, bf16[4,1152,128]{2,1,0:T(8,128)(2,1)}, bf16[4,1152,128]{2,1,0:T(8,128)(2,1)}) custom-call(s32[1]{0:T(128)} %bitcast.9.place_ref, ...), custom_call_target="tpu_custom_call", output_to_operand_aliasing={{0}: (11, {}), {1}: (12, {}), {2}: (13, {})} | custom-call | flops 4831838208 | bytes 7077888 | tf_op jit(solution)/shard_map/far_feed/pallas_call | solution.py:181
  179.9 5.4 %fusion.37 = f32[1024,1024]{1,0:T(8,128)S(1)} fusion(bf16[1024,1152]{1,0:T(8,128)(2,1)} %get-tuple-element.70, bf16[1024,1152]{1,0:T(8,128)(2,1)} %up_ref.7), kind=kOutput, calls=%fused_computation.139 | convolution fusion | flops 2415919104 | bytes 8912896 | tf_op jit(solution)/shard_map/dot_general | solution.py:55
  189.6 3.3 add_convert_fusion.1
  195.3 8.0 %collective-permute-done.9 = bf16[2,1152,128]{2,1,0:T(8,128)(2,1)S(1)} collective-permute-done((bf16[2,1152,128]{2,1,0:T(8,128)(2,1)S(1)}, bf16[2,1152,128]{2,1,0:T(8,128)(2,1)S(1)}, u32[]{:S(2)}, u32[]{:S(2)}) %collective-permute-start.9) | collective-permute-done | bytes 589856 | tf_op jit(solution)/shard_map/ppermute | solution.py:26
  206.9 12.6 %collective-permute-done.14 = bf16[1,1152,128]{2,1,0:T(8,128)(2,1)S(1)} collective-permute-done((bf16[1,1152,128]{2,1,0:T(8,128)(2,1)S(1)}, bf16[1,1152,128]{2,1,0:T(8,128)(2,1)S(1)}, u32[]{:S(2)}, u32[]{:S(2)}) %collective-permute-start.14) | collective-permute-done | bytes 294944 | tf_op jit(solution)/shard_map/ppermute | solution.py:26
  223.4 4.7 %fusion.38 = f32[1024,1024]{1,0:T(8,128)S(1)} fusion(bf16[1024,1152]{1,0:T(8,128)(2,1)} %get-tuple-element.73, bf16[1024,1152]{1,0:T(8,128)(2,1)S(1)} %copy-done), kind=kOutput, calls=%fused_computation.140 | convolution fusion | flops 2415919104 | bytes 8912896 | tf_op jit(solution)/shard_map/dot_general | solution.py:55
  228.2 3.1 add_convert_fusion
  234.2 3.1 convolution_convert_fusion.1
  239.1 14.0 %collective-permute-done.19 = bf16[2,1152,128]{2,1,0:T(8,128)(2,1)S(1)} collective-permute-done((bf16[2,1152,128]{2,1,0:T(8,128)(2,1)S(1)}, bf16[2,1152,128]{2,1,0:T(8,128)(2,1)S(1)}, u32[]{:S(2)}, u32[]{:S(2)}) %collective-permute-start.19) | collective-permute-done | bytes 589856 | tf_op jit(solution)/shard_map/ppermute | solution.py:26
  253.2 3.1 convolution_convert_fusion.2
  256.6 9.9 %collective-permute-done.21.refs_2_ = bf16[2,1152,128]{2,1,0:T(8,128)(2,1)S(1)} collective-permute-done((bf16[2,1152,128]{2,1,0:T(8,128)(2,1)S(1)}, bf16[2,1152,128]{2,1,0:T(8,128)(2,1)S(1)}, u32[]{:S(2)}, u32[]{:S(2)}) %collective-permute-start.21) | collective-permute-done | bytes 589856 | tf_op jit(solution)/shard_map/ppermute | solution.py:26
  270.5 13.1 %collective-permute-done.39.refs_1_ = bf16[1,1152,128]{2,1,0:T(8,128)(2,1)S(1)} collective-permute-done((bf16[1,1152,128]{2,1,0:T(8,128)(2,1)S(1)}, bf16[1,1152,128]{2,1,0:T(8,128)(2,1)S(1)}, u32[]{:S(2)}, u32[]{:S(2)}) %collective-permute-start.39) | collective-permute-done | bytes 294944 | tf_op jit(solution)/shard_map/ppermute | solution.py:26
  284.7 14.3 %collective-permute-done.40.refs_2_ = bf16[2,1152,128]{2,1,0:T(8,128)(2,1)S(1)} collective-permute-done((bf16[2,1152,128]{2,1,0:T(8,128)(2,1)S(1)}, bf16[2,1152,128]{2,1,0:T(8,128)(2,1)S(1)}, u32[]{:S(2)}, u32[]{:S(2)}) %collective-permute-start.40) | collective-permute-done | bytes 589856 | tf_op jit(solution)/shard_map/ppermute | solution.py:26
  305.0 3.7 multiply_reduce_fusion.3
  316.5 3.8 convolution_convert_fusion
  327.2 4.3 copy.51
  335.7 7.5 %multiply_reduce_fusion.5 = (f32[512]{0:T(512)S(1)}, f32[512,1024]{1,0:T(8,128)S(1)}) fusion(bf16[1,512,1024]{2,1,0:T(8,128)(2,1)S(1)} %copy-done.20, f32[1024]{0:T(1024)S(1)} %get-tuple-element.145, f32[512]{0:T(512)S(1)} %slice.230, bf16[512,3072]{1,0:T(8,128)(2,1)} %copy-done.21, bf16[1024,4224]{1,0:T(8,128)(2,1)} %all-gather.2.cloned.1.call-done), kind=kOutput, calls=%fused_computation.33 | convolution fusion | flops 3223846400 | bytes 12591104 | tf_op jit(solution)/shard_map/dot_general | solution.py:55
  343.2 7.5 %collective-permute-done.35 = bf16[1,1152,128]{2,1,0:T(8,128)(2,1)S(1)} collective-permute-done((bf16[1,1152,128]{2,1,0:T(8,128)(2,1)S(1)}, bf16[1,1152,128]{2,1,0:T(8,128)(2,1)S(1)}, u32[]{:S(2)}, u32[]{:S(2)}) %collective-permute-start.35) | collective-permute-done | bytes 294944 | tf_op jit(solution)/shard_map/ppermute | solution.py:26
  361.4 5.7 %collective-permute-done.36.refs_1_ = bf16[1,1152,128]{2,1,0:T(8,128)(2,1)S(1)} collective-permute-done((bf16[1,1152,128]{2,1,0:T(8,128)(2,1)S(1)}, bf16[1,1152,128]{2,1,0:T(8,128)(2,1)S(1)}, u32[]{:S(2)}, u32[]{:S(2)}) %collective-permute-start.36) | collective-permute-done | bytes 294944 | tf_op jit(solution)/shard_map/ppermute | solution.py:26
  368.0 4.1 unpack.3
  372.1 4.1 unpack.4
  376.2 29.4 %collective-permute-done.30 = bf16[8,32,1152]{2,1,0:T(8,128)(2,1)} collective-permute-done((bf16[8,32,1152]{2,1,0:T(8,128)(2,1)}, bf16[8,32,1152]{2,1,0:T(8,128)(2,1)}, u32[]{:S(2)}, u32[]{:S(2)}) %collective-permute-start.30) | collective-permute-done | bytes 589856 | tf_op jit(solution)/shard_map/ppermute | solution.py:26
  419.3 14.5 %collective-permute-done.26 = bf16[4,32,3072]{2,1,0:T(8,128)(2,1)S(1)} collective-permute-done((bf16[4,32,3072]{2,1,0:T(8,128)(2,1)S(1)}, bf16[4,32,3072]{2,1,0:T(8,128)(2,1)S(1)}, u32[]{:S(2)}, u32[]{:S(2)}) %collective-permute-start.26) | collective-permute-done | bytes 786464 | tf_op jit(solution)/shard_map/ppermute | solution.py:26
  436.9 7.0 %collective-permute-done.27 = bf16[2,32,3072]{2,1,0:T(8,128)(2,1)S(1)} collective-permute-done((bf16[2,32,3072]{2,1,0:T(8,128)(2,1)S(1)}, bf16[2,32,3072]{2,1,0:T(8,128)(2,1)S(1)}, u32[]{:S(2)}, u32[]{:S(2)}) %collective-permute-start.27) | collective-permute-done | bytes 393248 | tf_op jit(solution)/shard_map/ppermute | solution.py:26
  448.8 8.1 %collective-permute-done.38.refs_3_ = bf16[4,1152,128]{2,1,0:T(8,128)(2,1)S(1)} collective-permute-done((bf16[4,1152,128]{2,1,0:T(8,128)(2,1)}, bf16[4,1152,128]{2,1,0:T(8,128)(2,1)S(1)}, u32[]{:S(2)}, u32[]{:S(2)}) %collective-permute-start.38) | collective-permute-done | bytes 1179680 | tf_op jit(solution)/shard_map/ppermute | solution.py:26
  457.9 4.1 unpack.5
  (265 shorter events, 115.8 us)
Async XLA Ops:
  7.2 87.1 %all-gather.2.cloned.1.call-start = ((), (), s32[]{:S(2)}) async-start(), calls=%async_computation | async-start | bytes 8921088 | tf_op jit(solution)/shard_map/all_gather | solution.py:338
  9.8 105.9 %collective-permute-start.3 = (bf16[512,1024]{1,0:T(8,128)(2,1)}, bf16[512,1024]{1,0:T(8,128)(2,1)}, u32[]{:S(2)}, u32[]{:S(2)}) collective-permute-start(bf16[512,1024]{1,0:T(8,128)(2,1)} %bitcast.131), channel_id=1, source_target_pairs={{0,1},{1,0},{2,3},{3,2},{4,5},{5,4},{6,7},{7,6},{8,9},{9,8},{10,11... | collective-permute-start | bytes 3145736 | tf_op jit(solution)/shard_map/ppermute | solution.py:26
  10.3 103.7 %collective-permute-start.6 = (bf16[512,1024]{1,0:T(8,128)(2,1)}, bf16[512,1024]{1,0:T(8,128)(2,1)S(1)}, u32[]{:S(2)}, u32[]{:S(2)}) collective-permute-start(bf16[512,1024]{1,0:T(8,128)(2,1)} %bitcast.132), channel_id=1, source_target_pairs={{0,2},{1,3},{2,0},{3,1},{4,6},{5,7},{6,4},{7,5},{8,10},{9,11},{10,... | collective-permute-start | bytes 3145736 | tf_op jit(solution)/shard_map/ppermute | solution.py:26
  113.9 26.2 %collective-permute-start.7 = (bf16[512,1024]{1,0:T(8,128)(2,1)S(1)}, bf16[512,1024]{1,0:T(8,128)(2,1)}, u32[]{:S(2)}, u32[]{:S(2)}) collective-permute-start(bf16[512,1024]{1,0:T(8,128)(2,1)S(1)} %collective-permute-done.6.ga_ref), channel_id=1, source_target_pairs={{0,1},{1,0},{2,3},{3,2},{4,5},{5,4},{6,7},{7,6},{8,9},{9,8},{10,11... | collective-permute-start | bytes 3145736 | tf_op jit(solution)/shard_map/ppermute | solution.py:26
  114.2 25.6 %collective-permute-start.4 = (bf16[512,1024]{1,0:T(8,128)(2,1)}, bf16[512,1024]{1,0:T(8,128)(2,1)}, u32[]{:S(2)}, u32[]{:S(2)}) collective-permute-start(bf16[512,1024]{1,0:T(8,128)(2,1)} %multiply_convert_fusion.2.xa_ref), channel_id=1, source_target_pairs={{0,2},{1,3},{2,0},{3,1},{4,6},{5,7},{6,4},{7,5},{8,10},{9,11},{10,... | collective-permute-start | bytes 3145736 | tf_op jit(solution)/shard_map/ppermute | solution.py:26
  154.6 30.8 %collective-permute-start.8 = (bf16[4,1152,128]{2,1,0:T(8,128)(2,1)}, bf16[4,1152,128]{2,1,0:T(8,128)(2,1)S(1)}, u32[]{:S(2)}, u32[]{:S(2)}) collective-permute-start(bf16[4,1152,128]{2,1,0:T(8,128)(2,1)} %get-tuple-element.66), channel_id=1, source_target_pairs={{0,4},{4,0},{8,12},{12,8},{16,20},{20,16},{24,28},{28,24},{1,5},{5... | collective-permute-start | bytes 3538952 | tf_op jit(solution)/shard_map/ppermute | solution.py:26
  195.3 25.4 %collective-permute-start.10 = (bf16[512,1024]{1,0:T(8,128)(2,1)}, bf16[512,1024]{1,0:T(8,128)(2,1)}, u32[]{:S(2)}, u32[]{:S(2)}) collective-permute-start(bf16[512,1024]{1,0:T(8,128)(2,1)} %slice.219), channel_id=1, source_target_pairs={{0,1},{1,0},{2,3},{3,2},{4,5},{5,4},{6,7},{7,6},{8,9},{9,8},{10,11... | collective-permute-start | bytes 3145736 | tf_op jit(solution)/shard_map/ppermute | solution.py:26
  204.2 15.3 %collective-permute-start.14 = (bf16[1,1152,128]{2,1,0:T(8,128)(2,1)S(1)}, bf16[1,1152,128]{2,1,0:T(8,128)(2,1)S(1)}, u32[]{:S(2)}, u32[]{:S(2)}) collective-permute-start(bf16[1,1152,128]{2,1,0:T(8,128)(2,1)S(1)} %add_convert_fusion.19), channel_id=1, source_target_pairs={{0,16},{4,20},{8,24},{12,28},{16,0},{20,4},{24,8},{28,12},{1,17},{... | collective-permute-start | bytes 884744 | tf_op jit(solution)/shard_map/ppermute | solution.py:26
  206.3 26.9 %collective-permute-start.15 = (bf16[4,1152,128]{2,1,0:T(8,128)(2,1)}, bf16[4,1152,128]{2,1,0:T(8,128)(2,1)S(1)}, u32[]{:S(2)}, u32[]{:S(2)}) collective-permute-start(bf16[4,1152,128]{2,1,0:T(8,128)(2,1)} %get-tuple-element.78), channel_id=1, source_target_pairs={{0,4},{4,0},{8,12},{12,8},{16,20},{20,16},{24,28},{28,24},{1,5},{5... | collective-permute-start | bytes 3538952 | tf_op jit(solution)/shard_map/ppermute | solution.py:26
  220.6 16.8 %collective-permute-start.18 = (bf16[1,1152,128]{2,1,0:T(8,128)(2,1)S(1)}, bf16[1,1152,128]{2,1,0:T(8,128)(2,1)S(1)}, u32[]{:S(2)}, u32[]{:S(2)}) collective-permute-start(bf16[1,1152,128]{2,1,0:T(8,128)(2,1)S(1)} %add_convert_fusion.17.refs_0_), channel_id=1, source_target_pairs={{0,16},{4,20},{8,24},{12,28},{16,0},{20,4},{24,8},{28,12},{1,17},{... | collective-permute-start | bytes 884744 | tf_op jit(solution)/shard_map/ppermute | solution.py:26
  222.7 45.8 %collective-permute-start.13 = (bf16[512,1024]{1,0:T(8,128)(2,1)S(1)}, bf16[512,1024]{1,0:T(8,128)(2,1)S(1)}, u32[]{:S(2)}, u32[]{:S(2)}) collective-permute-start(bf16[512,1024]{1,0:T(8,128)(2,1)S(1)} %add_convert_fusion.4), channel_id=1, source_target_pairs={{0,2},{1,3},{2,0},{3,1},{4,6},{5,7},{6,4},{7,5},{8,10},{9,11},{10,... | collective-permute-start | bytes 3145736 | tf_op jit(solution)/shard_map/ppermute | solution.py:26
  233.6 19.5 %collective-permute-start.19 = (bf16[2,1152,128]{2,1,0:T(8,128)(2,1)S(1)}, bf16[2,1152,128]{2,1,0:T(8,128)(2,1)S(1)}, u32[]{:S(2)}, u32[]{:S(2)}) collective-permute-start(bf16[2,1152,128]{2,1,0:T(8,128)(2,1)S(1)} %get-tuple-element.158), channel_id=1, source_target_pairs={{0,8},{4,12},{8,0},{12,4},{16,24},{20,28},{24,16},{28,20},{1,9},{5... | collective-permute-start | bytes 1769480 | tf_op jit(solution)/shard_map/ppermute | solution.py:26
  237.4 30.7 %collective-permute-start.12 = (bf16[512,1024]{1,0:T(8,128)(2,1)S(1)}, bf16[512,1024]{1,0:T(8,128)(2,1)S(1)}, u32[]{:S(2)}, u32[]{:S(2)}) collective-permute-start(bf16[512,1024]{1,0:T(8,128)(2,1)S(1)} %slice.274), channel_id=1, source_target_pairs={{0,1},{1,0},{2,3},{3,2},{4,5},{5,4},{6,7},{7,6},{8,9},{9,8},{10,11... | collective-permute-start | bytes 3145736 | tf_op jit(solution)/shard_map/ppermute | solution.py:26
  237.5 28.9 %collective-permute-start.21 = (bf16[2,1152,128]{2,1,0:T(8,128)(2,1)S(1)}, bf16[2,1152,128]{2,1,0:T(8,128)(2,1)S(1)}, u32[]{:S(2)}, u32[]{:S(2)}) collective-permute-start(bf16[2,1152,128]{2,1,0:T(8,128)(2,1)S(1)} %pad_maximum_fusion.6), channel_id=1, source_target_pairs={{0,8},{4,12},{8,0},{12,4},{16,24},{20,28},{24,16},{28,20},{1,9},{5... | collective-permute-start | bytes 1769480 | tf_op jit(solution)/shard_map/ppermute | solution.py:26
  266.4 17.3 %collective-permute-start.17 = (bf16[512,1024]{1,0:T(8,128)(2,1)S(1)}, bf16[512,1024]{1,0:T(8,128)(2,1)S(1)}, u32[]{:S(2)}, u32[]{:S(2)}) collective-permute-start(bf16[512,1024]{1,0:T(8,128)(2,1)S(1)} %slice.279), channel_id=1, source_target_pairs={{0,1},{1,0},{2,3},{3,2},{4,5},{5,4},{6,7},{7,6},{8,9},{9,8},{10,11... | collective-permute-start | bytes 3145736 | tf_op jit(solution)/shard_map/ppermute | solution.py:26
  267.8 15.8 %collective-permute-start.39 = (bf16[1,1152,128]{2,1,0:T(8,128)(2,1)S(1)}, bf16[1,1152,128]{2,1,0:T(8,128)(2,1)S(1)}, u32[]{:S(2)}, u32[]{:S(2)}) collective-permute-start(bf16[1,1152,128]{2,1,0:T(8,128)(2,1)S(1)} %add_convert_fusion.14.refs_0_), channel_id=1, source_target_pairs={{0,16},{4,20},{8,24},{12,28},{16,0},{20,4},{24,8},{28,12},{1,17},{... | collective-permute-start | bytes 884744 | tf_op jit(solution)/shard_map/ppermute | solution.py:26
  268.5 33.7 %collective-permute-start.16 = (bf16[512,1024]{1,0:T(8,128)(2,1)S(1)}, bf16[512,1024]{1,0:T(8,128)(2,1)S(1)}, u32[]{:S(2)}, u32[]{:S(2)}) collective-permute-start(bf16[512,1024]{1,0:T(8,128)(2,1)S(1)} %add_convert_fusion.3), channel_id=1, source_target_pairs={{0,2},{1,3},{2,0},{3,1},{4,6},{5,7},{6,4},{7,5},{8,10},{9,11},{10,... | collective-permute-start | bytes 3145736 | tf_op jit(solution)/shard_map/ppermute | solution.py:26
  269.9 44.5 %collective-permute-start.23 = (bf16[4,1152,128]{2,1,0:T(8,128)(2,1)S(1)}, bf16[4,1152,128]{2,1,0:T(8,128)(2,1)S(1)}, u32[]{:S(2)}, u32[]{:S(2)}) collective-permute-start(bf16[4,1152,128]{2,1,0:T(8,128)(2,1)S(1)} %copy-done.45), channel_id=1, source_target_pairs={{0,4},{4,0},{8,12},{12,8},{16,20},{20,16},{24,28},{28,24},{1,5},{5... | collective-permute-start | bytes 3538952 | tf_op jit(solution)/shard_map/ppermute | solution.py:26
  283.6 15.4 %collective-permute-start.40 = (bf16[2,1152,128]{2,1,0:T(8,128)(2,1)S(1)}, bf16[2,1152,128]{2,1,0:T(8,128)(2,1)S(1)}, u32[]{:S(2)}, u32[]{:S(2)}) collective-permute-start(bf16[2,1152,128]{2,1,0:T(8,128)(2,1)S(1)} %pad_maximum_fusion.8), channel_id=1, source_target_pairs={{0,8},{4,12},{8,0},{12,4},{16,24},{20,28},{24,16},{28,20},{1,9},{5... | collective-permute-start | bytes 1769480 | tf_op jit(solution)/shard_map/ppermute | solution.py:26
  301.1 71.0 %collective-permute-start.41 = (bf16[4,1152,128]{2,1,0:T(8,128)(2,1)}, bf16[4,1152,128]{2,1,0:T(8,128)(2,1)}, u32[]{:S(2)}, u32[]{:S(2)}) collective-permute-start(bf16[4,1152,128]{2,1,0:T(8,128)(2,1)} %pad_maximum_fusion.5), channel_id=1, source_target_pairs={{0,4},{4,0},{8,12},{12,8},{16,20},{20,16},{24,28},{28,24},{1,5},{5... | collective-permute-start | bytes 3538952 | tf_op jit(solution)/shard_map/ppermute | solution.py:26
  315.5 18.8 %collective-permute-start.34 = (bf16[2,1152,128]{2,1,0:T(8,128)(2,1)S(1)}, bf16[2,1152,128]{2,1,0:T(8,128)(2,1)S(1)}, u32[]{:S(2)}, u32[]{:S(2)}) collective-permute-start(bf16[2,1152,128]{2,1,0:T(8,128)(2,1)S(1)} %get-tuple-element.156), channel_id=1, source_target_pairs={{0,8},{4,12},{8,0},{12,4},{16,24},{20,28},{24,16},{28,20},{1,9},{5... | collective-permute-start | bytes 1769480 | tf_op jit(solution)/shard_map/ppermute | solution.py:26
  323.9 28.3 %collective-permute-start.24 = (bf16[16,32,3072]{2,1,0:T(8,128)(2,1)}, bf16[16,32,3072]{2,1,0:T(8,128)(2,1)}, u32[]{:S(2)}, u32[]{:S(2)}) collective-permute-start(bf16[16,32,3072]{2,1,0:T(8,128)(2,1)} %dynamic-slice_bitcast_fusion), channel_id=1, source_target_pairs={{0,1},{1,0},{2,3},{3,2},{4,5},{5,4},{6,7},{7,6},{8,9},{9,8},{10,11... | collective-permute-start | bytes 9437192 | tf_op jit(solution)/shard_map/ppermute | solution.py:26
  333.0 18.8 %collective-permute-start.29 = (bf16[16,32,1152]{2,1,0:T(8,128)(2,1)S(1)}, bf16[16,32,1152]{2,1,0:T(8,128)(2,1)S(1)}, u32[]{:S(2)}, u32[]{:S(2)}) collective-permute-start(bf16[16,32,1152]{2,1,0:T(8,128)(2,1)S(1)} %dynamic-slice_bitcast_fusion.2), channel_id=1, source_target_pairs={{0,1},{1,0},{2,3},{3,2},{4,5},{5,4},{6,7},{7,6},{8,9},{9,8},{10,11... | collective-permute-start | bytes 3538952 | tf_op jit(solution)/shard_map/ppermute | solution.py:26
  333.1 34.9 %collective-permute-start.42 = (bf16[4,1152,128]{2,1,0:T(8,128)(2,1)S(1)}, bf16[4,1152,128]{2,1,0:T(8,128)(2,1)}, u32[]{:S(2)}, u32[]{:S(2)}) collective-permute-start(bf16[4,1152,128]{2,1,0:T(8,128)(2,1)S(1)} %copy-done.34), channel_id=1, source_target_pairs={{0,4},{4,0},{8,12},{12,8},{16,20},{20,16},{24,28},{28,24},{1,5},{5... | collective-permute-start | bytes 3538952 | tf_op jit(solution)/shard_map/ppermute | solution.py:26
  334.4 16.4 %collective-permute-start.35 = (bf16[1,1152,128]{2,1,0:T(8,128)(2,1)S(1)}, bf16[1,1152,128]{2,1,0:T(8,128)(2,1)S(1)}, u32[]{:S(2)}, u32[]{:S(2)}) collective-permute-start(bf16[1,1152,128]{2,1,0:T(8,128)(2,1)S(1)} %add_convert_fusion.12), channel_id=1, source_target_pairs={{0,16},{4,20},{8,24},{12,28},{16,0},{20,4},{24,8},{28,12},{1,17},{... | collective-permute-start | bytes 884744 | tf_op jit(solution)/shard_map/ppermute | solution.py:26
  356.6 51.3 %collective-permute-start.25 = (bf16[8,32,3072]{2,1,0:T(8,128)(2,1)}, bf16[8,32,3072]{2,1,0:T(8,128)(2,1)}, u32[]{:S(2)}, u32[]{:S(2)}) collective-permute-start(bf16[8,32,3072]{2,1,0:T(8,128)(2,1)} %dynamic-slice_bitcast_fusion.1), channel_id=1, source_target_pairs={{0,2},{1,3},{2,0},{3,1},{4,6},{5,7},{6,4},{7,5},{8,10},{9,11},{10,... | collective-permute-start | bytes 4718600 | tf_op jit(solution)/shard_map/ppermute | solution.py:26
  357.8 47.8 %collective-permute-start.30 = (bf16[8,32,1152]{2,1,0:T(8,128)(2,1)}, bf16[8,32,1152]{2,1,0:T(8,128)(2,1)}, u32[]{:S(2)}, u32[]{:S(2)}) collective-permute-start(bf16[8,32,1152]{2,1,0:T(8,128)(2,1)} %dynamic-slice_bitcast_fusion.4), channel_id=1, source_target_pairs={{0,2},{1,3},{2,0},{3,1},{4,6},{5,7},{6,4},{7,5},{8,10},{9,11},{10,... | collective-permute-start | bytes 1769480 | tf_op jit(solution)/shard_map/ppermute | solution.py:26
  368.0 43.6 %collective-permute-start.37 = (bf16[2,1152,128]{2,1,0:T(8,128)(2,1)}, bf16[2,1152,128]{2,1,0:T(8,128)(2,1)}, u32[]{:S(2)}, u32[]{:S(2)}) collective-permute-start(bf16[2,1152,128]{2,1,0:T(8,128)(2,1)} %pad_maximum_fusion.7), channel_id=1, source_target_pairs={{0,8},{4,12},{8,0},{12,4},{16,24},{20,28},{24,16},{28,20},{1,9},{5... | collective-permute-start | bytes 1769480 | tf_op jit(solution)/shard_map/ppermute | solution.py:26
  410.5 23.3 %collective-permute-start.26 = (bf16[4,32,3072]{2,1,0:T(8,128)(2,1)S(1)}, bf16[4,32,3072]{2,1,0:T(8,128)(2,1)S(1)}, u32[]{:S(2)}, u32[]{:S(2)}) collective-permute-start(bf16[4,32,3072]{2,1,0:T(8,128)(2,1)S(1)} %dynamic-slice_bitcast_fusion.3), channel_id=1, source_target_pairs={{0,4},{4,0},{8,12},{12,8},{16,20},{20,16},{24,28},{28,24},{1,5},{5... | collective-permute-start | bytes 2359304 | tf_op jit(solution)/shard_map/ppermute | solution.py:26
  413.8 43.1 %collective-permute-start.38 = (bf16[4,1152,128]{2,1,0:T(8,128)(2,1)}, bf16[4,1152,128]{2,1,0:T(8,128)(2,1)S(1)}, u32[]{:S(2)}, u32[]{:S(2)}) collective-permute-start(bf16[4,1152,128]{2,1,0:T(8,128)(2,1)} %pad_maximum_fusion.4), channel_id=1, source_target_pairs={{0,4},{4,0},{8,12},{12,8},{16,20},{20,16},{24,28},{28,24},{1,5},{5... | collective-permute-start | bytes 3538952 | tf_op jit(solution)/shard_map/ppermute | solution.py:26
  417.0 19.3 %collective-permute-start.32 = (bf16[2,32,1152]{2,1,0:T(8,128)(2,1)S(1)}, bf16[2,32,1152]{2,1,0:T(8,128)(2,1)S(1)}, u32[]{:S(2)}, u32[]{:S(2)}) collective-permute-start(bf16[2,32,1152]{2,1,0:T(8,128)(2,1)S(1)} %dynamic-slice_bitcast_fusion.7), channel_id=1, source_target_pairs={{0,8},{4,12},{8,0},{12,4},{16,24},{20,28},{24,16},{28,20},{1,9},{5... | collective-permute-start | bytes 442376 | tf_op jit(solution)/shard_map/ppermute | solution.py:26
  444.0 18.0 %collective-permute-start.28 = (bf16[1,32,3072]{2,1,0:T(8,128)(2,1)S(1)}, bf16[1,32,3072]{2,1,0:T(8,128)(2,1)S(1)}, u32[]{:S(2)}, u32[]{:S(2)}) collective-permute-start(bf16[1,32,3072]{2,1,0:T(8,128)(2,1)S(1)} %constant_dynamic-slice_fusion.1), channel_id=1, source_target_pairs={{0,16},{4,20},{8,24},{12,28},{16,0},{20,4},{24,8},{28,12},{1,17},{... | collective-permute-start | bytes 589832 | tf_op jit(solution)/shard_map/ppermute | solution.py:26
  (64 other events, 620.6 us)
Sparse Core Ops, SparseCore 0:
  11.5 82.6 all-gather.1

commit v4 on v3

v4 whole, which is shorter than its diff:
```python
import functools

import jax
import jax.numpy as jnp
from jax import lax
from jax.experimental import pallas as pl
from jax.experimental.pallas import tpu as pltpu
from jax.sharding import PartitionSpec as P

KERNEL = 3
LANES = 128
BF16 = jnp.bfloat16
F32 = jnp.float32
HALVINGS = 3
PARTS = 1 << HALVINGS
NN = (((1,), (0,)), ((), ()))
NT = (((1,), (1,)), ((), ()))
TN = (((0,), (0,)), ((), ()))
VMEM_LIMIT = 60 * 1024 * 1024
LONG = pl.CostEstimate(flops=10**11, transcendentals=0, bytes_accessed=0)

epsilon = 1e-05


def swap(block, axis, bit):
    size = lax.axis_size(axis)
    return lax.ppermute(block, axis, [(i, i ^ (1 << bit)) for i in range(size)])


def shift(block, axis, distance):
    devices = range(lax.axis_size(axis))
    route = [(i - distance, i) for i in devices if i - distance in devices]
    return lax.ppermute(block, axis, route)


def bit_of(axis, bit):
    return (lax.axis_index(axis) >> bit) & 1


def bits_of(axis):
    size = lax.axis_size(axis)
    assert size & (size - 1) == 0
    return size.bit_length() - 1


def after(values, *before):
    return lax.optimization_barrier((values, before))[0]


class Order:
    def __init__(self):
        self.last = ()

    def __call__(self, values):
        return after(values, self.last)

    def mark(self, out):
        self.last = out
        return out


def away(bits):
    top = len(bits) - 1
    return [sum(((q >> (top - n)) & 1) << bit for n, bit in enumerate(bits)) for q in range(PARTS)]


def dot(left, right, dims):
    return lax.dot_general(left, right, dims, preferred_element_type=F32)


def activate(gate_val, up_val, hidden_grad):
    sig = 1.0 / (1.0 + jnp.exp(-gate_val))
    silu = gate_val * sig
    return (
        (silu * up_val).astype(BF16),
        (hidden_grad * up_val * (sig * (1.0 + gate_val * (1.0 - sig)))).astype(BF16),
        (hidden_grad * silu).astype(BF16),
    )


def feed(x_ref, go_ref, gate_ref, up_ref, down_ref, acts, outs):
    for n in range(2):
        step = x_ref.shape[0] // 2
        part = slice(n * step, (n + 1) * step)
        gate_val = dot(x_ref[part], gate_ref[...], NN)
        up_val = dot(x_ref[part], up_ref[...], NN)
        hidden_grad = dot(go_ref[part], down_ref[...], NT)
        for m, value in enumerate(activate(gate_val, up_val, hidden_grad)):
            acts[m][part] = value
            outs[2 * m + n][...] = value


def join(first, xa_ref, xb_ref, ga_ref, gb_ref, x_ref, go_ref):
    rows = xa_ref.shape[0]

    @pl.when(first)
    def _():
        x_ref[:rows] = xa_ref[...]
        x_ref[rows:] = xb_ref[...]
        go_ref[:rows] = ga_ref[...]
        go_ref[rows:] = gb_ref[...]


def near_kernel(xa_ref, xb_ref, ga_ref, gb_ref, gate_ref, up_ref, down_ref,
                *refs):
    outs = refs[:6]
    og_ref, ou_ref, od_ref, x_ref, go_ref, hid_ref, gl_ref, ul_ref = refs[6:]
    join(pl.program_id(0) == 0, xa_ref, xb_ref, ga_ref, gb_ref, x_ref, go_ref)
    feed(x_ref, go_ref, gate_ref, up_ref, down_ref, (hid_ref, gl_ref, ul_ref), outs)
    og_ref[...] = dot(x_ref[...], gl_ref[...], TN).astype(BF16)
    ou_ref[...] = dot(x_ref[...], ul_ref[...], TN).astype(BF16)
    od_ref[...] = dot(hid_ref[...], go_ref[...], TN).astype(BF16)


def near_feed(xs, gos, gate, up, down):
    rows, features = xs[0].shape
    hidden = gate.shape[1]
    wide = 256
    tokens = 2 * rows
    whole = pl.BlockSpec((rows, features), lambda i: (0, 0), pipeline_mode=pl.Buffered(1))
    col = pl.BlockSpec((features, wide), lambda i: (0, i))
    row = pl.BlockSpec((wide, features), lambda i: (i, 0))
    act = pl.BlockSpec((rows, wide), lambda i: (0, i))
    return pl.pallas_call(
        near_kernel,
        grid=(pl.cdiv(hidden, wide),),
        in_specs=[whole] * 4 + [col, col, row],
        out_specs=[act] * 6 + [col, col, row],
        out_shape=[jax.ShapeDtypeStruct((rows, hidden), BF16)] * 6
        + [jax.ShapeDtypeStruct((features, hidden), BF16)] * 2
        + [jax.ShapeDtypeStruct((hidden, features), BF16)],
        scratch_shapes=[pltpu.VMEM((tokens, features), BF16)] * 2
        + [pltpu.VMEM((tokens, wide), BF16)] * 3,
        compiler_params=pltpu.CompilerParams(vmem_limit_bytes=VMEM_LIMIT),
        cost_estimate=LONG,
        name="near_feed",
    )(*xs, *gos, gate, up, down)


def far_kernel(orders, place_ref, xa_ref, xb_ref, ga_ref, gb_ref, gate_ref, up_ref, down_ref,
               ng_ref, nu_ref, nd_ref, *refs):
    blocks = len(orders)
    x_ref, go_ref, tg_ref, tu_ref, td_ref, hid_ref, gl_ref, ul_ref = refs[-8:]
    packs = refs[-8 - 2 * blocks : -8]
    outs = refs[-14 - 2 * blocks : -8 - 2 * blocks]
    now = pl.program_id(0)
    join(now == 0, xa_ref, xb_ref, ga_ref, gb_ref, x_ref, go_ref)
    feed(x_ref, go_ref, gate_ref, up_ref, down_ref, (hid_ref, gl_ref, ul_ref), outs)
    tg_ref[...] = ng_ref[...].astype(F32) + dot(x_ref[...], gl_ref[...], TN)
    tu_ref[...] = nu_ref[...].astype(F32) + dot(x_ref[...], ul_ref[...], TN)
    td_ref[...] = nd_ref[...].astype(F32) + dot(hid_ref[...], go_ref[...], TN)
    features, wide = tg_ref.shape
    tall, low = features // PARTS, wide // PARTS
    for n, bits in enumerate(orders):

        @pl.when(now == n)
        def _(n=n, bits=bits):
            for q, far in enumerate(away(bits or (0, 1, 2))):
                part = place_ref[0] ^ far if bits else far
                half = PARTS // 2
                out = packs[2 * n + q // half].at[q % half]
                rows = pl.ds(part * tall, tall)
                at = 0
                for grad_ref in (tg_ref, tu_ref):
                    for c in range(0, wide, LANES):
                        out[at : at + tall] = grad_ref[rows, c : c + LANES].astype(BF16)
                        at += tall
                rows = pl.ds(part * low, low)
                for c in range(0, features, LANES):
                    out[at : at + low] = td_ref[rows, c : c + LANES].astype(BF16)
                    at += low


def far_feed(place, xs, gos, gate, up, down, near_grads, before, orders, wide, index):
    rows, features = xs[0].shape
    tokens = 2 * rows
    hidden = gate.shape[1]
    blocks = len(orders)
    whole = pl.BlockSpec((rows, features), lambda i, _: (0, 0), pipeline_mode=pl.Buffered(1))
    col = pl.BlockSpec((features, wide), lambda i, _: (0, index + i))
    row = pl.BlockSpec((wide, features), lambda i, _: (index + i, 0))
    act = pl.BlockSpec((rows, wide), lambda i, _: (0, index + i))
    packed = 3 * features * wide // PARTS // LANES
    half = pl.BlockSpec((PARTS // 2, packed, LANES), lambda i, _: (0, 0, 0), pipeline_mode=pl.Buffered(1))
    first = 1 + 4 + 3 + 3
    results = pl.pallas_call(
        functools.partial(far_kernel, orders),
        grid_spec=pltpu.PrefetchScalarGridSpec(
            num_scalar_prefetch=1,
            grid=(blocks,),
            in_specs=[whole] * 4
            + [col, col, row] * 2
            + [pl.BlockSpec(memory_space=pl.ANY)] * len(before),
            out_specs=[act] * 6 + [half] * (2 * blocks),
            scratch_shapes=[pltpu.VMEM((tokens, features), BF16)] * 2
            + [pltpu.VMEM((features, wide), F32)] * 2
            + [pltpu.VMEM((wide, features), F32)]
            + [pltpu.VMEM((tokens, wide), BF16)] * 3,
        ),
        out_shape=[jax.ShapeDtypeStruct((rows, hidden), BF16)] * 6
        + [jax.ShapeDtypeStruct((PARTS // 2, packed, LANES), BF16)] * (2 * blocks),
        input_output_aliases={first + n: n for n in range(len(before))},
        compiler_params=pltpu.CompilerParams(vmem_limit_bytes=VMEM_LIMIT),
        cost_estimate=LONG,
        name="far_feed",
    )(place, *xs, *gos, gate, up, down, *near_grads, *before)
    return results[:6], list(zip(results[6::2], results[7::2]))


def unpack_kernel(bits, pieces, place_ref, *refs):
    og_ref, ou_ref, od_ref = refs[-3:]
    features, wide = og_ref.shape
    tall, low = features // PARTS, wide // PARTS
    sources = [ref.at[n] for ref in refs[:pieces] for n in range(ref.shape[0])]
    for source, far in zip(sources, away(bits or (0, 1, 2))):
        part = place_ref[0] ^ far if bits else far
        rows = pl.ds(part * tall, tall)
        at = 0
        for out in (og_ref, ou_ref):
            for c in range(0, wide, LANES):
                out[rows, c : c + LANES] = source[at : at + tall].astype(F32)
                at += tall
        rows = pl.ds(part * low, low)
        for c in range(0, features, LANES):
            od_ref[rows, c : c + LANES] = source[at : at + low].astype(F32)
            at += low


def unpack(place, pieces, before, bits, wide, index, features, hidden):
    packed = pieces[0].shape[1]
    ins = [
        pl.BlockSpec((piece.shape[0], packed, LANES), lambda i, _: (0, 0, 0)) for piece in pieces
    ]
    col = pl.BlockSpec((features, wide), lambda i, _: (0, index))
    row = pl.BlockSpec((wide, features), lambda i, _: (index, 0))
    keep = [pl.BlockSpec(memory_space=pl.ANY)] * len(before)
    return pl.pallas_call(
        functools.partial(unpack_kernel, bits, len(pieces)),
        grid_spec=pltpu.PrefetchScalarGridSpec(
            num_scalar_prefetch=1,
            grid=(1,),
            in_specs=ins + keep,
            out_specs=[col, col, row],
        ),
        out_shape=[jax.ShapeDtypeStruct((features, hidden), F32)] * 2
        + [jax.ShapeDtypeStruct((hidden, features), F32)],
        input_output_aliases={1 + len(ins) + n: n for n in range(len(before))},
        compiler_params=pltpu.CompilerParams(vmem_limit_bytes=VMEM_LIMIT),
        cost_estimate=LONG,
        name="unpack",
    )(place, *pieces, *before)


def add_low(one, two):
    return (one.astype(F32) + two.astype(F32)).astype(BF16)


def whole(array):
    return pl.BlockSpec(array.shape, lambda i: (0,) * array.ndim)


def halve_kernel(kept_ref, got_ref, *outs):
    half = outs[-1].shape[0]
    for n, out in enumerate(outs):
        part = slice(n * half, (n + 1) * half)
        out[...] = (kept_ref[part].astype(F32) + got_ref[part].astype(F32)).astype(out.dtype)


def halve(kept, got, halves=2, dtype=BF16):
    count, tall, wide = kept.shape
    shapes = [jax.ShapeDtypeStruct((count // halves, tall, wide), dtype)] * halves
    return pl.pallas_call(
        halve_kernel,
        grid=(1,),
        in_specs=[whole(kept), whole(got)],
        out_specs=[whole(s) for s in shapes],
        out_shape=shapes,
        compiler_params=pltpu.CompilerParams(vmem_limit_bytes=VMEM_LIMIT),
        cost_estimate=LONG,
        name="halve",
    )(kept, got)


def lay_kernel(*refs):
    at = 0
    for ref in refs[:-1]:
        refs[-1][at : at + ref.shape[0]] = ref[...]
        at += ref.shape[0]


def lay(pieces):
    _, tall, wide = pieces[0].shape
    shape = jax.ShapeDtypeStruct((sum(p.shape[0] for p in pieces), tall, wide), pieces[0].dtype)
    return pl.pallas_call(
        lay_kernel,
        grid=(1,),
        in_specs=[whole(p) for p in pieces],
        out_specs=whole(shape),
        out_shape=shape,
        compiler_params=pltpu.CompilerParams(vmem_limit_bytes=VMEM_LIMIT),
        cost_estimate=LONG,
        name="lay",
    )(*pieces)


def pack_rows(place, bits, grad_ref, kept_ref, sent_ref, lane):
    count = len(bits)
    half, tall, _ = kept_ref.shape
    wide = grad_ref.shape[1]

    def move(q, out_ref, slot):
        far = 0
        for n, bit in enumerate(bits):
            far = far | (((q >> (count - 1 - n)) & 1) << bit)
        rows = pl.ds(pl.multiple_of((place ^ far) * tall, tall), tall)
        out_ref[slot, :, lane : lane + wide] = grad_ref[rows].astype(BF16)

    @pl.loop(0, half)
    def _(q):
        move(q, kept_ref, q)
        move(q + half, sent_ref, q)


STRIP = 64
RIM = 8


def fold(values):
    return jnp.sum(values.reshape(values.shape[0] // 8, 8, values.shape[1]), axis=0)


def assemble(place, bits, sources, width, target_ref, lane, sems):
    half, tall, _ = sources[0][0].shape
    count = len(bits)

    def copy(q, n):
        ref, start = sources[n]
        far = 0
        for m, bit in enumerate(bits):
            far = far | ((((q + n * half) >> m) & 1) << bit)
        rows = pl.ds(pl.multiple_of((place ^ far) * tall, tall), tall)
        return pltpu.make_async_copy(
            ref.at[q, :, start : start + width],
            target_ref.at[rows, lane : lane + width],
            sems.at[n * half + q],
        )

    @pl.loop(0, half)
    def _(q):
        for n in range(2):
            copy(q, n).start()

    def wait():
        @pl.loop(0, half)
        def _(q):
            for n in range(2):
                copy(q, n).wait()

    return wait


def mix_front_kernel(bits, place_ref, in_any, c0, c1, x_ref, before_ref, same_ref,
                     mix_any, low_any, gated_any, vec_ref, res_ref, second_ref,
                     w_ref, wo_ref, mix_ref, low_ref, gated_ref, ext_ref, sems, in_sem, out_sem):
    place = place_ref[0]
    rows, features = x_ref.shape
    last = features + LANES
    wide = features
    loads = [
        pltpu.make_async_copy(
            in_any.at[:, n * wide : (n + 1) * wide], w_ref.at[:, n * wide : (n + 1) * wide], in_sem.at[n]
        )
        for n in range(3)
    ]
    wait_out = assemble(place, bits, [(c0, 0), (c1, 0)], features + LANES, wo_ref, 0, sems)
    for load in loads:
        load.start()
    wait_out()
    vec_ref[...] = wo_ref[:, features:].astype(F32).T[:8]
    gain_one, gain_two = vec_ref[0:1], vec_ref[1:2]
    taps = [vec_ref[2 + k : 3 + k] for k in range(KERNEL)]

    def normed(values, gain):
        inverse = lax.rsqrt(jnp.mean(values * values, axis=-1, keepdims=True) + epsilon)
        return (values * inverse * gain).astype(BF16)

    low_ref[:RIM] = normed(before_ref[...].astype(F32), gain_one)

    @pl.loop(0, rows // STRIP)
    def _(i):
        at = pl.ds(pl.multiple_of(i * STRIP, STRIP), STRIP)
        inner = pl.ds(pl.multiple_of(i * STRIP + RIM, RIM), STRIP)
        low_ref[inner] = normed(x_ref[at].astype(F32), gain_one)

    stores = [pltpu.make_async_copy(low_ref, low_any, out_sem.at[0])]
    stores[0].start()
    for n, load in enumerate(loads):
        load.wait()
        part = slice(n * wide, (n + 1) * wide)
        mix_ref[:, part] = dot(low_ref[...], w_ref[:, part], NN)
        stores.append(
            pltpu.make_async_copy(mix_ref.at[:, part], mix_any.at[:, part], out_sem.at[1 + n])
        )
        stores[-1].start()
    ext_ref[:RIM] = mix_ref[:RIM, :features] * mix_ref[:RIM, 2 * features :]

    @pl.loop(0, rows // STRIP)
    def _(i):
        at = pl.ds(pl.multiple_of(i * STRIP + RIM, RIM), STRIP)
        ext_ref[at] = mix_ref[at, :features] * mix_ref[at, 2 * features :]

    @pl.loop(0, rows // STRIP)
    def _(i):
        at = pl.ds(pl.multiple_of(i * STRIP, STRIP), STRIP)
        inner = pl.ds(pl.multiple_of(i * STRIP + RIM, RIM), STRIP)
        window = ext_ref[pl.ds(pl.multiple_of(i * STRIP, STRIP), STRIP + RIM)]
        skip = RIM - (KERNEL - 1)
        conv = 0.0
        for k in range(KERNEL):
            same = same_ref[at, k : k + 1] > 0.5
            conv += jnp.where(same, window[skip + k : skip + k + STRIP], 0.0) * taps[k]
        gated_ref[at] = (mix_ref[inner, features : 2 * features] * conv).astype(BF16)

    stores.append(pltpu.make_async_copy(gated_ref, gated_any, out_sem.at[4]))
    stores[-1].start()
    res_ref[...] = dot(gated_ref[...], wo_ref[:, :features], NN)

    @pl.loop(0, rows // STRIP)
    def _(i):
        at = pl.ds(pl.multiple_of(i * STRIP, STRIP), STRIP)
        residual = x_ref[at].astype(F32) + res_ref[at]
        res_ref[at] = residual
        second_ref[at] = normed(residual, gain_two)

    for store in stores:
        store.wait()


def mix_front(place, bits, weight_in, gathered, x, before, same):
    rows, features = x.shape
    anywhere = pl.BlockSpec(memory_space=pl.ANY)
    outs = [
        jax.ShapeDtypeStruct((rows + RIM, 3 * features), F32),
        jax.ShapeDtypeStruct((rows + RIM, features), BF16),
        jax.ShapeDtypeStruct((rows, features), BF16),
        jax.ShapeDtypeStruct((8, features), F32),
        jax.ShapeDtypeStruct((rows, features), F32),
        jax.ShapeDtypeStruct((rows, features), BF16),
    ]
    return pl.pallas_call(
        functools.partial(mix_front_kernel, bits),
        grid_spec=pltpu.PrefetchScalarGridSpec(
            num_scalar_prefetch=1,
            grid=(1,),
            in_specs=[anywhere] * 3 + [once(x), once(before), once(same)],
            out_specs=[anywhere] * 3 + [once(s) for s in outs[3:]],
            scratch_shapes=[
                pltpu.VMEM((features, 3 * features), BF16),
                pltpu.VMEM((features, features + LANES), BF16),
                pltpu.VMEM((rows + RIM, 3 * features), F32),
                pltpu.VMEM((rows + RIM, features), BF16),
                pltpu.VMEM((rows, features), BF16),
                pltpu.VMEM((rows + RIM, features), F32),
                pltpu.SemaphoreType.DMA((1 << len(bits),)),
                pltpu.SemaphoreType.DMA((3,)),
                pltpu.SemaphoreType.DMA((5,)),
            ],
        ),
        out_shape=outs,
        compiler_params=pltpu.CompilerParams(vmem_limit_bytes=VMEM_LIMIT),
        cost_estimate=LONG,
        name="mix_front",
    )(place, weight_in, *gathered, x, before, same)


def mix_back_kernel(bits, place_ref, near_ref, beside_ref, across_ref, cot_ref, res_ref, mix_ref,
                    c0, c1, vec_ref, same_ref,
                    rg_ref, rlow_ref, cl_ref, pg_ref, rim_ref, sums_ref,
                    ext_ref, gg_ref, d0_ref, d1_ref, d2_ref, w_ref, sems):
    rows, features = res_ref.shape
    wait = assemble(place_ref[0], bits, [(c0, 0), (c1, 0)], features, w_ref, 0, sems)
    sums_ref[...] = jnp.zeros_like(sums_ref)
    gain = vec_ref[1:2]
    taps = [vec_ref[2 + k : 3 + k] for k in range(KERNEL)]

    @pl.loop(0, rows // STRIP)
    def _(i):
        at = pl.ds(pl.multiple_of(i * STRIP, STRIP), STRIP)
        second = near_ref[at].astype(F32) + beside_ref[at].astype(F32) + across_ref[at].astype(F32)
        residual = res_ref[at]
        inverse = lax.rsqrt(jnp.mean(residual * residual, axis=-1, keepdims=True) + epsilon)
        unit = residual * inverse
        weighted = second * gain
        mean = jnp.mean(weighted * unit, axis=-1, keepdims=True)
        grad = cot_ref[at].astype(F32) + inverse * (weighted - unit * mean)
        rg_ref[at] = grad
        rlow_ref[at] = grad.astype(BF16)
        sums_ref[0] += fold(second * unit)

    wait()
    gg_ref[...] = dot(rlow_ref[...], w_ref[...], NT)
    ext_ref[:RIM] = mix_ref[:RIM, :features] * mix_ref[:RIM, 2 * features :]

    @pl.loop(0, rows // STRIP)
    def _(i):
        at = pl.ds(pl.multiple_of(i * STRIP + RIM, RIM), STRIP)
        ext_ref[at] = mix_ref[at, :features] * mix_ref[at, 2 * features :]

    zeros = jnp.zeros((RIM, features), F32)
    for d_ref in (d0_ref, d1_ref, d2_ref):
        d_ref[:RIM] = zeros
        d_ref[rows + RIM :] = zeros

    @pl.loop(0, rows // STRIP)
    def _(i):
        at = pl.ds(pl.multiple_of(i * STRIP, STRIP), STRIP)
        inner = pl.ds(pl.multiple_of(i * STRIP + RIM, RIM), STRIP)
        window = ext_ref[pl.ds(pl.multiple_of(i * STRIP, STRIP), STRIP + RIM)]
        skip = RIM - (KERNEL - 1)
        same = [same_ref[at, k : k + 1] > 0.5 for k in range(KERNEL)]
        past = [
            jnp.where(same[k], window[skip + k : skip + k + STRIP], 0.0) for k in range(KERNEL)
        ]
        conv = past[0] * taps[0] + past[1] * taps[1] + past[2] * taps[2]
        gated_grad = gg_ref[at]
        cl_ref[at] = (gated_grad * conv).astype(BF16)
        conv_grad = gated_grad * mix_ref[inner, features : 2 * features]
        for k, d_ref in enumerate((d0_ref, d1_ref, d2_ref)):
            sums_ref[1 + k] += fold(conv_grad * past[k])
            d_ref[inner] = jnp.where(same[k], conv_grad * taps[k], 0.0)

    rim_ref[...] = d0_ref[2 : 2 + RIM] + d1_ref[1 : 1 + RIM]

    @pl.loop(0, rows // STRIP)
    def _(i):
        at = pl.ds(pl.multiple_of(i * STRIP, STRIP), STRIP)
        window = pl.ds(pl.multiple_of(i * STRIP + RIM, RIM), STRIP + RIM)
        inner = pl.ds(pl.multiple_of(i * STRIP + RIM, RIM), STRIP)
        pg_ref[at] = (
            d2_ref[inner] + d1_ref[window][1 : 1 + STRIP] + d0_ref[window][2 : 2 + STRIP]
        )


def mix_outer_kernel(bits, place_ref, gated_ref, rlow_ref, low_ref, cl_ref, sums_ref,
                     out_kept, out_sent, acc_ref):
    place = place_ref[0]
    features = acc_ref.shape[0]
    acc_ref[...] = dot(gated_ref[...], rlow_ref[...], TN)
    pack_rows(place, bits, acc_ref, out_kept, out_sent, 0)
    totals = jnp.sum(sums_ref[...], axis=1)
    totals = jnp.concatenate([totals, jnp.zeros_like(totals)], 0)[:8].astype(BF16)
    units = lax.broadcasted_iota(jnp.int32, (8, LANES), 0) == lax.broadcasted_iota(
        jnp.int32, (8, LANES), 1
    )
    acc_ref[:, :LANES] = dot(totals, jnp.where(units, 1.0, 0.0).astype(BF16), TN)
    pack_rows(place, bits, acc_ref.at[:, :LANES], out_kept, out_sent, features)
    acc_ref[...] = dot(low_ref[RIM:], cl_ref[...], TN)
    pack_rows(place, bits, acc_ref, out_kept, out_sent, features + LANES)


def once(array):
    return pl.BlockSpec(array.shape, lambda *_: (0,) * array.ndim, pipeline_mode=pl.Buffered(1))


def mix_back(place, bits, near, beside, across, cot, res, mix, gathered, vec, same):
    rows, features = res.shape
    shapes = [
        jax.ShapeDtypeStruct((rows, features), F32),
        jax.ShapeDtypeStruct((rows, features), BF16),
        jax.ShapeDtypeStruct((rows, features), BF16),
        jax.ShapeDtypeStruct((rows, features), F32),
        jax.ShapeDtypeStruct((RIM, features), F32),
        jax.ShapeDtypeStruct((1 + KERNEL, 8, features), F32),
    ]
    ins = [near, beside, across, cot, res, mix]
    anywhere = pl.BlockSpec(memory_space=pl.ANY)
    return pl.pallas_call(
        functools.partial(mix_back_kernel, bits),
        grid_spec=pltpu.PrefetchScalarGridSpec(
            num_scalar_prefetch=1,
            grid=(1,),
            in_specs=[once(a) for a in ins] + [anywhere] * 2 + [once(vec), once(same)],
            out_specs=[once(s) for s in shapes],
            scratch_shapes=[
                pltpu.VMEM((rows + RIM, features), F32),
                pltpu.VMEM((rows, features), F32),
                *[pltpu.VMEM((rows + 2 * RIM, features), F32)] * 3,
                pltpu.VMEM((features, features), BF16),
                pltpu.SemaphoreType.DMA((1 << len(bits),)),
            ],
        ),
        out_shape=shapes,
        compiler_params=pltpu.CompilerParams(vmem_limit_bytes=VMEM_LIMIT),
        cost_estimate=LONG,
        name="mix_back",
    )(place, *ins, *gathered, vec, same)


def mix_outer(place, bits, gated, rlow, low, cl, sums):
    features = gated.shape[1]
    parts = 1 << len(bits)
    ins = [gated, rlow, low, cl, sums]
    shapes = [
        jax.ShapeDtypeStruct((parts // 2, features // parts, 2 * features + LANES), BF16)
    ] * 2
    return pl.pallas_call(
        functools.partial(mix_outer_kernel, bits),
        grid_spec=pltpu.PrefetchScalarGridSpec(
            num_scalar_prefetch=1,
            grid=(1,),
            in_specs=[once(a) for a in ins],
            out_specs=[once(s) for s in shapes],
            scratch_shapes=[pltpu.VMEM((features, features), F32)],
        ),
        out_shape=shapes,
        compiler_params=pltpu.CompilerParams(vmem_limit_bytes=VMEM_LIMIT),
        cost_estimate=LONG,
        name="mix_outer",
    )(place, *ins)


def mix_grads_kernel(bits, place_ref, pg_ref, rim_ref, mix_ref, low_ref,
                     first_ref, last_ref, kept_ref, sent_ref, acc_ref):
    place = place_ref[0]
    rows, features = pg_ref.shape

    @pl.loop(0, rows // STRIP)
    def _(i):
        at = pl.ds(pl.multiple_of(i * STRIP, STRIP), STRIP)
        inner = pl.ds(pl.multiple_of(i * STRIP + RIM, RIM), STRIP)
        grad = pg_ref[at]
        first_ref[at] = (grad * mix_ref[inner, 2 * features :]).astype(BF16)
        last_ref[at] = (grad * mix_ref[inner, :features]).astype(BF16)

    grad = pg_ref[rows - RIM :] + rim_ref[...]
    first_ref[rows - RIM :] = (grad * mix_ref[rows:, 2 * features :]).astype(BF16)
    last_ref[rows - RIM :] = (grad * mix_ref[rows:, :features]).astype(BF16)
    for n, grad_ref in enumerate((first_ref, last_ref)):
        acc_ref[...] = dot(low_ref[RIM:], grad_ref[...], TN)
        pack_rows(place, bits, acc_ref, kept_ref, sent_ref, n * features)


def mix_grads(place, bits, pg, rim, mix, low):
    rows, features = pg.shape
    parts = 1 << len(bits)
    tall = features // parts

    def whole(array):
        return pl.BlockSpec(
            array.shape, lambda i, _: (0,) * array.ndim, pipeline_mode=pl.Buffered(1)
        )

    shapes = [jax.ShapeDtypeStruct((rows, features), BF16)] * 2
    shapes += [jax.ShapeDtypeStruct((parts // 2, tall, 2 * features), BF16)] * 2
    return pl.pallas_call(
        functools.partial(mix_grads_kernel, bits),
        grid_spec=pltpu.PrefetchScalarGridSpec(
            num_scalar_prefetch=1,
            grid=(1,),
            in_specs=[whole(a) for a in (pg, rim, mix, low)],
            out_specs=[whole(s) for s in shapes],
            scratch_shapes=[pltpu.VMEM((features, features), F32)],
        ),
        out_shape=shapes,
        compiler_params=pltpu.CompilerParams(vmem_limit_bytes=VMEM_LIMIT),
        cost_estimate=LONG,
        name="mix_grads",
    )(place, pg, rim, mix, low)


def input_back_kernel(first_ref, mid_ref, last_ref, w_ref, rg_ref, x_ref, vec_ref, out_ref, fg_ref):
    rows, features = rg_ref.shape
    fg_ref[...] = dot(first_ref[...], w_ref[:, :features], NT)
    fg_ref[...] += dot(mid_ref[...], w_ref[:, features : 2 * features], NT)
    fg_ref[...] += dot(last_ref[...], w_ref[:, 2 * features :], NT)

    @pl.loop(0, rows // STRIP)
    def _(i):
        at = pl.ds(pl.multiple_of(i * STRIP, STRIP), STRIP)
        values = x_ref[at].astype(F32)
        inverse = lax.rsqrt(jnp.mean(values * values, axis=-1, keepdims=True) + epsilon)
        unit = values * inverse
        weighted = fg_ref[at] * vec_ref[0:1]
        mean = jnp.mean(weighted * unit, axis=-1, keepdims=True)
        out_ref[at] = rg_ref[at] + inverse * (weighted - unit * mean)


def input_back(first, mid, last, weight_in, rg, x, vec):
    rows, features = rg.shape
    ins = [first, mid, last, weight_in, rg, x, vec]
    return pl.pallas_call(
        input_back_kernel,
        grid=(1,),
        in_specs=[once(a) for a in ins],
        out_specs=once(rg),
        out_shape=jax.ShapeDtypeStruct((rows, features), F32),
        scratch_shapes=[pltpu.VMEM((rows, features), F32)],
        compiler_params=pltpu.CompilerParams(vmem_limit_bytes=VMEM_LIMIT),
        cost_estimate=LONG,
        name="input_back",
    )(*ins)


def gather_mp(own):
    size = lax.axis_size("mp")
    blocks = [own] + [None] * (size - 1)
    for bit in reversed(range(bits_of("mp"))):
        for r in [r for r in range(size) if blocks[r] is not None]:
            blocks[r ^ (1 << bit)] = swap(blocks[r], "mp", bit)
    return blocks


class Sum:
    def __init__(self, order, kept, sent, bits):
        self.order, self.kept, self.sent, self.bits, self.step = order, kept, sent, bits, 0

    def send(self):
        steps = len(self.bits)
        bit = self.bits[self.step] if self.step < steps else self.bits[2 * steps - 1 - self.step]
        self.got = swap(self.sent, "dp", bit)

    def add(self):
        self.step += 1
        steps = len(self.bits)
        got = self.order(self.got)
        if self.step < steps:
            self.kept, self.sent = halve(self.kept, got)
        elif self.step == steps:
            (own,) = halve(self.kept, got, 1)
            for bit in range(HALVINGS, bits_of("dp")):
                (own,) = halve(own, swap(own, "dp", bit), 1)
            self.pieces = [own]
            self.sent = own
        else:
            self.pieces.append(got)
            if self.step == 2 * steps:
                return
            self.sent = lay(self.pieces)
        self.order.mark(self.sent)


class Scatter:
    def __init__(self, order, kept, sent, bits):
        self.order, self.kept, self.sent, self.bits, self.step = order, kept, sent, bits, 0

    def send(self):
        inner = bits_of("mp")
        bit = self.bits[self.step]
        axis, bit = ("mp", bit) if bit < inner else ("dp", bit - inner)
        self.got = swap(self.sent, axis, bit)

    def add(self):
        self.step += 1
        got = self.order(self.got)
        if self.step < len(self.bits):
            self.kept, self.sent = halve(self.kept, got)
            self.order.mark(self.sent)
        else:
            (total,) = halve(self.kept, got, 1, F32)
            self.total = self.order.mark(total)[0]

    def finish(self):
        while self.step < len(self.bits):
            self.add()
            if self.step < len(self.bits):
                self.send()


def per_device(
    block_in,
    segment_ids,
    first_gain,
    in_proj,
    conv_kernel,
    out_proj,
    second_gain,
    gate_proj,
    up_proj,
    down_proj,
    out_grad,
):
    rows = block_in.shape[1]
    features = block_in.shape[2]
    x = block_in.reshape(rows, features)
    own_ids = segment_ids.reshape(rows)
    cotangent = out_grad.reshape(rows, features)
    inner = lax.axis_size("mp")
    place = (lax.axis_index("dp") % PARTS).reshape(1).astype(jnp.int32)
    place_all = (lax.axis_index("dp") * inner + lax.axis_index("mp")).reshape(1).astype(jnp.int32)
    order = Order()

    def swap_all(block, bit):
        outer = bit - bits_of("mp")
        return swap(block, "mp", bit) if outer < 0 else swap(block, "dp", outer)

    before = shift(x[rows - RIM :], "mp", 1)
    ids_before = shift(own_ids[rows - RIM :].astype(F32), "mp", 1).astype(jnp.int32)
    ids_before = jnp.where(lax.axis_index("mp") == 0, -1, ids_before)
    ids = jnp.concatenate([ids_before, own_ids], 0)
    skip = RIM - (KERNEL - 1)
    same = [(ids[skip + k : skip + k + rows] == own_ids)[:, None] for k in range(KERNEL)]
    same = jnp.pad(jnp.concatenate(same, 1).astype(F32), ((0, 0), (0, LANES - KERNEL)))

    weight_in = lax.all_gather(in_proj, ("dp", "mp"), axis=0, tiled=True)
    small = jnp.concatenate(
        [first_gain[:, None], second_gain[:, None], conv_kernel], 1
    )
    small = jnp.pad(small, ((0, 0), (0, LANES - small.shape[1])))
    weight_bits = list(reversed(range(bits_of("mp") + bits_of("dp"))))
    gathered = [jnp.concatenate([out_proj, small], 1)[None]]
    for bit in weight_bits:
        held = jnp.concatenate(gathered, 0)
        gathered = [held, swap_all(held, bit)]
    group_grad = gather_mp(cotangent)
    weight_in = after(weight_in, gathered, before, group_grad)

    mixer_all, low_all, gated_low, vec, residual, second_low = mix_front(
        place_all, weight_bits, weight_in, gathered, x, before, same
    )

    hidden_units = gate_proj.shape[1]
    bits_all = list(range(bits_of("mp") + bits_of("dp")))
    beside = swap(second_low, "mp", 0)
    across = swap(second_low, "mp", 1)
    *near_acts, og, ou, od = near_feed(
        [second_low, beside], group_grad[:2], gate_proj, up_proj, down_proj
    )
    near_grads = [og, ou, od]
    order.mark(near_grads[0])
    across = order(across)
    far = (
        place, [across, swap(across, "mp", 0)], group_grad[2:], gate_proj, up_proj, down_proj,
        near_grads,
    )
    wide = hidden_units // 3
    assert wide % LANES == 0
    far_acts, sums = (), []
    for n in range(3):
        far_acts, [pair] = far_feed(*far, far_acts, [(0, 1, 2)], wide, n)
        order.mark(pair[1])
        sums.append(Sum(order, *pair, (0, 1, 2)))
        if n == 0:
            sums[0].send()
    one, two, three = sums

    def back(acts, n):
        gate_low, up_low = order((acts[2 + n], acts[4 + n]))
        grad = dot(gate_low, gate_proj, NT) + dot(up_low, up_proj, NT)
        return order.mark(grad.astype(BF16))

    def onward(acts, n):
        return order.mark(dot(order(acts[n]), down_proj, NN).astype(BF16))

    def both(kept, got):
        (total,) = halve(kept[None], order(got)[None], 1)
        return order.mark(total)[0]

    got = swap(back(far_acts, 1), "mp", 0)
    one.add()
    one.send()
    two.send()
    back_across = swap(both(back(far_acts, 0), got), "mp", 1)
    back_beside = swap(back(near_acts, 1), "mp", 0)
    one.add()
    one.send()
    back_near = back(near_acts, 0)
    two.add()
    two.send()
    three.send()
    one.add()
    one.send()

    back_across, back_beside = order((back_across, back_beside))
    residual_grad, residual_low, closing_low, product_part, rim_out, totals = mix_back(
        place_all, weight_bits, back_near, back_beside, back_across, cotangent, residual,
        mixer_all, gathered, vec, same,
    )
    order.mark(rim_out)
    rim_back = shift(rim_out, "mp", -1)
    one.add()
    one.send()
    two.add()
    two.send()
    halves = mix_outer(
        place_all, bits_all, gated_low, order(residual_low), low_all, closing_low, totals
    )
    order.mark(halves[1])
    outer = Scatter(order, *halves, bits_all)
    outer.send()
    three.add()
    three.send()
    outer.add()
    outer.send()
    one.add()
    one.send()
    first_part, last_part, *halves = mix_grads(
        place_all, bits_all, product_part, order(rim_back), mixer_all, low_all
    )
    order.mark(halves[1])
    rest = Scatter(order, *halves, bits_all)
    rest.send()
    two.add()
    two.send()
    rest.add()
    rest.send()
    three.add()
    three.send()
    input_grad = input_back(
        order(first_part), closing_low, last_part, weight_in, residual_grad, x, vec,
    )
    order.mark(input_grad)
    input_grad = input_grad.reshape(1, rows, features)
    two.add()
    two.send()
    three.add()
    three.send()
    outer.add()
    outer.send()
    one.add()
    got = swap(onward(far_acts, 1), "mp", 0)
    two.add()
    two.send()
    three.add()
    three.send()
    on_far = both(onward(far_acts, 0), got)
    rest.add()
    rest.send()
    outer.add()
    outer.send()
    three.add()
    three.send()
    on_across = swap(order(on_far), "mp", 1)
    on_beside = swap(onward(near_acts, 1), "mp", 0)
    on_near = onward(near_acts, 0)
    rest.add()
    rest.send()
    outer.add()
    outer.send()
    done = unpack(place, one.pieces, (), one.bits, wide, 0, features, hidden_units)
    order.mark(done[0])
    rest.add()
    rest.send()
    outer.finish()
    two.add()
    done = unpack(place, two.pieces, done, two.bits, wide, 1, features, hidden_units)
    order.mark(done[0])
    rest.finish()
    branch = on_near.astype(F32) + on_beside.astype(F32) + order(on_across).astype(F32)
    layer_out = order.mark((residual + branch).astype(BF16)).reshape(1, rows, features)
    grad_out = outer.total[:, :features]
    grad_second = outer.total[:, features]
    grad_conv = outer.total[:, features + 1 : features + 1 + KERNEL]
    ends = rest.total
    grad_in = jnp.concatenate(
        [ends[:, :features], outer.total[:, features + LANES :], ends[:, features:]], 1
    )
    grad_first = jnp.sum(grad_in * in_proj.astype(F32), axis=1) / first_gain.astype(F32)
    three.add()
    grad_gate, grad_up, grad_down = unpack(
        place, three.pieces, done, three.bits, wide, 2, features, hidden_units
    )
    return (
        layer_out,
        input_grad,
        grad_first,
        grad_in,
        grad_conv,
        grad_out,
        grad_second,
        grad_gate,
        grad_up,
        grad_down,
    )


def solution(mesh):
    in_specs = (
        P("dp", "mp", None),
        P("dp", "mp"),
        P(("dp", "mp")),
        P(("dp", "mp"), None),
        P(("dp", "mp"), None),
        P(("dp", "mp"), None),
        P(("dp", "mp")),
        P(None, "mp"),
        P(None, "mp"),
        P("mp", None),
        P("dp", "mp", None),
    )
    out_specs = (
        P("dp", "mp", None),
        P("dp", "mp", None),
        P(("dp", "mp")),
        P(("dp", "mp"), None),
        P(("dp", "mp"), None),
        P(("dp", "mp"), None),
        P(("dp", "mp")),
        P(None, "mp"),
        P(None, "mp"),
        P("mp", None),
    )
    return jax.shard_map(
        per_device, mesh=mesh, in_specs=in_specs, out_specs=out_specs, check_vma=False
    )
```

time: 479 us -> 434 us (0.906)
  Pallas kernels: 71 us -> 193 us
  waiting for transfers between devices: 225 us -> 119 us
  other arithmetic: 41.8 us -> 7.42 us
  matrix products: 48.3 us -> 31.4 us
  local copies, waits for them, and re-layouts: 28.6 us -> 12.3 us
  starting transfers between devices: 40.1 us -> 49 us
    pallas_call x0 -> x32, Pallas kernels: none -> 121 us  [the longest x21 50.4 us: halve(): pl.pallas_call(halve_kernel, grid=(1,), in_specs=[whole(kept), whole(got)...]
    all_gather x1, waiting for transfers between devices: 73.1 us -> 12.5 us  [per_device(): weight_in = lax.all_gather(in_proj, ('dp', 'mp'), axis=0, tiled=True)]
    ppermute x40 -> x45, waiting for transfers between devices: 152 us -> 105 us  [swap(): return lax.ppermute(block, axis, [(i, i ^ 1 << bit) for i in range(size)])]
    convert_element_type x27 -> x2, other arithmetic: 23.2 us -> 3.34 us  [the longest x1 3.27 us: per_device(): (residual + branch).astype(BF16)]
    dot_general x2 -> x0, matrix products: 9.31 us -> none  [the longest x1 5.97 us: per_device(): mixer_all = jnp.dot(low_all, weight_in, preferred_element_type=F32)]
    concatenate x10 -> x5, other arithmetic: 9.53 us -> 0.29 us  [the longest x3 0.14 us: per_device(): held = jnp.concatenate(gathered, 0)]
    ppermute x40 -> x45, starting transfers between devices: 34.8 us -> 43.3 us  [swap(): return lax.ppermute(block, axis, [(i, i ^ 1 << bit) for i in range(size)])]
    dot_general x10 -> x12, matrix products: 39 us -> 31.4 us  [dot(): return lax.dot_general(left, right, dims, preferred_element_type=F32)]
  transfers between devices with their start and end apart: 44 -> 49, of which waited for: 19 -> 15; matrix products, arithmetic and copies ran while one was open for 21% -> 10% of each run, Pallas kernels for 13% -> 38%
where the time goes in v4:
time: 434 us; the launch traced here: 426 us
  Pallas kernels  193 us (44%)
  waiting for transfers between devices  119 us (27%)
  starting transfers between devices  49 us (11%)
  matrix products  31.4 us (7%)
  between operations  14.7 us (3%)
  local copies, waits for them, and re-layouts  12.3 us (3%)
  other arithmetic  7.42 us (2%)
    ppermute x45, waiting for transfers between devices, swap(): return lax.ppermute(block, axis, [(i, i ^ 1 << bit) for i in range(size)])  105 us
    pallas_call x21, Pallas kernels, halve(): pl.pallas_call(halve_kernel, grid=(1,), in_specs=[whole(kept), whole(got)...  50.4 us
    ppermute x45, starting transfers between devices, swap(): return lax.ppermute(block, axis, [(i, i ^ 1 << bit) for i in range(size)])  43.3 us
    pallas_call x3, Pallas kernels, far_feed(): pl.pallas_call(functools.partial(far_kernel, orders), grid_spec=pltpu.Pre...  36.2 us
    dot_general x12, matrix products, dot(): return lax.dot_general(left, right, dims, preferred_element_type=F32)  31.4 us
    pallas_call x1, Pallas kernels, near_feed(): pl.pallas_call(near_kernel, grid=(pl.cdiv(hidden, wide),), in_specs=[whol...  23 us
    pallas_call x1, Pallas kernels, mix_back(): pl.pallas_call(functools.partial(mix_back_kernel, bits), grid_spec=pltpu....  14.3 us
    pallas_call x1, Pallas kernels, mix_front(): pl.pallas_call(functools.partial(mix_front_kernel, bits), grid_spec=pltpu...  13.8 us
  transfers between devices with their start and end apart: 49, of which 15 were waited for; matrix products, arithmetic and copies ran while one was open for 10% of the time, Pallas kernels for 38%

profile of v4, /device:TPU:0, one launch (start us, length us, event | category | flops | bytes accessed | tf_op | source)
XLA Modules:
  0.0 426.0 jit_solution(9522898990911302016)
XLA Ops:
  9.6 4.0 collective-permute-start
  13.6 3.9 collective-permute-done
  18.3 4.5 %collective-permute-done.1 = bf16[2,32,1152]{2,1,0:T(8,128)(2,1)S(1)} collective-permute-done((bf16[2,32,1152]{2,1,0:T(8,128)(2,1)S(1)}, bf16[2,32,1152]{2,1,0:T(8,128)(2,1)S(1)}, u32[]{:S(2)}, u32[]{:S(2)}) %collective-permute-start.1) | collective-permute-done | bytes 147488 | tf_op jit(solution)/shard_map/ppermute | solution.py:27
  26.1 4.6 %collective-permute-done.2 = bf16[4,32,1152]{2,1,0:T(8,128)(2,1)S(1)} collective-permute-done((bf16[4,32,1152]{2,1,0:T(8,128)(2,1)S(1)}, bf16[4,32,1152]{2,1,0:T(8,128)(2,1)S(1)}, u32[]{:S(2)}, u32[]{:S(2)}) %collective-permute-start.2) | collective-permute-done | bytes 294944 | tf_op jit(solution)/shard_map/ppermute | solution.py:27
  32.5 32.7 %collective-permute-done.3 = bf16[8,32,1152]{2,1,0:T(8,128)(2,1)S(1)} collective-permute-done((bf16[8,32,1152]{2,1,0:T(8,128)(2,1)S(1)}, bf16[8,32,1152]{2,1,0:T(8,128)(2,1)S(1)}, u32[]{:S(2)}, u32[]{:S(2)}) %collective-permute-start.3) | collective-permute-done | bytes 589856 | tf_op jit(solution)/shard_map/ppermute | solution.py:27
  74.0 12.5 %all-gather.2.cloned.1.call-done.in_any.w_ref = bf16[1024,3072]{1,0:T(8,128)(2,1)} async-done(((bf16[32,3072]{1,0:T(8,128)(2,1)}), bf16[1024,3072]{1,0:T(8,128)(2,1)}) %all-gather.2.cloned.1.call-update) | async-done | bytes 6291472 | tf_op jit(solution)/shard_map/all_gather | solution.py:804
  86.4 13.8 %mix_front.1 = (f32[520,3072]{1,0:T(8,128)}, bf16[520,1024]{1,0:T(8,128)(2,1)}, bf16[512,1024]{1,0:T(8,128)(2,1)}, f32[8,1024]{1,0:T(8,128)}, f32[512,1024]{1,0:T(8,128)}, /*index=5*/bf16[512,1024]{1,0:T(8,128)(2,1)}) custom-call(s32[1]{0:T(128)} %bitcast.place_ref, bf16[1024,3072]{1,0:T(8,128)(2,1)} %all-gather.2.cloned.1.call-done.in_any.w_ref, ...), custom_call_target="tpu_custom_call" | custom-call | flops 99999997952 | tf_op jit(solution)/shard_map/mix_front/pallas_call | solution.py:450
  104.2 23.0 %near_feed.1 = (bf16[512,1152]{1,0:T(8,128)(2,1)}, bf16[512,1152]{1,0:T(8,128)(2,1)}, bf16[512,1152]{1,0:T(8,128)(2,1)}, bf16[512,1152]{1,0:T(8,128)(2,1)}, bf16...) custom-call(bf16[512,1024]{1,0:T(8,128)(2,1)} %get-tuple-element.151, ...), custom_call_target="tpu_custom_call" | custom-call | flops 99999997952 | tf_op jit(solution)/shard_map/near_feed/pallas_call | solution.py:124
  130.9 11.8 %far_feed.3 = (bf16[512,1152]{1,0:T(8,128)(2,1)}, bf16[512,1152]{1,0:T(8,128)(2,1)}, bf16[512,1152]{1,0:T(8,128)(2,1)}, bf16[512,1152]{1,0:T(8,128)(2,1)}, bf16[...) custom-call(s32[1]{0:T(128)} %bitcast.9.place_ref, ...), custom_call_target="tpu_custom_call" | custom-call | flops 99999997952 | tf_op jit(solution)/shard_map/far_feed/pallas_call | solution.py:186
  144.2 12.2 %far_feed.4 = (bf16[512,1152]{1,0:T(8,128)(2,1)}, bf16[512,1152]{1,0:T(8,128)(2,1)}, bf16[512,1152]{1,0:T(8,128)(2,1)}, bf16[512,1152]{1,0:T(8,128)(2,1)}, bf16[...) custom-call(s32[1]{0:T(128)} %bitcast.9.place_ref, ...), custom_call_target="tpu_custom_call", output_to_operand_aliasing={{0}: (11, {}), {1}: (12, {}), {2}: (13, {}), {3}: (14, {}),... | custom-call | flops 99999997952 | tf_op jit(solution)/shard_map/far_feed/pallas_call | solution.py:186
  156.4 12.2 %far_feed.5 = (bf16[512,1152]{1,0:T(8,128)(2,1)}, bf16[512,1152]{1,0:T(8,128)(2,1)}, bf16[512,1152]{1,0:T(8,128)(2,1)}, bf16[512,1152]{1,0:T(8,128)(2,1)}, bf16[...) custom-call(s32[1]{0:T(128)} %bitcast.9.place_ref, ...), custom_call_target="tpu_custom_call", output_to_operand_aliasing={{0}: (11, {}), {1}: (12, {}), {2}: (13, {}), {3}: (14, {}),... | custom-call | flops 99999997952 | tf_op jit(solution)/shard_map/far_feed/pallas_call | solution.py:186
  169.1 3.0 fusion.5
  179.7 3.0 fusion.6
  188.0 3.4 fusion.7
  198.6 3.0 fusion.8
  204.1 17.9 %collective-permute-done.20.got_ref = bf16[4,1152,128]{2,1,0:T(8,128)(2,1)} collective-permute-done((bf16[4,1152,128]{2,1,0:T(8,128)(2,1)}, bf16[4,1152,128]{2,1,0:T(8,128)(2,1)}, u32[]{:S(2)}, u32[]{:S(2)}) %collective-permute-start.20) | collective-permute-done | bytes 1179680 | tf_op jit(solution)/shard_map/ppermute | solution.py:27
  229.7 14.3 %mix_back.1 = (f32[512,1024]{1,0:T(8,128)}, bf16[512,1024]{1,0:T(8,128)(2,1)}, bf16[512,1024]{1,0:T(8,128)(2,1)}, f32[512,1024]{1,0:T(8,128)}, f32[8,1024]{1,0:T(8,128)}, /*index=5*/f32[4,8,1024]{2,1,0:T(8,128)}) custom-call(s32[1]{0:T(128)} %bitcast.place_ref, bf16[512,1024]{1,0:T(8,128)(2,1)} %add_convert_fusion.1.near_ref, ...), custom_call_target="tpu_custom_call" | custom-call | flops 99999997952 | tf_op jit(solution)/shard_map/mix_back/pallas_call | solution.py:577
  253.0 8.4 %mix_outer.1 = (bf16[16,32,2176]{2,1,0:T(8,128)(2,1)}, bf16[16,32,2176]{2,1,0:T(8,128)(2,1)}) custom-call(s32[1]{0:T(128)} %bitcast.place_ref, bf16[512,1024]{1,0:T(8,128)(2,1)} %get-tuple-element.172.gated_ref, bf16[512,1024]{1,0:T(8,128)(2,1)} %get-tuple-element.213.rlow_ref, bf16[520,1024]{1,0:T(8,128)(2,1)} %get-tuple-element.214.low_ref, ...), custom_call_target="tpu_custom_call" | custom-call | flops 99999997952 | tf_op jit(solution)/shard_map/mix_outer/pallas_call | solution.py:606
  267.6 3.9 halve.28
  276.2 10.0 %mix_grads.1 = (bf16[512,1024]{1,0:T(8,128)(2,1)}, bf16[512,1024]{1,0:T(8,128)(2,1)}, bf16[16,32,2048]{2,1,0:T(8,128)(2,1)}, bf16[16,32,2048]{2,1,0:T(8,128)(2,1)}) custom-call(s32[1]{0:T(128)} %bitcast.place_ref, f32[512,1024]{1,0:T(8,128)} %get-tuple-element.221.pg_ref, f32[8,1024]{1,0:T(8,128)} %collective-permute-done.24.rim_ref, ...), custom_call_target="tpu_custom_call" | custom-call | flops 99999997952 | tf_op jit(solution)/shard_map/mix_grads/pallas_call | solution.py:655
  292.0 3.8 halve.30
  301.3 11.3 %input_back.1 = f32[512,1024]{1,0:T(8,128)} custom-call(bf16[512,1024]{1,0:T(8,128)(2,1)} %get-tuple-element.237.first_ref, bf16[512,1024]{1,0:T(8,128)(2,1)} %get-tuple-element.215.cl_ref.mid_ref, bf16[512,1024]{1,0:T(8,128)(2,1)} %get-tuple-element.238.last_ref, bf16[1024,3072]{1,0:T(8,128)(2,1)} %all-gather.2.cloned.1.call-done.in_any.w_ref, ...), custom_call_target="tpu_custom_call" | custom-call | flops 99999997952 | tf_op jit(solution)/shard_map/input_back/pallas_call | solution.py:691
  314.8 3.0 collective-permute-done.29.got_ref
  326.3 4.1 unpack.3
  330.4 6.3 %collective-permute-done.32.refs_2_ = bf16[2,1152,128]{2,1,0:T(8,128)(2,1)} collective-permute-done((bf16[2,1152,128]{2,1,0:T(8,128)(2,1)}, bf16[2,1152,128]{2,1,0:T(8,128)(2,1)}, u32[]{:S(2)}, u32[]{:S(2)}) %collective-permute-start.32) | collective-permute-done | bytes 589856 | tf_op jit(solution)/shard_map/ppermute | solution.py:27
  355.3 3.4 collective-permute-done.34.refs_2_
  366.5 12.9 %collective-permute-done.40.got_ref = bf16[4,32,2048]{2,1,0:T(8,128)(2,1)} collective-permute-done((bf16[4,32,2048]{2,1,0:T(8,128)(2,1)}, bf16[4,32,2048]{2,1,0:T(8,128)(2,1)}, u32[]{:S(2)}, u32[]{:S(2)}) %collective-permute-start.40) | collective-permute-done | bytes 524320 | tf_op jit(solution)/shard_map/ppermute | solution.py:27
  384.6 4.8 %collective-permute-done.41.got_ref = bf16[2,32,2048]{2,1,0:T(8,128)(2,1)S(1)} collective-permute-done((bf16[2,32,2048]{2,1,0:T(8,128)(2,1)}, bf16[2,32,2048]{2,1,0:T(8,128)(2,1)S(1)}, u32[]{:S(2)}, u32[]{:S(2)}) %collective-permute-start.41) | collective-permute-done | bytes 262176 | tf_op jit(solution)/shard_map/ppermute | solution.py:27
  391.8 6.8 %collective-permute-done.46.got_ref = bf16[1,32,2176]{2,1,0:T(8,128)(2,1)S(1)} collective-permute-done((bf16[1,32,2176]{2,1,0:T(8,128)(2,1)}, bf16[1,32,2176]{2,1,0:T(8,128)(2,1)S(1)}, u32[]{:S(2)}, u32[]{:S(2)}) %collective-permute-start.46) | collective-permute-done | bytes 139296 | tf_op jit(solution)/shard_map/ppermute | solution.py:27
  401.0 4.1 unpack.4
  411.6 3.3 add_convert_fusion
  414.9 4.1 unpack.5
  (222 shorter events, 141.3 us)
Async XLA Ops:
  7.2 79.2 %all-gather.2.cloned.1.call-start = ((), (), s32[]{:S(2)}) async-start(), calls=%async_computation | async-start | bytes 6488064 | tf_op jit(solution)/shard_map/all_gather | solution.py:804
  24.6 43.2 %collective-permute-start.7 = (bf16[512,1024]{1,0:T(8,128)(2,1)S(1)}, bf16[512,1024]{1,0:T(8,128)(2,1)}, u32[]{:S(2)}, u32[]{:S(2)}) collective-permute-start(bf16[512,1024]{1,0:T(8,128)(2,1)S(1)} %bitcast.63), channel_id=1, source_target_pairs={{0,2},{1,3},{2,0},{3,1},{4,6},{5,7},{6,4},{7,5},{8,10},{9,11},{10,... | collective-permute-start | bytes 3145736 | tf_op jit(solution)/shard_map/ppermute | solution.py:27
  26.1 47.8 %collective-permute-start.6 = (bf16[512,1024]{1,0:T(8,128)(2,1)S(1)}, bf16[512,1024]{1,0:T(8,128)(2,1)}, u32[]{:S(2)}, u32[]{:S(2)}) collective-permute-start(bf16[512,1024]{1,0:T(8,128)(2,1)S(1)} %bitcast.64), channel_id=1, source_target_pairs={{0,1},{1,0},{2,3},{3,2},{4,5},{5,4},{6,7},{7,6},{8,9},{9,8},{10,11... | collective-permute-start | bytes 3145736 | tf_op jit(solution)/shard_map/ppermute | solution.py:27
  30.8 34.4 %collective-permute-start.3 = (bf16[8,32,1152]{2,1,0:T(8,128)(2,1)S(1)}, bf16[8,32,1152]{2,1,0:T(8,128)(2,1)S(1)}, u32[]{:S(2)}, u32[]{:S(2)}) collective-permute-start(bf16[8,32,1152]{2,1,0:T(8,128)(2,1)S(1)} %pad_maximum_fusion), channel_id=1, source_target_pairs={{0,2},{1,3},{2,0},{3,1},{4,6},{5,7},{6,4},{7,5},{8,10},{9,11},{10,... | collective-permute-start | bytes 1769480 | tf_op jit(solution)/shard_map/ppermute | solution.py:27
  100.5 26.7 %collective-permute-start.11 = (bf16[512,1024]{1,0:T(8,128)(2,1)}, bf16[512,1024]{1,0:T(8,128)(2,1)S(1)}, u32[]{:S(2)}, u32[]{:S(2)}) collective-permute-start(bf16[512,1024]{1,0:T(8,128)(2,1)} %get-tuple-element.151.xa_ref), channel_id=1, source_target_pairs={{0,2},{1,3},{2,0},{3,1},{4,6},{5,7},{6,4},{7,5},{8,10},{9,11},{10,... | collective-permute-start | bytes 3145736 | tf_op jit(solution)/shard_map/ppermute | solution.py:27
  142.7 32.6 %collective-permute-start.14 = (bf16[4,1152,128]{2,1,0:T(8,128)(2,1)}, bf16[4,1152,128]{2,1,0:T(8,128)(2,1)}, u32[]{:S(2)}, u32[]{:S(2)}) collective-permute-start(bf16[4,1152,128]{2,1,0:T(8,128)(2,1)} %get-tuple-element.176), channel_id=1, source_target_pairs={{0,4},{4,0},{8,12},{12,8},{16,20},{20,16},{24,28},{28,24},{1,5},{5... | collective-permute-start | bytes 3538952 | tf_op jit(solution)/shard_map/ppermute | solution.py:27
  168.6 93.2 %collective-permute-start.13 = (bf16[4,1152,128]{2,1,0:T(8,128)(2,1)}, bf16[4,1152,128]{2,1,0:T(8,128)(2,1)}, u32[]{:S(2)}, u32[]{:S(2)}) collective-permute-start(bf16[4,1152,128]{2,1,0:T(8,128)(2,1)} %get-tuple-element.171), channel_id=1, source_target_pairs={{0,4},{4,0},{8,12},{12,8},{16,20},{20,16},{24,28},{28,24},{1,5},{5... | collective-permute-start | bytes 3538952 | tf_op jit(solution)/shard_map/ppermute | solution.py:27
  173.7 48.3 %collective-permute-start.20 = (bf16[4,1152,128]{2,1,0:T(8,128)(2,1)}, bf16[4,1152,128]{2,1,0:T(8,128)(2,1)}, u32[]{:S(2)}, u32[]{:S(2)}) collective-permute-start(bf16[4,1152,128]{2,1,0:T(8,128)(2,1)} %get-tuple-element.199), channel_id=1, source_target_pairs={{0,4},{4,0},{8,12},{12,8},{16,20},{20,16},{24,28},{28,24},{1,5},{5... | collective-permute-start | bytes 3538952 | tf_op jit(solution)/shard_map/ppermute | solution.py:27
  193.9 35.7 %collective-permute-start.18 = (bf16[512,1024]{1,0:T(8,128)(2,1)}, bf16[512,1024]{1,0:T(8,128)(2,1)}, u32[]{:S(2)}, u32[]{:S(2)}) collective-permute-start(bf16[512,1024]{1,0:T(8,128)(2,1)} %add_convert_fusion.2), channel_id=1, source_target_pairs={{0,1},{1,0},{2,3},{3,2},{4,5},{5,4},{6,7},{7,6},{8,9},{9,8},{10,11... | collective-permute-start | bytes 3145736 | tf_op jit(solution)/shard_map/ppermute | solution.py:27
  193.9 35.7 %collective-permute-start.17 = (bf16[512,1024]{1,0:T(8,128)(2,1)}, bf16[512,1024]{1,0:T(8,128)(2,1)}, u32[]{:S(2)}, u32[]{:S(2)}) collective-permute-start(bf16[512,1024]{1,0:T(8,128)(2,1)} %bitcast.12), channel_id=1, source_target_pairs={{0,2},{1,3},{2,0},{3,1},{4,6},{5,7},{6,4},{7,5},{8,10},{9,11},{10,... | collective-permute-start | bytes 3145736 | tf_op jit(solution)/shard_map/ppermute | solution.py:27
  197.4 29.0 %collective-permute-start.19 = (bf16[1,1152,128]{2,1,0:T(8,128)(2,1)}, bf16[1,1152,128]{2,1,0:T(8,128)(2,1)S(1)}, u32[]{:S(2)}, u32[]{:S(2)}) collective-permute-start(bf16[1,1152,128]{2,1,0:T(8,128)(2,1)} %get-tuple-element.194), channel_id=1, source_target_pairs={{0,16},{4,20},{8,24},{12,28},{16,0},{20,4},{24,8},{28,12},{1,17},{... | collective-permute-start | bytes 884744 | tf_op jit(solution)/shard_map/ppermute | solution.py:27
  224.8 25.5 %collective-permute-start.21 = (bf16[2,1152,128]{2,1,0:T(8,128)(2,1)}, bf16[2,1152,128]{2,1,0:T(8,128)(2,1)}, u32[]{:S(2)}, u32[]{:S(2)}) collective-permute-start(bf16[2,1152,128]{2,1,0:T(8,128)(2,1)} %get-tuple-element.201), channel_id=1, source_target_pairs={{0,8},{4,12},{8,0},{12,4},{16,24},{20,28},{24,16},{28,20},{1,9},{5... | collective-permute-start | bytes 1769480 | tf_op jit(solution)/shard_map/ppermute | solution.py:27
  244.0 32.2 %collective-permute-start.24 = (f32[8,1024]{1,0:T(8,128)}, f32[8,1024]{1,0:T(8,128)}, u32[]{:S(2)}, u32[]{:S(2)}) collective-permute-start(f32[8,1024]{1,0:T(8,128)} %get-tuple-element.209), channel_id=1, source_target_pairs={{1,0},{2,1},{3,2},{5,4},{6,5},{7,6},{9,8},{10,9},{11,10},{13,12},{... | collective-permute-start | bytes 98312 | tf_op jit(solution)/shard_map/ppermute | solution.py:33
  248.0 25.1 %collective-permute-start.25 = (bf16[2,1152,128]{2,1,0:T(8,128)(2,1)}, bf16[2,1152,128]{2,1,0:T(8,128)(2,1)}, u32[]{:S(2)}, u32[]{:S(2)}) collective-permute-start(bf16[2,1152,128]{2,1,0:T(8,128)(2,1)} %lay.6), channel_id=1, source_target_pairs={{0,8},{4,12},{8,0},{12,4},{16,24},{20,28},{24,16},{28,20},{1,9},{5... | collective-permute-start | bytes 1769480 | tf_op jit(solution)/shard_map/ppermute | solution.py:27
  252.4 33.9 %collective-permute-start.28 = (bf16[1,1152,128]{2,1,0:T(8,128)(2,1)}, bf16[1,1152,128]{2,1,0:T(8,128)(2,1)}, u32[]{:S(2)}, u32[]{:S(2)}) collective-permute-start(bf16[1,1152,128]{2,1,0:T(8,128)(2,1)} %get-tuple-element.212), channel_id=1, source_target_pairs={{0,16},{4,20},{8,24},{12,28},{16,0},{20,4},{24,8},{28,12},{1,17},{... | collective-permute-start | bytes 884744 | tf_op jit(solution)/shard_map/ppermute | solution.py:27
  264.5 32.5 %collective-permute-start.23 = (bf16[2,1152,128]{2,1,0:T(8,128)(2,1)}, bf16[2,1152,128]{2,1,0:T(8,128)(2,1)}, u32[]{:S(2)}, u32[]{:S(2)}) collective-permute-start(bf16[2,1152,128]{2,1,0:T(8,128)(2,1)} %get-tuple-element.220), channel_id=1, source_target_pairs={{0,8},{4,12},{8,0},{12,4},{16,24},{20,28},{24,16},{28,20},{1,9},{5... | collective-permute-start | bytes 1769480 | tf_op jit(solution)/shard_map/ppermute | solution.py:27
  271.6 48.0 %collective-permute-start.33 = (bf16[8,32,2176]{2,1,0:T(8,128)(2,1)}, bf16[8,32,2176]{2,1,0:T(8,128)(2,1)}, u32[]{:S(2)}, u32[]{:S(2)}) collective-permute-start(bf16[8,32,2176]{2,1,0:T(8,128)(2,1)} %get-tuple-element.224), channel_id=1, source_target_pairs={{0,2},{1,3},{2,0},{3,1},{4,6},{5,7},{6,4},{7,5},{8,10},{9,11},{10,... | collective-permute-start | bytes 3342344 | tf_op jit(solution)/shard_map/ppermute | solution.py:27
  275.4 48.4 %collective-permute-start.42 = (bf16[4,1152,128]{2,1,0:T(8,128)(2,1)}, bf16[4,1152,128]{2,1,0:T(8,128)(2,1)}, u32[]{:S(2)}, u32[]{:S(2)}) collective-permute-start(bf16[4,1152,128]{2,1,0:T(8,128)(2,1)} %lay.7), channel_id=1, source_target_pairs={{0,4},{4,0},{8,12},{12,8},{16,20},{20,16},{24,28},{28,24},{1,5},{5... | collective-permute-start | bytes 3538952 | tf_op jit(solution)/shard_map/ppermute | solution.py:27
  288.1 24.5 %collective-permute-start.30 = (bf16[1,1152,128]{2,1,0:T(8,128)(2,1)}, bf16[1,1152,128]{2,1,0:T(8,128)(2,1)}, u32[]{:S(2)}, u32[]{:S(2)}) collective-permute-start(bf16[1,1152,128]{2,1,0:T(8,128)(2,1)} %halve.29.refs_0_), channel_id=1, source_target_pairs={{0,16},{4,20},{8,24},{12,28},{16,0},{20,4},{24,8},{28,12},{1,17},{... | collective-permute-start | bytes 884744 | tf_op jit(solution)/shard_map/ppermute | solution.py:27
  295.8 51.7 %collective-permute-start.36 = (bf16[8,32,2048]{2,1,0:T(8,128)(2,1)}, bf16[8,32,2048]{2,1,0:T(8,128)(2,1)}, u32[]{:S(2)}, u32[]{:S(2)}) collective-permute-start(bf16[8,32,2048]{2,1,0:T(8,128)(2,1)} %get-tuple-element.232), channel_id=1, source_target_pairs={{0,2},{1,3},{2,0},{3,1},{4,6},{5,7},{6,4},{7,5},{8,10},{9,11},{10,... | collective-permute-start | bytes 3145736 | tf_op jit(solution)/shard_map/ppermute | solution.py:27
  299.2 18.6 %collective-permute-start.29 = (bf16[1,1152,128]{2,1,0:T(8,128)(2,1)}, bf16[1,1152,128]{2,1,0:T(8,128)(2,1)}, u32[]{:S(2)}, u32[]{:S(2)}) collective-permute-start(bf16[1,1152,128]{2,1,0:T(8,128)(2,1)} %get-tuple-element.235), channel_id=1, source_target_pairs={{0,16},{4,20},{8,24},{12,28},{16,0},{20,4},{24,8},{28,12},{1,17},{... | collective-permute-start | bytes 884744 | tf_op jit(solution)/shard_map/ppermute | solution.py:27
  314.5 22.2 %collective-permute-start.32 = (bf16[2,1152,128]{2,1,0:T(8,128)(2,1)}, bf16[2,1152,128]{2,1,0:T(8,128)(2,1)}, u32[]{:S(2)}, u32[]{:S(2)}) collective-permute-start(bf16[2,1152,128]{2,1,0:T(8,128)(2,1)} %lay.8), channel_id=1, source_target_pairs={{0,8},{4,12},{8,0},{12,4},{16,24},{20,28},{24,16},{28,20},{1,9},{5... | collective-permute-start | bytes 1769480 | tf_op jit(solution)/shard_map/ppermute | solution.py:27
  319.6 20.6 %collective-permute-start.31 = (bf16[1,1152,128]{2,1,0:T(8,128)(2,1)}, bf16[1,1152,128]{2,1,0:T(8,128)(2,1)}, u32[]{:S(2)}, u32[]{:S(2)}) collective-permute-start(bf16[1,1152,128]{2,1,0:T(8,128)(2,1)} %halve.32.refs_0_), channel_id=1, source_target_pairs={{0,16},{4,20},{8,24},{12,28},{16,0},{20,4},{24,8},{28,12},{1,17},{... | collective-permute-start | bytes 884744 | tf_op jit(solution)/shard_map/ppermute | solution.py:27
  322.6 28.6 %collective-permute-start.35 = (bf16[4,32,2176]{2,1,0:T(8,128)(2,1)}, bf16[4,32,2176]{2,1,0:T(8,128)(2,1)}, u32[]{:S(2)}, u32[]{:S(2)}) collective-permute-start(bf16[4,32,2176]{2,1,0:T(8,128)(2,1)} %get-tuple-element.245), channel_id=1, source_target_pairs={{0,4},{4,0},{8,12},{12,8},{16,20},{20,16},{24,28},{28,24},{1,5},{5... | collective-permute-start | bytes 1671176 | tf_op jit(solution)/shard_map/ppermute | solution.py:27
  326.3 18.4 %collective-permute-start.37 = (bf16[512,1024]{1,0:T(8,128)(2,1)}, bf16[512,1024]{1,0:T(8,128)(2,1)}, u32[]{:S(2)}, u32[]{:S(2)}) collective-permute-start(bf16[512,1024]{1,0:T(8,128)(2,1)} %convolution_convert_fusion.3), channel_id=1, source_target_pairs={{0,1},{1,0},{2,3},{3,2},{4,5},{5,4},{6,7},{7,6},{8,9},{9,8},{10,11... | collective-permute-start | bytes 3145736 | tf_op jit(solution)/shard_map/ppermute | solution.py:27
  339.0 62.0 %collective-permute-start.44 = (bf16[4,1152,128]{2,1,0:T(8,128)(2,1)}, bf16[4,1152,128]{2,1,0:T(8,128)(2,1)}, u32[]{:S(2)}, u32[]{:S(2)}) collective-permute-start(bf16[4,1152,128]{2,1,0:T(8,128)(2,1)} %lay.9), channel_id=1, source_target_pairs={{0,4},{4,0},{8,12},{12,8},{16,20},{20,16},{24,28},{28,24},{1,5},{5... | collective-permute-start | bytes 3538952 | tf_op jit(solution)/shard_map/ppermute | solution.py:27
  342.1 16.5 %collective-permute-start.34 = (bf16[2,1152,128]{2,1,0:T(8,128)(2,1)}, bf16[2,1152,128]{2,1,0:T(8,128)(2,1)}, u32[]{:S(2)}, u32[]{:S(2)}) collective-permute-start(bf16[2,1152,128]{2,1,0:T(8,128)(2,1)} %lay.10), channel_id=1, source_target_pairs={{0,8},{4,12},{8,0},{12,4},{16,24},{20,28},{24,16},{28,20},{1,9},{5... | collective-permute-start | bytes 1769480 | tf_op jit(solution)/shard_map/ppermute | solution.py:27
  350.1 29.4 %collective-permute-start.40 = (bf16[4,32,2048]{2,1,0:T(8,128)(2,1)}, bf16[4,32,2048]{2,1,0:T(8,128)(2,1)}, u32[]{:S(2)}, u32[]{:S(2)}) collective-permute-start(bf16[4,32,2048]{2,1,0:T(8,128)(2,1)} %get-tuple-element.255), channel_id=1, source_target_pairs={{0,4},{4,0},{8,12},{12,8},{16,20},{20,16},{24,28},{28,24},{1,5},{5... | collective-permute-start | bytes 1572872 | tf_op jit(solution)/shard_map/ppermute | solution.py:27
  353.2 29.5 %collective-permute-start.45 = (bf16[2,32,2176]{2,1,0:T(8,128)(2,1)}, bf16[2,32,2176]{2,1,0:T(8,128)(2,1)}, u32[]{:S(2)}, u32[]{:S(2)}) collective-permute-start(bf16[2,32,2176]{2,1,0:T(8,128)(2,1)} %get-tuple-element.257), channel_id=1, source_target_pairs={{0,8},{4,12},{8,0},{12,4},{16,24},{20,28},{24,16},{28,20},{1,9},{5... | collective-permute-start | bytes 835592 | tf_op jit(solution)/shard_map/ppermute | solution.py:27
  361.1 53.8 %collective-permute-start.47 = (bf16[4,1152,128]{2,1,0:T(8,128)(2,1)}, bf16[4,1152,128]{2,1,0:T(8,128)(2,1)}, u32[]{:S(2)}, u32[]{:S(2)}) collective-permute-start(bf16[4,1152,128]{2,1,0:T(8,128)(2,1)} %lay.11), channel_id=1, source_target_pairs={{0,4},{4,0},{8,12},{12,8},{16,20},{20,16},{24,28},{28,24},{1,5},{5... | collective-permute-start | bytes 3538952 | tf_op jit(solution)/shard_map/ppermute | solution.py:27
  364.0 47.6 %collective-permute-start.38 = (bf16[512,1024]{1,0:T(8,128)(2,1)}, bf16[512,1024]{1,0:T(8,128)(2,1)}, u32[]{:S(2)}, u32[]{:S(2)}) collective-permute-start(bf16[512,1024]{1,0:T(8,128)(2,1)} %convolution_convert_fusion.1), channel_id=1, source_target_pairs={{0,1},{1,0},{2,3},{3,2},{4,5},{5,4},{6,7},{7,6},{8,9},{9,8},{10,11... | collective-permute-start | bytes 3145736 | tf_op jit(solution)/shard_map/ppermute | solution.py:27
  379.5 32.1 %collective-permute-start.39 = (bf16[512,1024]{1,0:T(8,128)(2,1)}, bf16[512,1024]{1,0:T(8,128)(2,1)}, u32[]{:S(2)}, u32[]{:S(2)}) collective-permute-start(bf16[512,1024]{1,0:T(8,128)(2,1)} %bitcast.15), channel_id=1, source_target_pairs={{0,2},{1,3},{2,0},{3,1},{4,6},{5,7},{6,4},{7,5},{8,10},{9,11},{10,... | collective-permute-start | bytes 3145736 | tf_op jit(solution)/shard_map/ppermute | solution.py:27
  (54 other events, 345.0 us)
Sparse Core Ops, SparseCore 0:
  10.9 75.4 all-gather.1

commit v5 on v4

--- a/solution.py
+++ b/solution.py
@@ -473,6 +473,33 @@
     )(place, weight_in, *gathered, x, before, same)
 
 
+def onward_kernel(place_ref, *refs):
+    *hids, down_ref, out_ref = refs
+    for n, hid_ref in enumerate(hids):
+
+        @pl.when(pl.program_id(0) == n)
+        def _(hid_ref=hid_ref):
+            out_ref[...] = dot(hid_ref[...], down_ref[...], NN).astype(BF16)
+
+
+def onward(place, hids, down):
+    rows, hidden = hids[0].shape
+    features = down.shape[1]
+    return pl.pallas_call(
+        onward_kernel,
+        grid_spec=pltpu.PrefetchScalarGridSpec(
+            num_scalar_prefetch=1,
+            grid=(len(hids),),
+            in_specs=[once(a) for a in (*hids, down)],
+            out_specs=pl.BlockSpec((rows, features), lambda i, place: (place[0] ^ i, 0)),
+        ),
+        out_shape=jax.ShapeDtypeStruct((len(hids) * rows, features), BF16),
+        compiler_params=pltpu.CompilerParams(vmem_limit_bytes=VMEM_LIMIT),
+        cost_estimate=LONG,
+        name="onward",
+    )(place, *hids, down)
+
+
 def mix_back_kernel(bits, place_ref, near_ref, beside_ref, across_ref, cot_ref, res_ref, mix_ref,
                     c0, c1, vec_ref, same_ref,
                     rg_ref, rlow_ref, cl_ref, pg_ref, rim_ref, sums_ref,
@@ -820,6 +847,7 @@
 
     hidden_units = gate_proj.shape[1]
     bits_all = list(range(bits_of("mp") + bits_of("dp")))
+    bits_all.append(bits_all.pop(bits_of("mp")))
     beside = swap(second_low, "mp", 0)
     across = swap(second_low, "mp", 1)
     *near_acts, og, ou, od = near_feed(
@@ -848,9 +876,6 @@
         grad = dot(gate_low, gate_proj, NT) + dot(up_low, up_proj, NT)
         return order.mark(grad.astype(BF16))
 
-    def onward(acts, n):
-        return order.mark(dot(order(acts[n]), down_proj, NN).astype(BF16))
-
     def both(kept, got):
         (total,) = halve(kept[None], order(got)[None], 1)
         return order.mark(total)[0]
@@ -864,11 +889,17 @@
     one.add()
     one.send()
     back_near = back(near_acts, 0)
+    hids = [near_acts[0], near_acts[1], far_acts[0], far_acts[1]]
+    place_in = lax.axis_index("mp").reshape(1).astype(jnp.int32)
+    parts = order.mark(onward(place_in, order(hids), down_proj))
+    branch = lax.psum_scatter(parts, "mp", scatter_dimension=0, tiled=True)
     two.add()
     two.send()
-    three.send()
     one.add()
     one.send()
+    three.send()
+    three.add()
+    three.send()
 
     back_across, back_beside = order((back_across, back_beside))
     residual_grad, residual_low, closing_low, product_part, rim_out, totals = mix_back(
@@ -889,6 +920,8 @@
     outer.send()
     three.add()
     three.send()
+    two.add()
+    two.send()
     outer.add()
     outer.send()
     one.add()
@@ -901,10 +934,10 @@
     rest.send()
     two.add()
     two.send()
+    three.add()
+    three.send()
     rest.add()
     rest.send()
-    three.add()
-    three.send()
     input_grad = input_back(
         order(first_part), closing_low, last_part, weight_in, residual_grad, x, vec,
     )
@@ -916,28 +949,21 @@
     three.send()
     outer.add()
     outer.send()
-    one.add()
-    got = swap(onward(far_acts, 1), "mp", 0)
-    two.add()
-    two.send()
+    rest.add()
+    rest.send()
     three.add()
     three.send()
-    on_far = both(onward(far_acts, 0), got)
+    layer_out = order.mark((residual + order(branch).astype(F32)).astype(BF16))
+    layer_out = layer_out.reshape(1, rows, features)
+    one.add()
+    done = unpack(place, one.pieces, (), one.bits, wide, 0, features, hidden_units)
+    order.mark(done[0])
+    outer.add()
+    outer.send()
     rest.add()
     rest.send()
     outer.add()
     outer.send()
-    three.add()
-    three.send()
-    on_across = swap(order(on_far), "mp", 1)
-    on_beside = swap(onward(near_acts, 1), "mp", 0)
-    on_near = onward(near_acts, 0)
-    rest.add()
-    rest.send()
-    outer.add()
-    outer.send()
-    done = unpack(place, one.pieces, (), one.bits, wide, 0, features, hidden_units)
-    order.mark(done[0])
     rest.add()
     rest.send()
     outer.finish()
@@ -945,8 +971,6 @@
     done = unpack(place, two.pieces, done, two.bits, wide, 1, features, hidden_units)
     order.mark(done[0])
     rest.finish()
-    branch = on_near.astype(F32) + on_beside.astype(F32) + order(on_across).astype(F32)
-    layer_out = order.mark((residual + branch).astype(BF16)).reshape(1, rows, features)
     grad_out = outer.total[:, :features]
     grad_second = outer.total[:, features]
     grad_conv = outer.total[:, features + 1 : features + 1 + KERNEL]

time: 434 us -> 426 us (0.982)
  matrix products: 31.4 us -> 21.2 us
  Pallas kernels: 193 us -> 201 us
  waiting for transfers between devices: 119 us -> 114 us
    pallas_call x0 -> x1, Pallas kernels: none -> 10.3 us  [onward(): pl.pallas_call(onward_kernel, grid_spec=pltpu.PrefetchScalarGridSpec(num_...]
    dot_general x12 -> x8, matrix products: 31.4 us -> 21.2 us  [dot(): return lax.dot_general(left, right, dims, preferred_element_type=F32)]
    ppermute x45 -> x42, waiting for transfers between devices: 105 us -> 100 us  [swap(): return lax.ppermute(block, axis, [(i, i ^ 1 << bit) for i in range(size)])]
    ppermute x45 -> x42, starting transfers between devices: 43.3 us -> 46.7 us  [swap(): return lax.ppermute(block, axis, [(i, i ^ 1 << bit) for i in range(size)])]
    unnamed x78 -> x56, local copies, waits for them, and re-layouts: 8.71 us -> 5.6 us
    pallas_call x21 -> x20, Pallas kernels: 50.4 us -> 47.6 us  [halve(): pl.pallas_call(halve_kernel, grid=(1,), in_specs=[whole(kept), whole(got)...]
  transfers between devices with their start and end apart: 49 -> 47, of which waited for: 15 -> 17; matrix products, arithmetic and copies ran while one was open for 10% -> 7% of each run, Pallas kernels for 38% -> 41%
where the time goes in v5:
time: 426 us; the launch traced here: 419 us
  Pallas kernels  201 us (47%)
  waiting for transfers between devices  114 us (27%)
  starting transfers between devices  52.4 us (12%)
  matrix products  21.2 us (5%)
  between operations  14.9 us (3%)
  local copies, waits for them, and re-layouts  9.15 us (2%)
  other arithmetic  6.71 us (2%)
    ppermute x42, waiting for transfers between devices, swap(): return lax.ppermute(block, axis, [(i, i ^ 1 << bit) for i in range(size)])  100 us
    pallas_call x20, Pallas kernels, halve(): pl.pallas_call(halve_kernel, grid=(1,), in_specs=[whole(kept), whole(got)...  47.6 us
    ppermute x42, starting transfers between devices, swap(): return lax.ppermute(block, axis, [(i, i ^ 1 << bit) for i in range(size)])  46.7 us
    pallas_call x3, Pallas kernels, far_feed(): pl.pallas_call(functools.partial(far_kernel, orders), grid_spec=pltpu.Pre...  36.3 us
    pallas_call x1, Pallas kernels, near_feed(): pl.pallas_call(near_kernel, grid=(pl.cdiv(hidden, wide),), in_specs=[whol...  23.3 us
    dot_general x8, matrix products, dot(): return lax.dot_general(left, right, dims, preferred_element_type=F32)  21.2 us
    pallas_call x1, Pallas kernels, mix_back(): pl.pallas_call(functools.partial(mix_back_kernel, bits), grid_spec=pltpu....  14.4 us
    pallas_call x1, Pallas kernels, mix_front(): pl.pallas_call(functools.partial(mix_front_kernel, bits), grid_spec=pltpu...  13.8 us
  transfers between devices with their start and end apart: 47, of which 17 were waited for; matrix products, arithmetic and copies ran while one was open for 7% of the time, Pallas kernels for 41%

profile of v5, /device:TPU:0, one launch (start us, length us, event | category | flops | bytes accessed | tf_op | source)
XLA Modules:
  0.0 418.6 jit_solution(12564206611166051438)
XLA Ops:
  9.6 4.0 collective-permute-start
  13.7 3.9 collective-permute-done
  18.3 4.5 %collective-permute-done.1 = bf16[2,32,1152]{2,1,0:T(8,128)(2,1)S(1)} collective-permute-done((bf16[2,32,1152]{2,1,0:T(8,128)(2,1)S(1)}, bf16[2,32,1152]{2,1,0:T(8,128)(2,1)S(1)}, u32[]{:S(2)}, u32[]{:S(2)}) %collective-permute-start.1) | collective-permute-done | bytes 147488 | tf_op jit(solution)/shard_map/ppermute | solution.py:27
  26.2 4.7 %collective-permute-done.2 = bf16[4,32,1152]{2,1,0:T(8,128)(2,1)S(1)} collective-permute-done((bf16[4,32,1152]{2,1,0:T(8,128)(2,1)S(1)}, bf16[4,32,1152]{2,1,0:T(8,128)(2,1)S(1)}, u32[]{:S(2)}, u32[]{:S(2)}) %collective-permute-start.2) | collective-permute-done | bytes 294944 | tf_op jit(solution)/shard_map/ppermute | solution.py:27
  32.5 32.6 %collective-permute-done.3 = bf16[8,32,1152]{2,1,0:T(8,128)(2,1)S(1)} collective-permute-done((bf16[8,32,1152]{2,1,0:T(8,128)(2,1)S(1)}, bf16[8,32,1152]{2,1,0:T(8,128)(2,1)S(1)}, u32[]{:S(2)}, u32[]{:S(2)}) %collective-permute-start.3) | collective-permute-done | bytes 589856 | tf_op jit(solution)/shard_map/ppermute | solution.py:27
  74.0 12.5 %all-gather.2.cloned.1.call-done.in_any.w_ref = bf16[1024,3072]{1,0:T(8,128)(2,1)} async-done(((bf16[32,3072]{1,0:T(8,128)(2,1)}), bf16[1024,3072]{1,0:T(8,128)(2,1)}) %all-gather.2.cloned.1.call-update) | async-done | bytes 6291472 | tf_op jit(solution)/shard_map/all_gather | solution.py:831
  86.5 13.8 %mix_front.1 = (f32[520,3072]{1,0:T(8,128)}, bf16[520,1024]{1,0:T(8,128)(2,1)}, bf16[512,1024]{1,0:T(8,128)(2,1)}, f32[8,1024]{1,0:T(8,128)}, f32[512,1024]{1,0:T(8,128)}, /*index=5*/bf16[512,1024]{1,0:T(8,128)(2,1)}) custom-call(s32[1]{0:T(128)} %bitcast.place_ref, bf16[1024,3072]{1,0:T(8,128)(2,1)} %all-gather.2.cloned.1.call-done.in_any.w_ref, ...), custom_call_target="tpu_custom_call" | custom-call | flops 99999997952 | tf_op jit(solution)/shard_map/mix_front/pallas_call | solution.py:450
  104.2 23.3 %near_feed.1 = (bf16[512,1152]{1,0:T(8,128)(2,1)}, bf16[512,1152]{1,0:T(8,128)(2,1)}, bf16[512,1152]{1,0:T(8,128)(2,1)}, bf16[512,1152]{1,0:T(8,128)(2,1)}, bf16...) custom-call(bf16[512,1024]{1,0:T(8,128)(2,1)} %get-tuple-element.149, ...), custom_call_target="tpu_custom_call" | custom-call | flops 99999997952 | tf_op jit(solution)/shard_map/near_feed/pallas_call | solution.py:124
  131.3 11.8 %far_feed.3 = (bf16[512,1152]{1,0:T(8,128)(2,1)}, bf16[512,1152]{1,0:T(8,128)(2,1)}, bf16[512,1152]{1,0:T(8,128)(2,1)}, bf16[512,1152]{1,0:T(8,128)(2,1)}, bf16[...) custom-call(s32[1]{0:T(128)} %bitcast.10.place_ref, ...), custom_call_target="tpu_custom_call" | custom-call | flops 99999997952 | tf_op jit(solution)/shard_map/far_feed/pallas_call | solution.py:186
  144.5 12.3 %far_feed.4 = (bf16[512,1152]{1,0:T(8,128)(2,1)}, bf16[512,1152]{1,0:T(8,128)(2,1)}, bf16[512,1152]{1,0:T(8,128)(2,1)}, bf16[512,1152]{1,0:T(8,128)(2,1)}, bf16[...) custom-call(s32[1]{0:T(128)} %bitcast.10.place_ref, ...), custom_call_target="tpu_custom_call", output_to_operand_aliasing={{0}: (11, {}), {1}: (12, {}), {2}: (13, {}), {3}: (14, {}),... | custom-call | flops 99999997952 | tf_op jit(solution)/shard_map/far_feed/pallas_call | solution.py:186
  156.8 12.2 %far_feed.5 = (bf16[512,1152]{1,0:T(8,128)(2,1)}, bf16[512,1152]{1,0:T(8,128)(2,1)}, bf16[512,1152]{1,0:T(8,128)(2,1)}, bf16[512,1152]{1,0:T(8,128)(2,1)}, bf16[...) custom-call(s32[1]{0:T(128)} %bitcast.10.place_ref, ...), custom_call_target="tpu_custom_call", output_to_operand_aliasing={{0}: (11, {}), {1}: (12, {}), {2}: (13, {}), {3}: (14, {}),... | custom-call | flops 99999997952 | tf_op jit(solution)/shard_map/far_feed/pallas_call | solution.py:186
  169.6 3.0 fusion.5
  180.2 3.0 fusion.6
  188.5 3.2 fusion.7
  199.0 3.0 fusion.8
  204.5 10.3 %onward.1 = bf16[2048,1024]{1,0:T(8,128)(2,1)} custom-call(s32[1]{0:T(128)} %bitcast.9.place_ref, bf16[512,1152]{1,0:T(8,128)(2,1)} %get-tuple-element.195.refs_0_, bf16[512,1152]{1,0:T(8,128)(2,1)} %get-tuple-element.196.refs_1_, bf16[512,1152]{1,0:T(8,128)(2,1)} %get-tuple-element.197.refs_2_, bf16[512,1152]{1,0:T(8,128)(2,1)} %get-tuple-element.198.refs_3_, ...), custom_call_target="tpu_custom_call" | custom-call | flops 99999997952 | tf_op jit(solution)/shard_map/onward/pallas_call | solution.py:488
  214.9 7.6 %collective-permute-done.18.got_ref = bf16[4,1152,128]{2,1,0:T(8,128)(2,1)} collective-permute-done((bf16[4,1152,128]{2,1,0:T(8,128)(2,1)}, bf16[4,1152,128]{2,1,0:T(8,128)(2,1)}, u32[]{:S(2)}, u32[]{:S(2)}) %collective-permute-start.18) | collective-permute-done | bytes 1179680 | tf_op jit(solution)/shard_map/ppermute | solution.py:27
  222.4 3.0 halve.23
  234.3 14.4 %mix_back.1 = (f32[512,1024]{1,0:T(8,128)}, bf16[512,1024]{1,0:T(8,128)(2,1)}, bf16[512,1024]{1,0:T(8,128)(2,1)}, f32[512,1024]{1,0:T(8,128)}, f32[8,1024]{1,0:T(8,128)}, /*index=5*/f32[4,8,1024]{2,1,0:T(8,128)}) custom-call(s32[1]{0:T(128)} %bitcast.place_ref, bf16[512,1024]{1,0:T(8,128)(2,1)} %add_convert_fusion.1.near_ref, ...), custom_call_target="tpu_custom_call" | custom-call | flops 99999997952 | tf_op jit(solution)/shard_map/mix_back/pallas_call | solution.py:604
  256.5 8.5 %mix_outer.1 = (bf16[16,32,2176]{2,1,0:T(8,128)(2,1)}, bf16[16,32,2176]{2,1,0:T(8,128)(2,1)}) custom-call(s32[1]{0:T(128)} %bitcast.place_ref, bf16[512,1024]{1,0:T(8,128)(2,1)} %get-tuple-element.209.gated_ref, bf16[512,1024]{1,0:T(8,128)(2,1)} %get-tuple-element.220.rlow_ref, bf16[520,1024]{1,0:T(8,128)(2,1)} %get-tuple-element.221.low_ref, ...), custom_call_target="tpu_custom_call" | custom-call | flops 99999997952 | tf_op jit(solution)/shard_map/mix_outer/pallas_call | solution.py:633
  269.5 9.7 %collective-permute-done.25.got_ref = bf16[1,1152,128]{2,1,0:T(8,128)(2,1)} collective-permute-done((bf16[1,1152,128]{2,1,0:T(8,128)(2,1)}, bf16[1,1152,128]{2,1,0:T(8,128)(2,1)}, u32[]{:S(2)}, u32[]{:S(2)}) %collective-permute-start.25) | collective-permute-done | bytes 294944 | tf_op jit(solution)/shard_map/ppermute | solution.py:27
  281.0 3.4 collective-permute-start.26
  284.4 4.0 halve.29
  293.0 10.0 %mix_grads.1 = (bf16[512,1024]{1,0:T(8,128)(2,1)}, bf16[512,1024]{1,0:T(8,128)(2,1)}, bf16[16,32,2048]{2,1,0:T(8,128)(2,1)}, bf16[16,32,2048]{2,1,0:T(8,128)(2,1)}) custom-call(s32[1]{0:T(128)} %bitcast.place_ref, f32[512,1024]{1,0:T(8,128)} %get-tuple-element.230.pg_ref, f32[8,1024]{1,0:T(8,128)} %collective-permute-done.27.rim_ref, ...), custom_call_target="tpu_custom_call" | custom-call | flops 99999997952 | tf_op jit(solution)/shard_map/mix_grads/pallas_call | solution.py:682
  309.4 3.8 halve.31
  314.9 11.1 %input_back.1 = f32[512,1024]{1,0:T(8,128)} custom-call(bf16[512,1024]{1,0:T(8,128)(2,1)} %get-tuple-element.243.first_ref, bf16[512,1024]{1,0:T(8,128)(2,1)} %get-tuple-element.222.cl_ref.mid_ref, bf16[512,1024]{1,0:T(8,128)(2,1)} %get-tuple-element.244.last_ref, bf16[1024,3072]{1,0:T(8,128)(2,1)} %all-gather.2.cloned.1.call-done.in_any.w_ref, ...), custom_call_target="tpu_custom_call" | custom-call | flops 99999997952 | tf_op jit(solution)/shard_map/input_back/pallas_call | solution.py:718
  341.3 7.8 %collective-permute-done.33.refs_2_ = bf16[2,1152,128]{2,1,0:T(8,128)(2,1)} collective-permute-done((bf16[2,1152,128]{2,1,0:T(8,128)(2,1)}, bf16[2,1152,128]{2,1,0:T(8,128)(2,1)}, u32[]{:S(2)}, u32[]{:S(2)}) %collective-permute-start.33) | collective-permute-done | bytes 589856 | tf_op jit(solution)/shard_map/ppermute | solution.py:27
  355.3 4.1 unpack.3
  363.6 12.0 %collective-permute-done.36.got_ref = bf16[4,32,2048]{2,1,0:T(8,128)(2,1)} collective-permute-done((bf16[4,32,2048]{2,1,0:T(8,128)(2,1)}, bf16[4,32,2048]{2,1,0:T(8,128)(2,1)}, u32[]{:S(2)}, u32[]{:S(2)}) %collective-permute-start.36) | collective-permute-done | bytes 524320 | tf_op jit(solution)/shard_map/ppermute | solution.py:27
  382.0 8.1 %collective-permute-done.39.got_ref = bf16[2,32,2048]{2,1,0:T(8,128)(2,1)S(1)} collective-permute-done((bf16[2,32,2048]{2,1,0:T(8,128)(2,1)}, bf16[2,32,2048]{2,1,0:T(8,128)(2,1)S(1)}, u32[]{:S(2)}, u32[]{:S(2)}) %collective-permute-start.39) | collective-permute-done | bytes 262176 | tf_op jit(solution)/shard_map/ppermute | solution.py:27
  396.9 4.1 unpack.4
  407.2 4.1 unpack.5
  (192 shorter events, 129.8 us)
Async XLA Ops:
  7.2 79.3 %all-gather.2.cloned.1.call-start = ((), (), s32[]{:S(2)}) async-start(), calls=%async_computation.1 | async-start | bytes 6488064 | tf_op jit(solution)/shard_map/all_gather | solution.py:831
  7.9 344.9 %reduce-scatter.2.cloned.1.call-start = ((), (), s32[]{:S(2)}) async-start(), calls=%async_computation.2 | async-start | bytes 5242880 | tf_op jit(solution)/shard_map/reduce_scatter | solution.py:895
  24.6 43.2 %collective-permute-start.7 = (bf16[512,1024]{1,0:T(8,128)(2,1)S(1)}, bf16[512,1024]{1,0:T(8,128)(2,1)}, u32[]{:S(2)}, u32[]{:S(2)}) collective-permute-start(bf16[512,1024]{1,0:T(8,128)(2,1)S(1)} %bitcast.53), channel_id=1, source_target_pairs={{0,2},{1,3},{2,0},{3,1},{4,6},{5,7},{6,4},{7,5},{8,10},{9,11},{10,... | collective-permute-start | bytes 3145736 | tf_op jit(solution)/shard_map/ppermute | solution.py:27
  26.2 47.8 %collective-permute-start.6 = (bf16[512,1024]{1,0:T(8,128)(2,1)S(1)}, bf16[512,1024]{1,0:T(8,128)(2,1)}, u32[]{:S(2)}, u32[]{:S(2)}) collective-permute-start(bf16[512,1024]{1,0:T(8,128)(2,1)S(1)} %bitcast.54), channel_id=1, source_target_pairs={{0,1},{1,0},{2,3},{3,2},{4,5},{5,4},{6,7},{7,6},{8,9},{9,8},{10,11... | collective-permute-start | bytes 3145736 | tf_op jit(solution)/shard_map/ppermute | solution.py:27
  30.9 34.3 %collective-permute-start.3 = (bf16[8,32,1152]{2,1,0:T(8,128)(2,1)S(1)}, bf16[8,32,1152]{2,1,0:T(8,128)(2,1)S(1)}, u32[]{:S(2)}, u32[]{:S(2)}) collective-permute-start(bf16[8,32,1152]{2,1,0:T(8,128)(2,1)S(1)} %pad_maximum_fusion), channel_id=1, source_target_pairs={{0,2},{1,3},{2,0},{3,1},{4,6},{5,7},{6,4},{7,5},{8,10},{9,11},{10,... | collective-permute-start | bytes 1769480 | tf_op jit(solution)/shard_map/ppermute | solution.py:27
  100.7 26.9 %collective-permute-start.11 = (bf16[512,1024]{1,0:T(8,128)(2,1)}, bf16[512,1024]{1,0:T(8,128)(2,1)S(1)}, u32[]{:S(2)}, u32[]{:S(2)}) collective-permute-start(bf16[512,1024]{1,0:T(8,128)(2,1)} %get-tuple-element.149.xa_ref), channel_id=1, source_target_pairs={{0,2},{1,3},{2,0},{3,1},{4,6},{5,7},{6,4},{7,5},{8,10},{9,11},{10,... | collective-permute-start | bytes 3145736 | tf_op jit(solution)/shard_map/ppermute | solution.py:27
  143.1 32.7 %collective-permute-start.13 = (bf16[4,1152,128]{2,1,0:T(8,128)(2,1)}, bf16[4,1152,128]{2,1,0:T(8,128)(2,1)}, u32[]{:S(2)}, u32[]{:S(2)}) collective-permute-start(bf16[4,1152,128]{2,1,0:T(8,128)(2,1)} %get-tuple-element.173), channel_id=1, source_target_pairs={{0,4},{4,0},{8,12},{12,8},{16,20},{20,16},{24,28},{28,24},{1,5},{5... | collective-permute-start | bytes 3538952 | tf_op jit(solution)/shard_map/ppermute | solution.py:27
  169.0 60.8 %collective-permute-start.16 = (bf16[4,1152,128]{2,1,0:T(8,128)(2,1)}, bf16[4,1152,128]{2,1,0:T(8,128)(2,1)}, u32[]{:S(2)}, u32[]{:S(2)}) collective-permute-start(bf16[4,1152,128]{2,1,0:T(8,128)(2,1)} %get-tuple-element.176), channel_id=1, source_target_pairs={{0,4},{4,0},{8,12},{12,8},{16,20},{20,16},{24,28},{28,24},{1,5},{5... | collective-permute-start | bytes 3538952 | tf_op jit(solution)/shard_map/ppermute | solution.py:27
  174.3 48.2 %collective-permute-start.18 = (bf16[4,1152,128]{2,1,0:T(8,128)(2,1)}, bf16[4,1152,128]{2,1,0:T(8,128)(2,1)}, u32[]{:S(2)}, u32[]{:S(2)}) collective-permute-start(bf16[4,1152,128]{2,1,0:T(8,128)(2,1)} %get-tuple-element.202), channel_id=1, source_target_pairs={{0,4},{4,0},{8,12},{12,8},{16,20},{20,16},{24,28},{28,24},{1,5},{5... | collective-permute-start | bytes 3538952 | tf_op jit(solution)/shard_map/ppermute | solution.py:27
  178.5 16.3 %collective-permute-start.14 = (bf16[2,1152,128]{2,1,0:T(8,128)(2,1)}, bf16[2,1152,128]{2,1,0:T(8,128)(2,1)S(1)}, u32[]{:S(2)}, u32[]{:S(2)}) collective-permute-start(bf16[2,1152,128]{2,1,0:T(8,128)(2,1)} %get-tuple-element.181), channel_id=1, source_target_pairs={{0,8},{4,12},{8,0},{12,4},{16,24},{20,28},{24,16},{28,20},{1,9},{5... | collective-permute-start | bytes 1769480 | tf_op jit(solution)/shard_map/ppermute | solution.py:27
  194.2 40.1 %collective-permute-start.21 = (bf16[512,1024]{1,0:T(8,128)(2,1)}, bf16[512,1024]{1,0:T(8,128)(2,1)}, u32[]{:S(2)}, u32[]{:S(2)}) collective-permute-start(bf16[512,1024]{1,0:T(8,128)(2,1)} %add_convert_fusion.2), channel_id=1, source_target_pairs={{0,1},{1,0},{2,3},{3,2},{4,5},{5,4},{6,7},{7,6},{8,9},{9,8},{10,11... | collective-permute-start | bytes 3145736 | tf_op jit(solution)/shard_map/ppermute | solution.py:27
  194.2 40.1 %collective-permute-start.20 = (bf16[512,1024]{1,0:T(8,128)(2,1)}, bf16[512,1024]{1,0:T(8,128)(2,1)}, u32[]{:S(2)}, u32[]{:S(2)}) collective-permute-start(bf16[512,1024]{1,0:T(8,128)(2,1)} %bitcast.13), channel_id=1, source_target_pairs={{0,2},{1,3},{2,0},{3,1},{4,6},{5,7},{6,4},{7,5},{8,10},{9,11},{10,... | collective-permute-start | bytes 3145736 | tf_op jit(solution)/shard_map/ppermute | solution.py:27
  197.8 29.4 %collective-permute-start.17 = (bf16[1,1152,128]{2,1,0:T(8,128)(2,1)}, bf16[1,1152,128]{2,1,0:T(8,128)(2,1)}, u32[]{:S(2)}, u32[]{:S(2)}) collective-permute-start(bf16[1,1152,128]{2,1,0:T(8,128)(2,1)} %get-tuple-element.192), channel_id=1, source_target_pairs={{0,16},{4,20},{8,24},{12,28},{16,0},{20,4},{24,8},{28,12},{1,17},{... | collective-permute-start | bytes 884744 | tf_op jit(solution)/shard_map/ppermute | solution.py:27
  225.4 27.1 %collective-permute-start.22 = (bf16[2,1152,128]{2,1,0:T(8,128)(2,1)}, bf16[2,1152,128]{2,1,0:T(8,128)(2,1)}, u32[]{:S(2)}, u32[]{:S(2)}) collective-permute-start(bf16[2,1152,128]{2,1,0:T(8,128)(2,1)} %get-tuple-element.204), channel_id=1, source_target_pairs={{0,8},{4,12},{8,0},{12,4},{16,24},{20,28},{24,16},{28,20},{1,9},{5... | collective-permute-start | bytes 1769480 | tf_op jit(solution)/shard_map/ppermute | solution.py:27
  228.9 21.1 %collective-permute-start.23 = (bf16[1,1152,128]{2,1,0:T(8,128)(2,1)}, bf16[1,1152,128]{2,1,0:T(8,128)(2,1)}, u32[]{:S(2)}, u32[]{:S(2)}) collective-permute-start(bf16[1,1152,128]{2,1,0:T(8,128)(2,1)} %halve.24.refs_0_), channel_id=1, source_target_pairs={{0,16},{4,20},{8,24},{12,28},{16,0},{20,4},{24,8},{28,12},{1,17},{... | collective-permute-start | bytes 884744 | tf_op jit(solution)/shard_map/ppermute | solution.py:27
  232.6 34.7 %collective-permute-start.19 = (bf16[2,1152,128]{2,1,0:T(8,128)(2,1)}, bf16[2,1152,128]{2,1,0:T(8,128)(2,1)}, u32[]{:S(2)}, u32[]{:S(2)}) collective-permute-start(bf16[2,1152,128]{2,1,0:T(8,128)(2,1)} %get-tuple-element.208), channel_id=1, source_target_pairs={{0,8},{4,12},{8,0},{12,4},{16,24},{20,28},{24,16},{28,20},{1,9},{5... | collective-permute-start | bytes 1769480 | tf_op jit(solution)/shard_map/ppermute | solution.py:27
  248.7 44.3 %collective-permute-start.27 = (f32[8,1024]{1,0:T(8,128)}, f32[8,1024]{1,0:T(8,128)}, u32[]{:S(2)}, u32[]{:S(2)}) collective-permute-start(f32[8,1024]{1,0:T(8,128)} %get-tuple-element.216), channel_id=1, source_target_pairs={{1,0},{2,1},{3,2},{5,4},{6,5},{7,6},{9,8},{10,9},{11,10},{13,12},{... | collective-permute-start | bytes 98312 | tf_op jit(solution)/shard_map/ppermute | solution.py:33
  251.9 37.6 %collective-permute-start.28 = (bf16[2,1152,128]{2,1,0:T(8,128)(2,1)}, bf16[2,1152,128]{2,1,0:T(8,128)(2,1)}, u32[]{:S(2)}, u32[]{:S(2)}) collective-permute-start(bf16[2,1152,128]{2,1,0:T(8,128)(2,1)} %lay.6), channel_id=1, source_target_pairs={{0,8},{4,12},{8,0},{12,4},{16,24},{20,28},{24,16},{28,20},{1,9},{5... | collective-permute-start | bytes 1769480 | tf_op jit(solution)/shard_map/ppermute | solution.py:27
  254.6 24.5 %collective-permute-start.25 = (bf16[1,1152,128]{2,1,0:T(8,128)(2,1)}, bf16[1,1152,128]{2,1,0:T(8,128)(2,1)}, u32[]{:S(2)}, u32[]{:S(2)}) collective-permute-start(bf16[1,1152,128]{2,1,0:T(8,128)(2,1)} %get-tuple-element.219), channel_id=1, source_target_pairs={{0,16},{4,20},{8,24},{12,28},{16,0},{20,4},{24,8},{28,12},{1,17},{... | collective-permute-start | bytes 884744 | tf_op jit(solution)/shard_map/ppermute | solution.py:27
  265.1 19.4 %collective-permute-start.29 = (bf16[16,32,2176]{2,1,0:T(8,128)(2,1)}, bf16[16,32,2176]{2,1,0:T(8,128)(2,1)}, u32[]{:S(2)}, u32[]{:S(2)}) collective-permute-start(bf16[16,32,2176]{2,1,0:T(8,128)(2,1)} %get-tuple-element.224), channel_id=1, source_target_pairs={{0,1},{1,0},{2,3},{3,2},{4,5},{5,4},{6,7},{7,6},{8,9},{9,8},{10,11... | collective-permute-start | bytes 6684680 | tf_op jit(solution)/shard_map/ppermute | solution.py:27
  269.4 35.7 %collective-permute-start.24 = (bf16[1,1152,128]{2,1,0:T(8,128)(2,1)}, bf16[1,1152,128]{2,1,0:T(8,128)(2,1)}, u32[]{:S(2)}, u32[]{:S(2)}) collective-permute-start(bf16[1,1152,128]{2,1,0:T(8,128)(2,1)} %get-tuple-element.227), channel_id=1, source_target_pairs={{0,16},{4,20},{8,24},{12,28},{16,0},{20,4},{24,8},{28,12},{1,17},{... | collective-permute-start | bytes 884744 | tf_op jit(solution)/shard_map/ppermute | solution.py:27
  281.0 22.2 %collective-permute-start.26 = (bf16[1,1152,128]{2,1,0:T(8,128)(2,1)}, bf16[1,1152,128]{2,1,0:T(8,128)(2,1)}, u32[]{:S(2)}, u32[]{:S(2)}) collective-permute-start(bf16[1,1152,128]{2,1,0:T(8,128)(2,1)} %halve.28.refs_0_), channel_id=1, source_target_pairs={{0,16},{4,20},{8,24},{12,28},{16,0},{20,4},{24,8},{28,12},{1,17},{... | collective-permute-start | bytes 884744 | tf_op jit(solution)/shard_map/ppermute | solution.py:27
  288.4 44.1 %collective-permute-start.35 = (bf16[8,32,2176]{2,1,0:T(8,128)(2,1)}, bf16[8,32,2176]{2,1,0:T(8,128)(2,1)}, u32[]{:S(2)}, u32[]{:S(2)}) collective-permute-start(bf16[8,32,2176]{2,1,0:T(8,128)(2,1)} %get-tuple-element.233), channel_id=1, source_target_pairs={{0,2},{1,3},{2,0},{3,1},{4,6},{5,7},{6,4},{7,5},{8,10},{9,11},{10,... | collective-permute-start | bytes 3342344 | tf_op jit(solution)/shard_map/ppermute | solution.py:27
  291.9 63.5 %collective-permute-start.38 = (bf16[4,1152,128]{2,1,0:T(8,128)(2,1)}, bf16[4,1152,128]{2,1,0:T(8,128)(2,1)}, u32[]{:S(2)}, u32[]{:S(2)}) collective-permute-start(bf16[4,1152,128]{2,1,0:T(8,128)(2,1)} %lay.7), channel_id=1, source_target_pairs={{0,4},{4,0},{8,12},{12,8},{16,20},{20,16},{24,28},{28,24},{1,5},{5... | collective-permute-start | bytes 3538952 | tf_op jit(solution)/shard_map/ppermute | solution.py:27
  305.1 22.3 %collective-permute-start.31 = (bf16[2,1152,128]{2,1,0:T(8,128)(2,1)}, bf16[2,1152,128]{2,1,0:T(8,128)(2,1)}, u32[]{:S(2)}, u32[]{:S(2)}) collective-permute-start(bf16[2,1152,128]{2,1,0:T(8,128)(2,1)} %lay.8), channel_id=1, source_target_pairs={{0,8},{4,12},{8,0},{12,4},{16,24},{20,28},{24,16},{28,20},{1,9},{5... | collective-permute-start | bytes 1769480 | tf_op jit(solution)/shard_map/ppermute | solution.py:27
  306.9 23.7 %collective-permute-start.30 = (bf16[1,1152,128]{2,1,0:T(8,128)(2,1)}, bf16[1,1152,128]{2,1,0:T(8,128)(2,1)}, u32[]{:S(2)}, u32[]{:S(2)}) collective-permute-start(bf16[1,1152,128]{2,1,0:T(8,128)(2,1)} %halve.30.refs_0_), channel_id=1, source_target_pairs={{0,16},{4,20},{8,24},{12,28},{16,0},{20,4},{24,8},{28,12},{1,17},{... | collective-permute-start | bytes 884744 | tf_op jit(solution)/shard_map/ppermute | solution.py:27
  313.2 25.1 %collective-permute-start.34 = (bf16[8,32,2048]{2,1,0:T(8,128)(2,1)}, bf16[8,32,2048]{2,1,0:T(8,128)(2,1)}, u32[]{:S(2)}, u32[]{:S(2)}) collective-permute-start(bf16[8,32,2048]{2,1,0:T(8,128)(2,1)} %get-tuple-element.242), channel_id=1, source_target_pairs={{0,2},{1,3},{2,0},{3,1},{4,6},{5,7},{6,4},{7,5},{8,10},{9,11},{10,... | collective-permute-start | bytes 3145736 | tf_op jit(solution)/shard_map/ppermute | solution.py:27
  329.7 67.1 %collective-permute-start.42 = (bf16[4,1152,128]{2,1,0:T(8,128)(2,1)}, bf16[4,1152,128]{2,1,0:T(8,128)(2,1)}, u32[]{:S(2)}, u32[]{:S(2)}) collective-permute-start(bf16[4,1152,128]{2,1,0:T(8,128)(2,1)} %lay.9), channel_id=1, source_target_pairs={{0,4},{4,0},{8,12},{12,8},{16,20},{20,16},{24,28},{28,24},{1,5},{5... | collective-permute-start | bytes 3538952 | tf_op jit(solution)/shard_map/ppermute | solution.py:27
  332.5 16.6 %collective-permute-start.33 = (bf16[2,1152,128]{2,1,0:T(8,128)(2,1)}, bf16[2,1152,128]{2,1,0:T(8,128)(2,1)}, u32[]{:S(2)}, u32[]{:S(2)}) collective-permute-start(bf16[2,1152,128]{2,1,0:T(8,128)(2,1)} %lay.10), channel_id=1, source_target_pairs={{0,8},{4,12},{8,0},{12,4},{16,24},{20,28},{24,16},{28,20},{1,9},{5... | collective-permute-start | bytes 1769480 | tf_op jit(solution)/shard_map/ppermute | solution.py:27
  335.2 25.8 %collective-permute-start.37 = (bf16[4,32,2176]{2,1,0:T(8,128)(2,1)}, bf16[4,32,2176]{2,1,0:T(8,128)(2,1)}, u32[]{:S(2)}, u32[]{:S(2)}) collective-permute-start(bf16[4,32,2176]{2,1,0:T(8,128)(2,1)} %get-tuple-element.251), channel_id=1, source_target_pairs={{0,8},{4,12},{8,0},{12,4},{16,24},{20,28},{24,16},{28,20},{1,9},{5... | collective-permute-start | bytes 1671176 | tf_op jit(solution)/shard_map/ppermute | solution.py:27
  341.0 34.7 %collective-permute-start.36 = (bf16[4,32,2048]{2,1,0:T(8,128)(2,1)}, bf16[4,32,2048]{2,1,0:T(8,128)(2,1)}, u32[]{:S(2)}, u32[]{:S(2)}) collective-permute-start(bf16[4,32,2048]{2,1,0:T(8,128)(2,1)} %get-tuple-element.253), channel_id=1, source_target_pairs={{0,8},{4,12},{8,0},{12,4},{16,24},{20,28},{24,16},{28,20},{1,9},{5... | collective-permute-start | bytes 1572872 | tf_op jit(solution)/shard_map/ppermute | solution.py:27
  351.6 51.8 %collective-permute-start.44 = (bf16[4,1152,128]{2,1,0:T(8,128)(2,1)}, bf16[4,1152,128]{2,1,0:T(8,128)(2,1)}, u32[]{:S(2)}, u32[]{:S(2)}) collective-permute-start(bf16[4,1152,128]{2,1,0:T(8,128)(2,1)} %lay.11), channel_id=1, source_target_pairs={{0,4},{4,0},{8,12},{12,8},{16,20},{20,16},{24,28},{28,24},{1,5},{5... | collective-permute-start | bytes 3538952 | tf_op jit(solution)/shard_map/ppermute | solution.py:27
  (41 other events, 294.0 us)
Sparse Core Ops, SparseCore 0:
  10.9 75.5 all-gather.1
  215.0 43.3 reduce-scatter.1

commit v6 on v5

--- a/solution.py
+++ b/solution.py
@@ -908,10 +908,10 @@
     )
     order.mark(rim_out)
     rim_back = shift(rim_out, "mp", -1)
+    two.add()
+    two.send()
     one.add()
     one.send()
-    two.add()
-    two.send()
     halves = mix_outer(
         place_all, bits_all, gated_low, order(residual_low), low_all, closing_low, totals
     )
@@ -920,10 +920,10 @@
     outer.send()
     three.add()
     three.send()
+    outer.add()
+    outer.send()
     two.add()
     two.send()
-    outer.add()
-    outer.send()
     one.add()
     one.send()
     first_part, last_part, *halves = mix_grads(

time: 426 us -> 421 us (0.988)
  no operation moved by 1% of the time
where the time goes in v6:
time: 421 us; the launch traced here: 414 us
  Pallas kernels  201 us (48%)
  waiting for transfers between devices  110 us (26%)
  starting transfers between devices  50 us (12%)
  matrix products  21.2 us (5%)
  between operations  14.9 us (4%)
  local copies, waits for them, and re-layouts  10.5 us (2%)
  other arithmetic  6.72 us (2%)
    ppermute x42, waiting for transfers between devices, swap(): return lax.ppermute(block, axis, [(i, i ^ 1 << bit) for i in range(size)])  96.6 us
    pallas_call x20, Pallas kernels, halve(): pl.pallas_call(halve_kernel, grid=(1,), in_specs=[whole(kept), whole(got)...  47.7 us
    ppermute x42, starting transfers between devices, swap(): return lax.ppermute(block, axis, [(i, i ^ 1 << bit) for i in range(size)])  44.4 us
    pallas_call x3, Pallas kernels, far_feed(): pl.pallas_call(functools.partial(far_kernel, orders), grid_spec=pltpu.Pre...  36.3 us
    pallas_call x1, Pallas kernels, near_feed(): pl.pallas_call(near_kernel, grid=(pl.cdiv(hidden, wide),), in_specs=[whol...  23.3 us
    dot_general x8, matrix products, dot(): return lax.dot_general(left, right, dims, preferred_element_type=F32)  21.2 us
    pallas_call x1, Pallas kernels, mix_back(): pl.pallas_call(functools.partial(mix_back_kernel, bits), grid_spec=pltpu....  14.4 us
    pallas_call x1, Pallas kernels, mix_front(): pl.pallas_call(functools.partial(mix_front_kernel, bits), grid_spec=pltpu...  13.8 us
  transfers between devices with their start and end apart: 47, of which 17 were waited for; matrix products, arithmetic and copies ran while one was open for 7% of the time, Pallas kernels for 41%

profile of v6, /device:TPU:0, one launch (start us, length us, event | category | flops | bytes accessed | tf_op | source)
XLA Modules:
  0.0 413.9 jit_solution(13581153090309317998)
XLA Ops:
  9.6 4.0 collective-permute-start
  13.7 3.9 collective-permute-done
  18.3 4.5 %collective-permute-done.1 = bf16[2,32,1152]{2,1,0:T(8,128)(2,1)S(1)} collective-permute-done((bf16[2,32,1152]{2,1,0:T(8,128)(2,1)S(1)}, bf16[2,32,1152]{2,1,0:T(8,128)(2,1)S(1)}, u32[]{:S(2)}, u32[]{:S(2)}) %collective-permute-start.1) | collective-permute-done | bytes 147488 | tf_op jit(solution)/shard_map/ppermute | solution.py:27
  26.2 4.7 %collective-permute-done.2 = bf16[4,32,1152]{2,1,0:T(8,128)(2,1)S(1)} collective-permute-done((bf16[4,32,1152]{2,1,0:T(8,128)(2,1)S(1)}, bf16[4,32,1152]{2,1,0:T(8,128)(2,1)S(1)}, u32[]{:S(2)}, u32[]{:S(2)}) %collective-permute-start.2) | collective-permute-done | bytes 294944 | tf_op jit(solution)/shard_map/ppermute | solution.py:27
  32.5 32.6 %collective-permute-done.3 = bf16[8,32,1152]{2,1,0:T(8,128)(2,1)S(1)} collective-permute-done((bf16[8,32,1152]{2,1,0:T(8,128)(2,1)S(1)}, bf16[8,32,1152]{2,1,0:T(8,128)(2,1)S(1)}, u32[]{:S(2)}, u32[]{:S(2)}) %collective-permute-start.3) | collective-permute-done | bytes 589856 | tf_op jit(solution)/shard_map/ppermute | solution.py:27
  74.0 12.5 %all-gather.2.cloned.1.call-done.in_any.w_ref = bf16[1024,3072]{1,0:T(8,128)(2,1)} async-done(((bf16[32,3072]{1,0:T(8,128)(2,1)}), bf16[1024,3072]{1,0:T(8,128)(2,1)}) %all-gather.2.cloned.1.call-update) | async-done | bytes 6291472 | tf_op jit(solution)/shard_map/all_gather | solution.py:831
  86.5 13.8 %mix_front.1 = (f32[520,3072]{1,0:T(8,128)}, bf16[520,1024]{1,0:T(8,128)(2,1)}, bf16[512,1024]{1,0:T(8,128)(2,1)}, f32[8,1024]{1,0:T(8,128)}, f32[512,1024]{1,0:T(8,128)}, /*index=5*/bf16[512,1024]{1,0:T(8,128)(2,1)}) custom-call(s32[1]{0:T(128)} %bitcast.place_ref, bf16[1024,3072]{1,0:T(8,128)(2,1)} %all-gather.2.cloned.1.call-done.in_any.w_ref, ...), custom_call_target="tpu_custom_call" | custom-call | flops 99999997952 | tf_op jit(solution)/shard_map/mix_front/pallas_call | solution.py:450
  104.2 23.3 %near_feed.1 = (bf16[512,1152]{1,0:T(8,128)(2,1)}, bf16[512,1152]{1,0:T(8,128)(2,1)}, bf16[512,1152]{1,0:T(8,128)(2,1)}, bf16[512,1152]{1,0:T(8,128)(2,1)}, bf16...) custom-call(bf16[512,1024]{1,0:T(8,128)(2,1)} %get-tuple-element.149, ...), custom_call_target="tpu_custom_call" | custom-call | flops 99999997952 | tf_op jit(solution)/shard_map/near_feed/pallas_call | solution.py:124
  131.2 11.8 %far_feed.3 = (bf16[512,1152]{1,0:T(8,128)(2,1)}, bf16[512,1152]{1,0:T(8,128)(2,1)}, bf16[512,1152]{1,0:T(8,128)(2,1)}, bf16[512,1152]{1,0:T(8,128)(2,1)}, bf16[...) custom-call(s32[1]{0:T(128)} %bitcast.10.place_ref, ...), custom_call_target="tpu_custom_call" | custom-call | flops 99999997952 | tf_op jit(solution)/shard_map/far_feed/pallas_call | solution.py:186
  144.5 12.3 %far_feed.4 = (bf16[512,1152]{1,0:T(8,128)(2,1)}, bf16[512,1152]{1,0:T(8,128)(2,1)}, bf16[512,1152]{1,0:T(8,128)(2,1)}, bf16[512,1152]{1,0:T(8,128)(2,1)}, bf16[...) custom-call(s32[1]{0:T(128)} %bitcast.10.place_ref, ...), custom_call_target="tpu_custom_call", output_to_operand_aliasing={{0}: (11, {}), {1}: (12, {}), {2}: (13, {}), {3}: (14, {}),... | custom-call | flops 99999997952 | tf_op jit(solution)/shard_map/far_feed/pallas_call | solution.py:186
  156.8 12.2 %far_feed.5 = (bf16[512,1152]{1,0:T(8,128)(2,1)}, bf16[512,1152]{1,0:T(8,128)(2,1)}, bf16[512,1152]{1,0:T(8,128)(2,1)}, bf16[512,1152]{1,0:T(8,128)(2,1)}, bf16[...) custom-call(s32[1]{0:T(128)} %bitcast.10.place_ref, ...), custom_call_target="tpu_custom_call", output_to_operand_aliasing={{0}: (11, {}), {1}: (12, {}), {2}: (13, {}), {3}: (14, {}),... | custom-call | flops 99999997952 | tf_op jit(solution)/shard_map/far_feed/pallas_call | solution.py:186
  169.6 3.0 fusion.5
  180.1 3.0 fusion.6
  188.4 3.2 fusion.7
  199.0 3.0 fusion.8
  204.5 10.3 %onward.1 = bf16[2048,1024]{1,0:T(8,128)(2,1)} custom-call(s32[1]{0:T(128)} %bitcast.9.place_ref, bf16[512,1152]{1,0:T(8,128)(2,1)} %get-tuple-element.195.refs_0_, bf16[512,1152]{1,0:T(8,128)(2,1)} %get-tuple-element.196.refs_1_, bf16[512,1152]{1,0:T(8,128)(2,1)} %get-tuple-element.197.refs_2_, bf16[512,1152]{1,0:T(8,128)(2,1)} %get-tuple-element.198.refs_3_, ...), custom_call_target="tpu_custom_call" | custom-call | flops 99999997952 | tf_op jit(solution)/shard_map/onward/pallas_call | solution.py:488
  214.8 7.6 %collective-permute-done.18.got_ref = bf16[4,1152,128]{2,1,0:T(8,128)(2,1)} collective-permute-done((bf16[4,1152,128]{2,1,0:T(8,128)(2,1)}, bf16[4,1152,128]{2,1,0:T(8,128)(2,1)}, u32[]{:S(2)}, u32[]{:S(2)}) %collective-permute-start.18) | collective-permute-done | bytes 1179680 | tf_op jit(solution)/shard_map/ppermute | solution.py:27
  222.4 3.0 halve.23
  229.8 2.8 halve.25
  234.3 14.4 %mix_back.1 = (f32[512,1024]{1,0:T(8,128)}, bf16[512,1024]{1,0:T(8,128)(2,1)}, bf16[512,1024]{1,0:T(8,128)(2,1)}, f32[512,1024]{1,0:T(8,128)}, f32[8,1024]{1,0:T(8,128)}, /*index=5*/f32[4,8,1024]{2,1,0:T(8,128)}) custom-call(s32[1]{0:T(128)} %bitcast.place_ref, bf16[512,1024]{1,0:T(8,128)(2,1)} %add_convert_fusion.1.near_ref, ...), custom_call_target="tpu_custom_call" | custom-call | flops 99999997952 | tf_op jit(solution)/shard_map/mix_back/pallas_call | solution.py:604
  256.5 8.5 %mix_outer.1 = (bf16[16,32,2176]{2,1,0:T(8,128)(2,1)}, bf16[16,32,2176]{2,1,0:T(8,128)(2,1)}) custom-call(s32[1]{0:T(128)} %bitcast.place_ref, bf16[512,1024]{1,0:T(8,128)(2,1)} %get-tuple-element.209.gated_ref, bf16[512,1024]{1,0:T(8,128)(2,1)} %get-tuple-element.220.rlow_ref, bf16[520,1024]{1,0:T(8,128)(2,1)} %get-tuple-element.221.low_ref, ...), custom_call_target="tpu_custom_call" | custom-call | flops 99999997952 | tf_op jit(solution)/shard_map/mix_outer/pallas_call | solution.py:633
  271.1 4.0 halve.28
  279.6 5.3 %collective-permute-done.29.refs_2_ = bf16[2,1152,128]{2,1,0:T(8,128)(2,1)} collective-permute-done((bf16[2,1152,128]{2,1,0:T(8,128)(2,1)}, bf16[2,1152,128]{2,1,0:T(8,128)(2,1)}, u32[]{:S(2)}, u32[]{:S(2)}) %collective-permute-start.29) | collective-permute-done | bytes 589856 | tf_op jit(solution)/shard_map/ppermute | solution.py:27
  288.7 10.0 %mix_grads.1 = (bf16[512,1024]{1,0:T(8,128)(2,1)}, bf16[512,1024]{1,0:T(8,128)(2,1)}, bf16[16,32,2048]{2,1,0:T(8,128)(2,1)}, bf16[16,32,2048]{2,1,0:T(8,128)(2,1)}) custom-call(s32[1]{0:T(128)} %bitcast.place_ref, f32[512,1024]{1,0:T(8,128)} %get-tuple-element.233.pg_ref, f32[8,1024]{1,0:T(8,128)} %collective-permute-done.28.rim_ref, ...), custom_call_target="tpu_custom_call" | custom-call | flops 99999997952 | tf_op jit(solution)/shard_map/mix_grads/pallas_call | solution.py:682
  305.3 3.8 halve.31
  310.2 11.1 %input_back.1 = f32[512,1024]{1,0:T(8,128)} custom-call(bf16[512,1024]{1,0:T(8,128)(2,1)} %get-tuple-element.243.first_ref, bf16[512,1024]{1,0:T(8,128)(2,1)} %get-tuple-element.222.cl_ref.mid_ref, bf16[512,1024]{1,0:T(8,128)(2,1)} %get-tuple-element.244.last_ref, bf16[1024,3072]{1,0:T(8,128)(2,1)} %all-gather.2.cloned.1.call-done.in_any.w_ref, ...), custom_call_target="tpu_custom_call" | custom-call | flops 99999997952 | tf_op jit(solution)/shard_map/input_back/pallas_call | solution.py:718
  337.0 8.2 %collective-permute-done.33.refs_2_ = bf16[2,1152,128]{2,1,0:T(8,128)(2,1)} collective-permute-done((bf16[2,1152,128]{2,1,0:T(8,128)(2,1)}, bf16[2,1152,128]{2,1,0:T(8,128)(2,1)}, u32[]{:S(2)}, u32[]{:S(2)}) %collective-permute-start.33) | collective-permute-done | bytes 589856 | tf_op jit(solution)/shard_map/ppermute | solution.py:27
  351.0 4.1 unpack.3
  359.7 12.0 %collective-permute-done.36.got_ref = bf16[4,32,2048]{2,1,0:T(8,128)(2,1)} collective-permute-done((bf16[4,32,2048]{2,1,0:T(8,128)(2,1)}, bf16[4,32,2048]{2,1,0:T(8,128)(2,1)}, u32[]{:S(2)}, u32[]{:S(2)}) %collective-permute-start.36) | collective-permute-done | bytes 524320 | tf_op jit(solution)/shard_map/ppermute | solution.py:27
  377.5 8.5 %collective-permute-done.39.got_ref = bf16[2,32,2048]{2,1,0:T(8,128)(2,1)S(1)} collective-permute-done((bf16[2,32,2048]{2,1,0:T(8,128)(2,1)}, bf16[2,32,2048]{2,1,0:T(8,128)(2,1)S(1)}, u32[]{:S(2)}, u32[]{:S(2)}) %collective-permute-start.39) | collective-permute-done | bytes 262176 | tf_op jit(solution)/shard_map/ppermute | solution.py:27
  392.2 4.1 unpack.4
  402.5 4.1 unpack.5
  (194 shorter events, 129.5 us)
Async XLA Ops:
  7.2 79.3 %all-gather.2.cloned.1.call-start = ((), (), s32[]{:S(2)}) async-start(), calls=%async_computation.1 | async-start | bytes 6488064 | tf_op jit(solution)/shard_map/all_gather | solution.py:831
  7.9 340.5 %reduce-scatter.2.cloned.1.call-start = ((), (), s32[]{:S(2)}) async-start(), calls=%async_computation.2 | async-start | bytes 5242880 | tf_op jit(solution)/shard_map/reduce_scatter | solution.py:895
  24.6 43.2 %collective-permute-start.7 = (bf16[512,1024]{1,0:T(8,128)(2,1)S(1)}, bf16[512,1024]{1,0:T(8,128)(2,1)}, u32[]{:S(2)}, u32[]{:S(2)}) collective-permute-start(bf16[512,1024]{1,0:T(8,128)(2,1)S(1)} %bitcast.53), channel_id=1, source_target_pairs={{0,2},{1,3},{2,0},{3,1},{4,6},{5,7},{6,4},{7,5},{8,10},{9,11},{10,... | collective-permute-start | bytes 3145736 | tf_op jit(solution)/shard_map/ppermute | solution.py:27
  26.2 47.8 %collective-permute-start.6 = (bf16[512,1024]{1,0:T(8,128)(2,1)S(1)}, bf16[512,1024]{1,0:T(8,128)(2,1)}, u32[]{:S(2)}, u32[]{:S(2)}) collective-permute-start(bf16[512,1024]{1,0:T(8,128)(2,1)S(1)} %bitcast.54), channel_id=1, source_target_pairs={{0,1},{1,0},{2,3},{3,2},{4,5},{5,4},{6,7},{7,6},{8,9},{9,8},{10,11... | collective-permute-start | bytes 3145736 | tf_op jit(solution)/shard_map/ppermute | solution.py:27
  30.9 34.3 %collective-permute-start.3 = (bf16[8,32,1152]{2,1,0:T(8,128)(2,1)S(1)}, bf16[8,32,1152]{2,1,0:T(8,128)(2,1)S(1)}, u32[]{:S(2)}, u32[]{:S(2)}) collective-permute-start(bf16[8,32,1152]{2,1,0:T(8,128)(2,1)S(1)} %pad_maximum_fusion), channel_id=1, source_target_pairs={{0,2},{1,3},{2,0},{3,1},{4,6},{5,7},{6,4},{7,5},{8,10},{9,11},{10,... | collective-permute-start | bytes 1769480 | tf_op jit(solution)/shard_map/ppermute | solution.py:27
  100.6 26.9 %collective-permute-start.11 = (bf16[512,1024]{1,0:T(8,128)(2,1)}, bf16[512,1024]{1,0:T(8,128)(2,1)S(1)}, u32[]{:S(2)}, u32[]{:S(2)}) collective-permute-start(bf16[512,1024]{1,0:T(8,128)(2,1)} %get-tuple-element.149.xa_ref), channel_id=1, source_target_pairs={{0,2},{1,3},{2,0},{3,1},{4,6},{5,7},{6,4},{7,5},{8,10},{9,11},{10,... | collective-permute-start | bytes 3145736 | tf_op jit(solution)/shard_map/ppermute | solution.py:27
  143.1 32.6 %collective-permute-start.13 = (bf16[4,1152,128]{2,1,0:T(8,128)(2,1)}, bf16[4,1152,128]{2,1,0:T(8,128)(2,1)}, u32[]{:S(2)}, u32[]{:S(2)}) collective-permute-start(bf16[4,1152,128]{2,1,0:T(8,128)(2,1)} %get-tuple-element.173), channel_id=1, source_target_pairs={{0,4},{4,0},{8,12},{12,8},{16,20},{20,16},{24,28},{28,24},{1,5},{5... | collective-permute-start | bytes 3538952 | tf_op jit(solution)/shard_map/ppermute | solution.py:27
  168.9 60.9 %collective-permute-start.16 = (bf16[4,1152,128]{2,1,0:T(8,128)(2,1)}, bf16[4,1152,128]{2,1,0:T(8,128)(2,1)}, u32[]{:S(2)}, u32[]{:S(2)}) collective-permute-start(bf16[4,1152,128]{2,1,0:T(8,128)(2,1)} %get-tuple-element.176), channel_id=1, source_target_pairs={{0,4},{4,0},{8,12},{12,8},{16,20},{20,16},{24,28},{28,24},{1,5},{5... | collective-permute-start | bytes 3538952 | tf_op jit(solution)/shard_map/ppermute | solution.py:27
  174.2 48.2 %collective-permute-start.18 = (bf16[4,1152,128]{2,1,0:T(8,128)(2,1)}, bf16[4,1152,128]{2,1,0:T(8,128)(2,1)}, u32[]{:S(2)}, u32[]{:S(2)}) collective-permute-start(bf16[4,1152,128]{2,1,0:T(8,128)(2,1)} %get-tuple-element.202), channel_id=1, source_target_pairs={{0,4},{4,0},{8,12},{12,8},{16,20},{20,16},{24,28},{28,24},{1,5},{5... | collective-permute-start | bytes 3538952 | tf_op jit(solution)/shard_map/ppermute | solution.py:27
  178.5 16.3 %collective-permute-start.14 = (bf16[2,1152,128]{2,1,0:T(8,128)(2,1)}, bf16[2,1152,128]{2,1,0:T(8,128)(2,1)S(1)}, u32[]{:S(2)}, u32[]{:S(2)}) collective-permute-start(bf16[2,1152,128]{2,1,0:T(8,128)(2,1)} %get-tuple-element.181), channel_id=1, source_target_pairs={{0,8},{4,12},{8,0},{12,4},{16,24},{20,28},{24,16},{28,20},{1,9},{5... | collective-permute-start | bytes 1769480 | tf_op jit(solution)/shard_map/ppermute | solution.py:27
  194.2 40.2 %collective-permute-start.21 = (bf16[512,1024]{1,0:T(8,128)(2,1)}, bf16[512,1024]{1,0:T(8,128)(2,1)}, u32[]{:S(2)}, u32[]{:S(2)}) collective-permute-start(bf16[512,1024]{1,0:T(8,128)(2,1)} %add_convert_fusion.2), channel_id=1, source_target_pairs={{0,1},{1,0},{2,3},{3,2},{4,5},{5,4},{6,7},{7,6},{8,9},{9,8},{10,11... | collective-permute-start | bytes 3145736 | tf_op jit(solution)/shard_map/ppermute | solution.py:27
  194.2 40.2 %collective-permute-start.20 = (bf16[512,1024]{1,0:T(8,128)(2,1)}, bf16[512,1024]{1,0:T(8,128)(2,1)}, u32[]{:S(2)}, u32[]{:S(2)}) collective-permute-start(bf16[512,1024]{1,0:T(8,128)(2,1)} %bitcast.13), channel_id=1, source_target_pairs={{0,2},{1,3},{2,0},{3,1},{4,6},{5,7},{6,4},{7,5},{8,10},{9,11},{10,... | collective-permute-start | bytes 3145736 | tf_op jit(solution)/shard_map/ppermute | solution.py:27
  197.7 29.4 %collective-permute-start.17 = (bf16[1,1152,128]{2,1,0:T(8,128)(2,1)}, bf16[1,1152,128]{2,1,0:T(8,128)(2,1)}, u32[]{:S(2)}, u32[]{:S(2)}) collective-permute-start(bf16[1,1152,128]{2,1,0:T(8,128)(2,1)} %get-tuple-element.192), channel_id=1, source_target_pairs={{0,16},{4,20},{8,24},{12,28},{16,0},{20,4},{24,8},{28,12},{1,17},{... | collective-permute-start | bytes 884744 | tf_op jit(solution)/shard_map/ppermute | solution.py:27
  225.4 24.6 %collective-permute-start.23 = (bf16[2,1152,128]{2,1,0:T(8,128)(2,1)}, bf16[2,1152,128]{2,1,0:T(8,128)(2,1)}, u32[]{:S(2)}, u32[]{:S(2)}) collective-permute-start(bf16[2,1152,128]{2,1,0:T(8,128)(2,1)} %get-tuple-element.204), channel_id=1, source_target_pairs={{0,8},{4,12},{8,0},{12,4},{16,24},{20,28},{24,16},{28,20},{1,9},{5... | collective-permute-start | bytes 1769480 | tf_op jit(solution)/shard_map/ppermute | solution.py:27
  228.9 24.1 %collective-permute-start.22 = (bf16[1,1152,128]{2,1,0:T(8,128)(2,1)}, bf16[1,1152,128]{2,1,0:T(8,128)(2,1)}, u32[]{:S(2)}, u32[]{:S(2)}) collective-permute-start(bf16[1,1152,128]{2,1,0:T(8,128)(2,1)} %halve.24.refs_0_), channel_id=1, source_target_pairs={{0,16},{4,20},{8,24},{12,28},{16,0},{20,4},{24,8},{28,12},{1,17},{... | collective-permute-start | bytes 884744 | tf_op jit(solution)/shard_map/ppermute | solution.py:27
  232.7 32.9 %collective-permute-start.19 = (bf16[2,1152,128]{2,1,0:T(8,128)(2,1)}, bf16[2,1152,128]{2,1,0:T(8,128)(2,1)}, u32[]{:S(2)}, u32[]{:S(2)}) collective-permute-start(bf16[2,1152,128]{2,1,0:T(8,128)(2,1)} %get-tuple-element.208), channel_id=1, source_target_pairs={{0,8},{4,12},{8,0},{12,4},{16,24},{20,28},{24,16},{28,20},{1,9},{5... | collective-permute-start | bytes 1769480 | tf_op jit(solution)/shard_map/ppermute | solution.py:27
  248.7 40.0 %collective-permute-start.28 = (f32[8,1024]{1,0:T(8,128)}, f32[8,1024]{1,0:T(8,128)}, u32[]{:S(2)}, u32[]{:S(2)}) collective-permute-start(f32[8,1024]{1,0:T(8,128)} %get-tuple-element.216), channel_id=1, source_target_pairs={{1,0},{2,1},{3,2},{5,4},{6,5},{7,6},{9,8},{10,9},{11,10},{13,12},{... | collective-permute-start | bytes 98312 | tf_op jit(solution)/shard_map/ppermute | solution.py:33
  252.2 24.7 %collective-permute-start.25 = (bf16[1,1152,128]{2,1,0:T(8,128)(2,1)}, bf16[1,1152,128]{2,1,0:T(8,128)(2,1)}, u32[]{:S(2)}, u32[]{:S(2)}) collective-permute-start(bf16[1,1152,128]{2,1,0:T(8,128)(2,1)} %get-tuple-element.218), channel_id=1, source_target_pairs={{0,16},{4,20},{8,24},{12,28},{16,0},{20,4},{24,8},{28,12},{1,17},{... | collective-permute-start | bytes 884744 | tf_op jit(solution)/shard_map/ppermute | solution.py:27
  254.9 30.0 %collective-permute-start.29 = (bf16[2,1152,128]{2,1,0:T(8,128)(2,1)}, bf16[2,1152,128]{2,1,0:T(8,128)(2,1)}, u32[]{:S(2)}, u32[]{:S(2)}) collective-permute-start(bf16[2,1152,128]{2,1,0:T(8,128)(2,1)} %lay.6), channel_id=1, source_target_pairs={{0,8},{4,12},{8,0},{12,4},{16,24},{20,28},{24,16},{28,20},{1,9},{5... | collective-permute-start | bytes 1769480 | tf_op jit(solution)/shard_map/ppermute | solution.py:27
  267.7 33.0 %collective-permute-start.24 = (bf16[1,1152,128]{2,1,0:T(8,128)(2,1)}, bf16[1,1152,128]{2,1,0:T(8,128)(2,1)}, u32[]{:S(2)}, u32[]{:S(2)}) collective-permute-start(bf16[1,1152,128]{2,1,0:T(8,128)(2,1)} %get-tuple-element.227), channel_id=1, source_target_pairs={{0,16},{4,20},{8,24},{12,28},{16,0},{20,4},{24,8},{28,12},{1,17},{... | collective-permute-start | bytes 884744 | tf_op jit(solution)/shard_map/ppermute | solution.py:27
  275.1 53.5 %collective-permute-start.35 = (bf16[8,32,2176]{2,1,0:T(8,128)(2,1)}, bf16[8,32,2176]{2,1,0:T(8,128)(2,1)}, u32[]{:S(2)}, u32[]{:S(2)}) collective-permute-start(bf16[8,32,2176]{2,1,0:T(8,128)(2,1)} %get-tuple-element.231), channel_id=1, source_target_pairs={{0,2},{1,3},{2,0},{3,1},{4,6},{5,7},{6,4},{7,5},{8,10},{9,11},{10,... | collective-permute-start | bytes 3342344 | tf_op jit(solution)/shard_map/ppermute | solution.py:27
  278.7 20.1 %collective-permute-start.27 = (bf16[1,1152,128]{2,1,0:T(8,128)(2,1)}, bf16[1,1152,128]{2,1,0:T(8,128)(2,1)}, u32[]{:S(2)}, u32[]{:S(2)}) collective-permute-start(bf16[1,1152,128]{2,1,0:T(8,128)(2,1)} %halve.29.refs_0_), channel_id=1, source_target_pairs={{0,16},{4,20},{8,24},{12,28},{16,0},{20,4},{24,8},{28,12},{1,17},{... | collective-permute-start | bytes 884744 | tf_op jit(solution)/shard_map/ppermute | solution.py:27
  287.2 63.8 %collective-permute-start.38 = (bf16[4,1152,128]{2,1,0:T(8,128)(2,1)}, bf16[4,1152,128]{2,1,0:T(8,128)(2,1)}, u32[]{:S(2)}, u32[]{:S(2)}) collective-permute-start(bf16[4,1152,128]{2,1,0:T(8,128)(2,1)} %lay.7), channel_id=1, source_target_pairs={{0,4},{4,0},{8,12},{12,8},{16,20},{20,16},{24,28},{28,24},{1,5},{5... | collective-permute-start | bytes 3538952 | tf_op jit(solution)/shard_map/ppermute | solution.py:27
  300.8 22.3 %collective-permute-start.31 = (bf16[2,1152,128]{2,1,0:T(8,128)(2,1)}, bf16[2,1152,128]{2,1,0:T(8,128)(2,1)}, u32[]{:S(2)}, u32[]{:S(2)}) collective-permute-start(bf16[2,1152,128]{2,1,0:T(8,128)(2,1)} %lay.8), channel_id=1, source_target_pairs={{0,8},{4,12},{8,0},{12,4},{16,24},{20,28},{24,16},{28,20},{1,9},{5... | collective-permute-start | bytes 1769480 | tf_op jit(solution)/shard_map/ppermute | solution.py:27
  302.6 24.1 %collective-permute-start.30 = (bf16[1,1152,128]{2,1,0:T(8,128)(2,1)}, bf16[1,1152,128]{2,1,0:T(8,128)(2,1)}, u32[]{:S(2)}, u32[]{:S(2)}) collective-permute-start(bf16[1,1152,128]{2,1,0:T(8,128)(2,1)} %halve.30.refs_0_), channel_id=1, source_target_pairs={{0,16},{4,20},{8,24},{12,28},{16,0},{20,4},{24,8},{28,12},{1,17},{... | collective-permute-start | bytes 884744 | tf_op jit(solution)/shard_map/ppermute | solution.py:27
  309.1 24.9 %collective-permute-start.34 = (bf16[8,32,2048]{2,1,0:T(8,128)(2,1)}, bf16[8,32,2048]{2,1,0:T(8,128)(2,1)}, u32[]{:S(2)}, u32[]{:S(2)}) collective-permute-start(bf16[8,32,2048]{2,1,0:T(8,128)(2,1)} %get-tuple-element.242), channel_id=1, source_target_pairs={{0,2},{1,3},{2,0},{3,1},{4,6},{5,7},{6,4},{7,5},{8,10},{9,11},{10,... | collective-permute-start | bytes 3145736 | tf_op jit(solution)/shard_map/ppermute | solution.py:27
  325.4 66.8 %collective-permute-start.42 = (bf16[4,1152,128]{2,1,0:T(8,128)(2,1)}, bf16[4,1152,128]{2,1,0:T(8,128)(2,1)}, u32[]{:S(2)}, u32[]{:S(2)}) collective-permute-start(bf16[4,1152,128]{2,1,0:T(8,128)(2,1)} %lay.9), channel_id=1, source_target_pairs={{0,4},{4,0},{8,12},{12,8},{16,20},{20,16},{24,28},{28,24},{1,5},{5... | collective-permute-start | bytes 3538952 | tf_op jit(solution)/shard_map/ppermute | solution.py:27
  328.6 16.6 %collective-permute-start.33 = (bf16[2,1152,128]{2,1,0:T(8,128)(2,1)}, bf16[2,1152,128]{2,1,0:T(8,128)(2,1)}, u32[]{:S(2)}, u32[]{:S(2)}) collective-permute-start(bf16[2,1152,128]{2,1,0:T(8,128)(2,1)} %lay.10), channel_id=1, source_target_pairs={{0,8},{4,12},{8,0},{12,4},{16,24},{20,28},{24,16},{28,20},{1,9},{5... | collective-permute-start | bytes 1769480 | tf_op jit(solution)/shard_map/ppermute | solution.py:27
  331.3 25.8 %collective-permute-start.37 = (bf16[4,32,2176]{2,1,0:T(8,128)(2,1)}, bf16[4,32,2176]{2,1,0:T(8,128)(2,1)}, u32[]{:S(2)}, u32[]{:S(2)}) collective-permute-start(bf16[4,32,2176]{2,1,0:T(8,128)(2,1)} %get-tuple-element.251), channel_id=1, source_target_pairs={{0,8},{4,12},{8,0},{12,4},{16,24},{20,28},{24,16},{28,20},{1,9},{5... | collective-permute-start | bytes 1671176 | tf_op jit(solution)/shard_map/ppermute | solution.py:27
  336.7 35.1 %collective-permute-start.36 = (bf16[4,32,2048]{2,1,0:T(8,128)(2,1)}, bf16[4,32,2048]{2,1,0:T(8,128)(2,1)}, u32[]{:S(2)}, u32[]{:S(2)}) collective-permute-start(bf16[4,32,2048]{2,1,0:T(8,128)(2,1)} %get-tuple-element.253), channel_id=1, source_target_pairs={{0,8},{4,12},{8,0},{12,4},{16,24},{20,28},{24,16},{28,20},{1,9},{5... | collective-permute-start | bytes 1572872 | tf_op jit(solution)/shard_map/ppermute | solution.py:27
  347.7 51.1 %collective-permute-start.44 = (bf16[4,1152,128]{2,1,0:T(8,128)(2,1)}, bf16[4,1152,128]{2,1,0:T(8,128)(2,1)}, u32[]{:S(2)}, u32[]{:S(2)}) collective-permute-start(bf16[4,1152,128]{2,1,0:T(8,128)(2,1)} %lay.11), channel_id=1, source_target_pairs={{0,4},{4,0},{8,12},{12,8},{16,20},{20,16},{24,28},{28,24},{1,5},{5... | collective-permute-start | bytes 3538952 | tf_op jit(solution)/shard_map/ppermute | solution.py:27
  359.2 14.7 %collective-permute-start.40 = (bf16[2,32,2176]{2,1,0:T(8,128)(2,1)}, bf16[2,32,2176]{2,1,0:T(8,128)(2,1)S(1)}, u32[]{:S(2)}, u32[]{:S(2)}) collective-permute-start(bf16[2,32,2176]{2,1,0:T(8,128)(2,1)} %get-tuple-element.261), channel_id=1, source_target_pairs={{0,16},{4,20},{8,24},{12,28},{16,0},{20,4},{24,8},{28,12},{1,17},{... | collective-permute-start | bytes 835592 | tf_op jit(solution)/shard_map/ppermute | solution.py:27
  (42 other events, 283.7 us)
Sparse Core Ops, SparseCore 0:
  10.9 75.5 all-gather.1
  215.0 43.3 reduce-scatter.1
